TPU v7x, 32 devices: a whole 2x2x4 slice. The times are simulated.
32 devices in a mesh: groups: 2 (over y), sect: 4 (over x, core), hid: 4 (over z).
Axes of the slice: x: 2, y: 2, z: 4, core: 2. Of those that a mesh axis runs over, the one named last changes fastest.
Arguments:
- resid: bfloat16 [1024, 4096], P(('groups', 'sect'), 'hid'), parts along dimension 0, may hold values from -64 to 64
- moe_gain: bfloat16 [4096], replicated, may hold values from 0.25 to 1.75
- routes: int32 [1024, 2], P(('groups', 'sect')), parts along dimension 0, may hold values from 0 to 3, all different within a row; in each aligned block of 128 rows (0 to 127, 128 to 255, ...) at most 128 rows name the same one
- gate_q: int32 [1024, 2], P(('groups', 'sect')), parts along dimension 0, may hold values from 16 to 255
- doc_lengths: int32 [8, 4], P(('groups', 'sect')), parts along dimension 0, may hold values from 1 to 64, 128 in all within a row
- w_gate: bfloat16 [4, 4096, 4096], P('sect', None, 'hid'), may hold values from -0.09375 to 0.09375
- w_up: bfloat16 [4, 4096, 4096], P('sect', None, 'hid'), may hold values from -0.09375 to 0.09375
- w_down: bfloat16 [4, 4096, 4096], P('sect', 'hid'), may hold values from -0.09375 to 0.09375
- attn_gain: bfloat16 [4096], replicated, may hold values from 0.25 to 1.75
- w_q: bfloat16 [4096, 4096], P('sect', 'hid')
- w_k: bfloat16 [4096, 1024], P('sect', 'hid')
- w_v: bfloat16 [4096, 1024], P('sect', 'hid'), may hold values from -0.09375 to 0.09375
Outputs:
- new_resid: bfloat16 [1024, 4096], P(('groups', 'sect'), 'hid'), parts along dimension 0
- context: bfloat16 [1024, 4096], P(('groups', 'sect'), 'hid'), parts along dimension 0
There are 2 independent parts, one for each index of `groups`. A program takes and returns all parts, laid end to end along the dimension named above; an argument that names none is the same for every part. Nothing has to cross between parts.
Inputs may be any that keep to these rules, and one draw needn't show every extreme that they name: `routes`: within the rows of one index of sect (aligned blocks of 128 rows) no expert is named by more than 128 rows. `doc_lengths`: each row sums to 128.
All inputs are finite; a program needn't handle non-finite values.
Results may differ from a plain program's by a relative error of at most 0.012.
The roundings to bfloat16 on the way count: a program that leaves them out, or rounds other values in their place, can miss the bound.
Values may be sent and summed in bfloat16 or wider, within the bound.
No kernel may reach another device: no remote copies, remote signals or barrier semaphores. Data moves between devices by JAX's collectives and lax.ppermute only.
A program may use at most 128 MiB of HBM per device.

v0:
```python
import math

import jax
import jax.numpy as jnp
from jax import lax
from jax.sharding import PartitionSpec as P

H = 32
KVH = 8
HD = 128


def layer_norm(values, gain):
    center = values - jnp.mean(values, axis=1, keepdims=True)
    spread = jnp.mean(center * center, axis=1, keepdims=True)
    return (center * lax.rsqrt(spread + 1e-05) * gain.astype(jnp.float32)).astype(jnp.bfloat16)


def slot_targets(route_rows, experts, capacity):
    flat = route_rows.reshape(-1)
    onehot = (flat[:, None] == jnp.arange(experts, dtype=jnp.int32)[None, :]).astype(jnp.int32)
    before = jnp.cumsum(onehot, axis=0, dtype=jnp.int32) - onehot
    return flat * capacity + jnp.sum(before * onehot, axis=1, dtype=jnp.int32)


def source_rows(targets, experts, capacity):
    count = targets.shape[0]
    filler = jnp.full((experts * capacity,), count, jnp.int32)
    return filler.at[targets].set(jnp.arange(count, dtype=jnp.int32)) // 2


def rotate(values, position, head):
    count = values.shape[0]
    split_heads = values.reshape(count, -1, head)
    half = head // 2
    freqs = jnp.exp(jnp.arange(half, dtype=jnp.float32) * (-2.0 * math.log(10000.0) / head))
    angles = position[:, None, None] * freqs[None, None, :]
    cosine = jnp.cos(angles)
    sine = jnp.sin(angles)
    first = split_heads[:, :, :half]
    second = split_heads[:, :, half:]
    turned = jnp.concatenate(
        [first * cosine - second * sine, second * cosine + first * sine], axis=2
    )
    return turned.reshape(count, -1)


def attend(query, keys, vals, lengths, head, group):
    count = query.shape[0]
    kv_heads = keys.shape[1] // head
    ends = jnp.cumsum(lengths, dtype=jnp.int32)
    places = jnp.arange(count, dtype=jnp.int32)
    after = (places[:, None] >= ends[None, :]).astype(jnp.int32)
    doc_ids = jnp.sum(after, axis=1, dtype=jnp.int32)
    starts = jnp.sum(after * lengths[None, :], axis=1, dtype=jnp.int32)
    position = (places - starts).astype(jnp.float32)
    rotated_q = (
        rotate(query, position, head).astype(jnp.bfloat16).reshape(count, kv_heads, group, head)
    )
    rotated_k = rotate(keys, position, head).astype(jnp.bfloat16).reshape(count, kv_heads, head)
    value_heads = vals.reshape(count, kv_heads, head)
    allowed = (doc_ids[:, None] == doc_ids[None, :]) & (places[None, :] <= places[:, None])
    scores = jnp.einsum(
        "tkgd,skd->kgts", rotated_q, rotated_k, preferred_element_type=jnp.float32
    ) * (1.0 / math.sqrt(head))
    scores = jnp.where(allowed[None, None], scores, -jnp.inf)
    highest = jnp.max(scores, axis=3, keepdims=True)
    weights = jnp.exp(scores - highest)
    probs = (weights / jnp.sum(weights, axis=3, keepdims=True)).astype(jnp.bfloat16)
    mixed = jnp.einsum("kgts,skd->tkgd", probs, value_heads, preferred_element_type=jnp.float32)
    return mixed.astype(jnp.bfloat16).reshape(count, -1)


def on_device(
    resid, moe_gain, routes, gate_q, doc_lengths, w_gate, w_up, w_down, attn_gain, w_q, w_k, w_v
):
    sections = lax.axis_size("sect")
    slices = lax.axis_size("hid")
    tokens_here, local_width = resid.shape
    width = local_width * slices
    capacity = 4 * tokens_here // sections
    entry = lax.all_gather(resid, "hid", axis=1, tiled=True)
    normed = layer_norm(entry.astype(jnp.float32), moe_gain)
    targets = slot_targets(routes, sections, capacity)
    sources = source_rows(targets, sections, capacity)
    padded = jnp.concatenate([normed, jnp.zeros((1, width), jnp.bfloat16)], axis=0)
    gate_w = w_gate[0]
    up_w = w_up[0]
    down_w = w_down[0]
    outgoing = padded[sources].reshape(sections, capacity, width)
    arrived = lax.all_to_all(outgoing, "sect", split_axis=0, concat_axis=0, tiled=True).reshape(
        sections * capacity, width
    )
    gate = jnp.dot(arrived, gate_w, preferred_element_type=jnp.float32)
    up = jnp.dot(arrived, up_w, preferred_element_type=jnp.float32)
    hidden = (jax.nn.silu(gate) * up).astype(jnp.bfloat16)
    weights = gate_q.reshape(-1).astype(jnp.float32) / 256.0
    own_resid = resid.astype(jnp.float32)
    outputs = jnp.dot(hidden, down_w, preferred_element_type=jnp.float32)
    mine = lax.psum_scatter(outputs, "hid", scatter_dimension=1, tiled=True)
    returned = lax.all_to_all(
        mine.reshape(sections, capacity, local_width),
        "sect",
        split_axis=0,
        concat_axis=0,
        tiled=True,
    )
    picked = returned.reshape(sections * capacity, local_width)[targets]
    mixture = jnp.sum((picked * weights[:, None]).reshape(tokens_here, 2, local_width), axis=1)
    new_local = (own_resid + mixture).astype(jnp.bfloat16)
    full_rows = lax.all_gather(new_local, "hid", axis=1, tiled=True)
    normed_next = layer_norm(full_rows.astype(jnp.float32), attn_gain)
    query = jnp.dot(
        normed_next,
        lax.all_gather(w_q, "sect", axis=0, tiled=True),
        preferred_element_type=jnp.float32,
    )
    keys = jnp.dot(
        normed_next,
        lax.all_gather(w_k, "sect", axis=0, tiled=True),
        preferred_element_type=jnp.float32,
    )
    vals = jnp.dot(
        normed_next,
        lax.all_gather(w_v, "sect", axis=0, tiled=True),
        preferred_element_type=jnp.float32,
    )
    context = attend(query, keys, vals.astype(jnp.bfloat16), doc_lengths[0], HD, H // KVH)
    return (new_local, context)


def solution(mesh):
    in_specs = (
        P(("groups", "sect"), "hid"),
        P(),
        P(("groups", "sect"), None),
        P(("groups", "sect"), None),
        P(("groups", "sect"), None),
        P("sect", None, "hid"),
        P("sect", None, "hid"),
        P("sect", "hid", None),
        P(),
        P("sect", "hid"),
        P("sect", "hid"),
        P("sect", "hid"),
    )
    out_specs = (P(("groups", "sect"), "hid"), P(("groups", "sect"), "hid"))
    return jax.shard_map(
        on_device, mesh=mesh, in_specs=in_specs, out_specs=out_specs, check_vma=False
    )
```

profile of v0, /device:TPU:0, one launch (start us, length us, event | category | flops | bytes accessed | tf_op | source)
XLA Modules:
  0.0 450.2 jit_solution(11100007344031387848)
XLA Ops:
  9.7 1.2 reduce-window.18
  12.3 1.4 scatter_custom_fusion
  13.7 26.5 %all-gather.6.cloned.1.call-done = bf16[128,4096]{1,0:T(8,128)(2,1)} async-done(((bf16[128,1024]{1,0:T(8,128)(2,1)}), bf16[128,4096]{1,0:T(8,128)(2,1)}) %all-gather.6.cloned.1.call-update) | async-done | bytes 1048592 | tf_op jit(solution)/shard_map/all_gather | solution.py:82
  40.2 1.5 convert_reduce_fusion.1
  41.8 1.7 fusion.14
  44.0 4.4 gather_fusion
  48.3 51.9 %all_to_all.10 = bf16[4,128,4096]{2,1,0:T(8,128)(2,1)S(1)} all-to-all(bf16[4,128,4096]{2,1,0:T(8,128)(2,1)} %bitcast.87), channel_id=1, replica_groups=mesh['groups'=2,'sect'=4,'hid'=4] {'sect'}, dimensions={0} | all-to-all | bytes 8388608 | tf_op jit(solution)/shard_map/all_to_all | solution.py:91
  100.2 2.0 copy-done.1
  102.2 6.9 %fusion.5 = f32[512,1024]{1,0:T(8,128)S(1)} fusion(bf16[512,4096]{1,0:T(8,128)(2,1)S(1)} %bitcast.89, bf16[1,4096,1024]{2,1,0:T(8,128)(2,1)} %param.17), kind=kOutput, calls=%fused_computation.8 | convolution fusion | flops 4294967296 | bytes 14680064 | tf_op jit(solution)/shard_map/dot_general | solution.py:94
  109.1 19.1 %fusion.1 = f32[512,4096]{1,0:T(8,128)} fusion(bf16[1,1024,4096]{2,1,0:T(8,128)(2,1)} %param.19, f32[512,1024]{1,0:T(8,128)S(1)} %fusion.5, bf16[512,4096]{1,0:T(8,128)(2,1)} %bitcast.90, bf16[1,4096,1024]{2,1,0:T(8,128)(2,1)} %param.18), kind=kOutput, calls=%fused_computation.4 | convolution fusion | flops 8593080320 | bytes 31457280 | tf_op jit(solution)/shard_map/dot_general | solution.py:99
  128.2 143.2 %reduce-scatter.2.cloned.1.call-done = f32[512,1024]{1,0:T(8,128)} async-done(((f32[512,4096]{1,0:T(8,128)}), f32[512,1024]{1,0:T(8,128)}) %reduce-scatter.2.cloned.1.call-update) | async-done | bytes 2097168 | tf_op jit(solution)/shard_map/reduce_scatter | solution.py:100
  271.4 3.7 all-to-all-start.1
  275.5 25.3 %all-to-all-done.1 = f32[4,128,1024]{2,1,0:T(8,128)S(1)} async-done(((f32[4,128,1024]{2,1,0:T(8,128)}), f32[4,128,1024]{2,1,0:T(8,128)S(1)}, u32[]{:S(2)}, u32[]{:S(2)}) %all-to-all-start.1) | async-done | bytes 2097184 | tf_op jit(solution)/shard_map/all_to_all | solution.py:101
  300.8 1.1 gather_fusion.1
  302.6 1.3 multiply_reduce_fusion
  307.2 25.4 %all-gather.8.cloned.1.call-done = bf16[128,4096]{1,0:T(8,128)(2,1)} async-done(((bf16[128,1024]{1,0:T(8,128)(2,1)}), bf16[128,4096]{1,0:T(8,128)(2,1)}) %all-gather.8.cloned.1.call-update) | async-done | bytes 1048592 | tf_op jit(solution)/shard_map/all_gather | solution.py:111
  332.6 1.5 convert_reduce_fusion
  334.2 1.7 fusion.11
  335.9 20.3 %all-gather.12.cloned.1.call-done = bf16[4096,256]{1,0:T(8,128)(2,1)} async-done(((bf16[1024,256]{1,0:T(8,128)(2,1)}), bf16[4096,256]{1,0:T(8,128)(2,1)}) %all-gather.12.cloned.1.call-update) | async-done | bytes 2097168 | tf_op jit(solution)/shard_map/all_gather | solution.py:120
  356.2 2.1 fusion.40
  358.4 57.5 %all-gather.14.cloned.1.call-done = bf16[4096,1024]{1,0:T(8,128)(2,1)} async-done(((bf16[1024,1024]{1,0:T(8,128)(2,1)}), bf16[4096,1024]{1,0:T(8,128)(2,1)}) %all-gather.14.cloned.1.call-update) | async-done | bytes 8388624 | tf_op jit(solution)/shard_map/all_gather | solution.py:115
  415.9 4.7 %convolution_bitcast_fusion = f32[16,8,8,128]{3,1,2,0:T(8,128)S(1)} fusion(bf16[4096,1024]{1,0:T(8,128)(2,1)} %all-gather.14.cloned.1.call-done, bf16[128,4096]{1,0:T(8,128)(2,1)S(1)} %copy-done.2, f32[4096]{0:T(1024)S(1)} %convert_element_type.80, f32[128]{0:T(128)S(1)} %add_rsqrt_fusion, f32[128]{0:T(128)S(1)} %broadcast_multiply_fusion.1), kind=kOutput, calls=%fused_computation.27 | convolution fusion | flops 1076363264 | bytes 9978880 | tf_op jit(solution)/shard_map/dot_general | solution.py:113
  422.1 17.9 %all-gather.10.cloned.1.call-done = bf16[4096,256]{1,0:T(8,128)(2,1)} async-done(((bf16[1024,256]{1,0:T(8,128)(2,1)}), bf16[4096,256]{1,0:T(8,128)(2,1)}) %all-gather.10.cloned.1.call-update) | async-done | bytes 2097168 | tf_op jit(solution)/shard_map/all_gather | solution.py:125
  439.9 2.1 convolution_convert_fusion.1
  (74 shorter events, 11.4 us)
Async XLA Ops:
  7.2 33.1 %all-gather.6.cloned.1.call-start = ((), (), s32[]{:S(2)}) async-start(), calls=%async_computation.3 | async-start | bytes 1310720 | tf_op jit(solution)/shard_map/all_gather | solution.py:82
  7.9 263.5 %reduce-scatter.2.cloned.1.call-start = ((), (), s32[]{:S(2)}) async-start(), calls=%async_computation.4 | async-start | bytes 10485760 | tf_op jit(solution)/shard_map/reduce_scatter | solution.py:100
  40.2 3.2 copy-start
  100.2 2.0 copy-start.1
  271.4 4.0 copy-start.5
  271.4 29.4 %all-to-all-start.1 = ((f32[4,128,1024]{2,1,0:T(8,128)}), f32[4,128,1024]{2,1,0:T(8,128)S(1)}, u32[]{:S(2)}, u32[]{:S(2)}) async-start(f32[4,128,1024]{2,1,0:T(8,128)} %bitcast.91), calls=%async_computation.2 | async-start | bytes 4194304 | tf_op jit(solution)/shard_map/all_to_all | solution.py:101
  275.2 57.5 %all-gather.8.cloned.1.call-start = ((), (), s32[]{:S(2)}) async-start(), calls=%async_computation.5 | async-start | bytes 1310720 | tf_op jit(solution)/shard_map/all_gather | solution.py:111
  301.9 2.0 copy-start.3
  303.9 2.6 copy-start.4
  303.9 2.6 copy-start.6
  304.7 51.4 %all-gather.12.cloned.1.call-start = ((), (), s32[]{:S(2)}) async-start(), calls=%async_computation.7 | async-start | bytes 2621440 | tf_op jit(solution)/shard_map/all_gather | solution.py:120
  305.3 110.6 %all-gather.14.cloned.1.call-start = ((), (), s32[]{:S(2)}) async-start(), calls=%async_computation.8 | async-start | bytes 10485760 | tf_op jit(solution)/shard_map/all_gather | solution.py:115
  305.9 134.0 %all-gather.10.cloned.1.call-start = ((), (), s32[]{:S(2)}) async-start(), calls=%async_computation.6 | async-start | bytes 2621440 | tf_op jit(solution)/shard_map/all_gather | solution.py:125
  332.6 23.5 %copy-start.2 = (bf16[128,4096]{1,0:T(8,128)(2,1)S(1)}, bf16[128,4096]{1,0:T(8,128)(2,1)}, u32[]{:S(2)}) copy-start(bf16[128,4096]{1,0:T(8,128)(2,1)} %all-gather.8.cloned.1.call-done) | copy-start | bytes 3145732
Sparse Core Ops, SparseCore 0:
  9.6 30.6 all-gather.5
  128.3 143.0 reduce-scatter.1
  304.9 27.7 all-gather.7
  334.1 22.0 all-gather.11
  357.6 58.2 all-gather.13
  417.3 22.5 all-gather.9
where the time goes:
time: 451 us; the launch traced here: 450 us
  waiting for transfers between devices  318 us (71%)
  blocking collectives  51.9 us (12%)
  matrix products  35.8 us (8%)
  between operations  14.4 us (3%)
  other arithmetic  12.8 us (3%)
  local copies, waits for them, and re-layouts  12.6 us (3%)
    reduce_scatter x1, waiting for transfers between devices, on_device(): mine = lax.psum_scatter(outputs, 'hid', scatter_dimension=1, tiled=True)  143 us
    all_gather x1, waiting for transfers between devices, on_device(): lax.all_gather(w_q, 'sect', axis=0, tiled=True)  57.5 us
    all_to_all x1, blocking collectives, on_device(): lax.all_to_all(outgoing, 'sect', split_axis=0, concat_axis=0, tiled=True)  51.9 us
    all_gather x1, waiting for transfers between devices, on_device(): entry = lax.all_gather(resid, 'hid', axis=1, tiled=True)  26.5 us
    all_gather x1, waiting for transfers between devices, on_device(): full_rows = lax.all_gather(new_local, 'hid', axis=1, tiled=True)  25.4 us
    all_to_all x1, waiting for transfers between devices, on_device(): lax.all_to_all(mine.reshape(sections, capacity, local_width), 'sect', spl...  25.3 us
    all_gather x1, waiting for transfers between devices, on_device(): lax.all_gather(w_k, 'sect', axis=0, tiled=True)  20.3 us
    dot_general x1, matrix products, on_device(): outputs = jnp.dot(hidden, down_w, preferred_element_type=jnp.float32)  19.1 us
  transfers between devices with their start and end apart: 7, of which 7 were waited for; matrix products, arithmetic and copies ran while one was open for 4% of the time, Pallas kernels for 0%

commit v1 on v0

--- a/solution.py
+++ b/solution.py
@@ -1,13 +1,285 @@
+import functools
 import math
 
 import jax
 import jax.numpy as jnp
 from jax import lax
+from jax.experimental import pallas as pl
+from jax.experimental.pallas import tpu as pltpu
 from jax.sharding import PartitionSpec as P
 
 H = 32
 KVH = 8
 HD = 128
+F32 = jnp.float32
+BF16 = jnp.bfloat16
+
+
+def norm_rows(pieces, gain_ref, block_of, store, rows, step):
+    width = sum(p.shape[1] for p in pieces)
+
+    def body(i, carry):
+        here = pl.ds(pl.multiple_of(i * step, step), step)
+        values = [p[here, :].astype(F32) for p in pieces]
+        total = values[0]
+        for v in values[1:]:
+            total = total + v
+        mean = jnp.sum(total, axis=1, keepdims=True) / width
+        centered = [v - mean for v in values]
+        squares = centered[0] * centered[0]
+        for c in centered[1:]:
+            squares = squares + c * c
+        spread = jnp.sum(squares, axis=1, keepdims=True) / width
+        scale = lax.rsqrt(spread + 1e-05)
+        for k, c in enumerate(centered):
+            gain = gain_ref[block_of(k)].astype(F32)
+            store(k, here, (c * scale * gain).astype(BF16))
+        return carry
+
+    lax.fori_loop(0, rows // step, body, 0)
+
+
+def up_body(place_ref, *refs):
+    pieces = refs[:8]
+    gain_ref, gate_ref, up_ref, out_ref, normed = refs[8:]
+    hid = place_ref[1]
+    rows, local = pieces[0].shape
+
+    @pl.when(pl.program_id(0) == 0)
+    def _():
+        for j in range(2):
+
+            def store(k, here, values, j=j):
+                where = pl.ds(pl.multiple_of((hid ^ k) * local, local), local)
+                normed[pl.ds(pl.multiple_of(j * rows + here.start, 16), here.size), where] = values
+
+            norm_rows(pieces[4 * j : 4 * j + 4], gain_ref, lambda k: hid ^ k, store, rows, 16)
+
+    lhs = normed[...]
+    gate = jnp.dot(lhs, gate_ref[...], preferred_element_type=F32)
+    up = jnp.dot(lhs, up_ref[...], preferred_element_type=F32)
+    out_ref[...] = (gate / (1.0 + jnp.exp(-gate)) * up).astype(BF16)
+
+
+def up_call(place, pieces, gain, gate_w, up_w):
+    rows, local = pieces[0].shape
+    width, units = gate_w.shape
+    block = 256
+    whole = pl.BlockSpec((rows, local), lambda i, p: (0, 0))
+    weight = pl.BlockSpec((width, block), lambda i, p: (0, i))
+    return pl.pallas_call(
+        up_body,
+        grid_spec=pltpu.PrefetchScalarGridSpec(
+            num_scalar_prefetch=1,
+            grid=(units // block,),
+            in_specs=[whole] * 8
+            + [pl.BlockSpec((4, 1, local), lambda i, p: (0, 0, 0)), weight, weight],
+            out_specs=pl.BlockSpec((2 * rows, block), lambda i, p: (0, i)),
+            scratch_shapes=[pltpu.VMEM((2 * rows, width), BF16)],
+        ),
+        out_shape=jax.ShapeDtypeStruct((2 * rows, units), BF16),
+        compiler_params=pltpu.CompilerParams(
+            dimension_semantics=("arbitrary",), vmem_limit_bytes=40 << 20
+        ),
+        name="up",
+    )(place, *pieces, gain, gate_w, up_w)
+
+
+def down_body(first, place_ref, hidden_ref, down_ref, share_ref, keep_ref, send_ref):
+    rows = keep_ref.shape[1]
+    out = jnp.dot(hidden_ref[...], down_ref[...], preferred_element_type=F32)
+    share = share_ref[...]
+    for i in range(out.shape[1] // 128):
+        cols = slice(i * 128, (i + 1) * 128)
+        scaled = out[:, cols] * share
+        keep_ref[0, :, cols] = scaled[:rows]
+        send_ref[0, :, cols] = scaled[rows:].astype(BF16)
+
+
+def down_call(place, hidden, down_w, share, first, count):
+    both, units = hidden.shape
+    rows = both // 2
+    local = down_w.shape[1] // 4
+    piece = pl.BlockSpec((1, rows, local), lambda i, p: (i, 0, 0))
+    return pl.pallas_call(
+        functools.partial(down_body, first),
+        grid_spec=pltpu.PrefetchScalarGridSpec(
+            num_scalar_prefetch=1,
+            grid=(count,),
+            in_specs=[
+                pl.BlockSpec((both, units), lambda i, p: (0, 0)),
+                pl.BlockSpec((units, local), lambda i, p: (0, p[1] ^ (i + first))),
+                pl.BlockSpec((both, 128), lambda i, p: (0, 0)),
+            ],
+            out_specs=[piece, piece],
+        ),
+        out_shape=[
+            jax.ShapeDtypeStruct((count, rows, local), F32),
+            jax.ShapeDtypeStruct((count, rows, local), BF16),
+        ],
+        compiler_params=pltpu.CompilerParams(
+            dimension_semantics=("arbitrary",), vmem_limit_bytes=40 << 20
+        ),
+        name="down",
+    )(place, hidden, down_w, share)
+
+
+def attend_body(place_ref, *refs):
+    pieces = refs[:4]
+    gain_ref, cos_ref, sin_ref, bias_ref = refs[4:8]
+    sources = refs[8:14]
+    out_ref = refs[14]
+    normed = refs[15]
+    buffers = refs[16:22]
+    sems = refs[22]
+    rows, local = pieces[0].shape
+    half = local // 2
+    group, hid, sect = place_ref[0], place_ref[1], place_ref[2]
+    copies = [
+        pltpu.make_async_copy(src, dst, sems.at[i])
+        for i, (src, dst) in enumerate(zip(sources, buffers))
+    ]
+    for c in copies:
+        c.start()
+
+    def store(k, here, values):
+        normed[2 * (hid ^ k), here, :] = values[:, :half]
+        normed[2 * (hid ^ k) + 1, here, :] = values[:, half:]
+
+    norm_rows(pieces, gain_ref, lambda k: hid ^ k, store, rows, 16)
+    total = None
+    for i in range(6):
+        copies[i].wait()
+        if i < 2:
+            base = 2 * (sect ^ i)
+            parts = [(base, slice(0, half)), (base + 1, slice(half, 2 * half))]
+        else:
+            which = group if i % 2 == 0 else 1 - group
+            parts = [(2 * (sect ^ (2 if i < 4 else 3)) + which, slice(0, half))]
+        for at, where in parts:
+            term = jnp.dot(normed[at], buffers[i][where, :], preferred_element_type=F32)
+            total = term if total is None else total + term
+    heads = local // HD
+    kv_heads = (total.shape[1] - local) // (2 * HD)
+    cos, sin, bias = cos_ref[...], sin_ref[...], bias_ref[...]
+
+    def turned(x):
+        return (x * cos + pltpu.roll(x, HD // 2, 1) * sin).astype(BF16)
+
+    for g in range(kv_heads):
+        key = turned(total[:, local + g * HD : local + (g + 1) * HD])
+        at = local + (kv_heads + g) * HD
+        val = total[:, at : at + HD].astype(BF16)
+        for r in range(heads // kv_heads):
+            cols = slice((g * (heads // kv_heads) + r) * HD, (g * (heads // kv_heads) + r + 1) * HD)
+            query = turned(total[:, cols])
+            scores = lax.dot_general(
+                query, key, (((1,), (1,)), ((), ())), preferred_element_type=F32
+            ) * (1.0 / math.sqrt(HD)) + bias
+            weights = jnp.exp(scores - jnp.max(scores, axis=1, keepdims=True))
+            probs = (weights / jnp.sum(weights, axis=1, keepdims=True)).astype(BF16)
+            out_ref[:, cols] = jnp.dot(probs, val, preferred_element_type=F32).astype(BF16)
+
+
+def attend_call(place, pieces, gain, cos, sin, bias, weights):
+    rows, local = pieces[0].shape
+    vmem = pl.BlockSpec(memory_space=pltpu.VMEM)
+    return pl.pallas_call(
+        attend_body,
+        in_specs=[pl.BlockSpec(memory_space=pltpu.SMEM)]
+        + [vmem] * 8
+        + [pl.BlockSpec(memory_space=pl.ANY)] * 6,
+        out_specs=vmem,
+        out_shape=jax.ShapeDtypeStruct((rows, local), BF16),
+        scratch_shapes=[pltpu.VMEM((8, rows, local // 2), BF16)]
+        + [pltpu.VMEM(w.shape, BF16) for w in weights]
+        + [pltpu.SemaphoreType.DMA((6,))],
+        compiler_params=pltpu.CompilerParams(vmem_limit_bytes=40 << 20),
+        name="attend",
+    )(place, *pieces, gain, cos, sin, bias, *weights)
+
+
+def swap(value, axis, size, by):
+    return lax.ppermute(value, axis, [(i, i ^ by) for i in range(size)])
+
+
+def position_tables(lengths, count):
+    ends = jnp.cumsum(lengths, dtype=jnp.int32)
+    places = jnp.arange(count, dtype=jnp.int32)
+    after = (places[:, None] >= ends[None, :]).astype(jnp.int32)
+    doc_ids = jnp.sum(after, axis=1, dtype=jnp.int32)
+    starts = jnp.sum(after * lengths[None, :], axis=1, dtype=jnp.int32)
+    position = (places - starts).astype(F32)
+    half = HD // 2
+    freqs = jnp.exp(jnp.arange(half, dtype=F32) * (-2.0 * math.log(10000.0) / HD))
+    angles = position[:, None] * freqs[None, :]
+    cosine = jnp.cos(angles)
+    sine = jnp.sin(angles)
+    allowed = (doc_ids[:, None] == doc_ids[None, :]) & (places[None, :] <= places[:, None])
+    bias = jnp.where(allowed, 0.0, -jnp.inf).astype(F32)
+    return (
+        jnp.concatenate([cosine, cosine], axis=1),
+        jnp.concatenate([-sine, sine], axis=1),
+        bias,
+    )
+
+
+def on_grid(
+    resid, moe_gain, routes, gate_q, doc_lengths, w_gate, w_up, w_down, attn_gain, w_q, w_k, w_v
+):
+    tokens, local = resid.shape
+    group = lax.axis_index("groups")
+    sect = lax.axis_index("sect")
+    hid = lax.axis_index("hid")
+    place = jnp.stack([group, hid, sect]).astype(jnp.int32)
+
+    over_hid = lambda v, by: swap(v, "hid", 4, by)
+    over_core = lambda v: swap(v, "sect", 4, 1)
+    over_chip = lambda v: swap(v, "sect", 4, 2)
+    over_group = lambda v: swap(v, "groups", 2, 1)
+
+    own = [resid, over_hid(resid, 1), over_hid(resid, 2), over_hid(resid, 3)]
+    own_pair = own + [over_core(v) for v in own]
+    far = [over_chip(v) for v in own]
+    far_pair = far + [over_core(v) for v in far]
+
+    weights = gate_q.astype(F32) / 256.0
+    shares = []
+    for j in range(4):
+        mine = jnp.sum(jnp.where(routes == (sect ^ j), weights, 0.0), axis=1).reshape(1, tokens)
+        shares.append(mine if j == 0 else swap(mine, "sect", 4, j))
+    wide = [jnp.broadcast_to(v.reshape(tokens, 1), (tokens, 128)) for v in shares]
+    near_share = jnp.concatenate(wide[:2], axis=0)
+    far_share = jnp.concatenate(wide[2:], axis=0)
+
+    w_all = jnp.concatenate([w_q, w_k, w_v], axis=1)
+    w_half = lax.dynamic_slice_in_dim(w_all, group * (local // 2), local // 2, axis=0)
+    w_far = over_chip(w_half)
+    w_far_other = over_group(w_far)
+    proj = [w_all, over_core(w_all), w_far, w_far_other, over_core(w_far), over_core(w_far_other)]
+
+    gain = moe_gain.reshape(4, 1, local)
+    hidden = up_call(place, own_pair, gain, w_gate[0], w_up[0])
+    near_keep, near_send = down_call(place, hidden, w_down[0], near_share, 0, 4)
+    near_got = over_core(near_send)
+    near = near_keep + near_got.astype(F32)
+
+    hidden_far = up_call(place, far_pair, gain, w_gate[0], w_up[0])
+    parts = [None] * 4
+    for k in (3, 2, 1, 0):
+        keep, send = down_call(place, hidden_far, w_down[0], far_share, k, 1)
+        summed = (keep[0] + over_core(send[0]).astype(F32)).astype(BF16)
+        part = near[k] + over_chip(summed).astype(F32)
+        parts[k] = part if k == 0 else over_hid(part.astype(BF16), k)
+    mixture = parts[0]
+    for k in (1, 2, 3):
+        mixture = mixture + parts[k].astype(F32)
+    new_local = (resid.astype(F32) + mixture).astype(BF16)
+
+    rows = [new_local, over_hid(new_local, 1), over_hid(new_local, 2), over_hid(new_local, 3)]
+    cos, sin, bias = position_tables(doc_lengths[0], tokens)
+    context = attend_call(place, rows, attn_gain.reshape(4, 1, local), cos, sin, bias, proj)
+    return (new_local, context)
 
 
 def layer_norm(values, gain):
@@ -145,6 +417,9 @@
         P("sect", "hid"),
     )
     out_specs = (P(("groups", "sect"), "hid"), P(("groups", "sect"), "hid"))
+    plan = on_device
+    if dict(mesh.shape) == {"groups": 2, "sect": 4, "hid": 4}:
+        plan = on_grid
     return jax.shard_map(
-        on_device, mesh=mesh, in_specs=in_specs, out_specs=out_specs, check_vma=False
-    )
+        plan, mesh=mesh, in_specs=in_specs, out_specs=out_specs, check_vma=False
+    )

time: 451 us -> 216 us (0.48)
  waiting for transfers between devices: 318 us -> 103 us
  blocking collectives: 51.9 us -> 0 us
  Pallas kernels: 0 us -> 43 us
  starting transfers between devices: 4.15 us -> 40.5 us
  matrix products: 35.8 us -> 0 us
  between operations: 14.4 us -> 1.05 us
  local copies, waits for them, and re-layouts: 12.6 us -> 19.8 us
  other arithmetic: 12.8 us -> 7.44 us
    all_gather x5 -> x0, waiting for transfers between devices: 148 us -> none  [the longest x1 57.5 us: on_device(): lax.all_gather(w_q, 'sect', axis=0, tiled=True)]
    reduce_scatter x1 -> x0, waiting for transfers between devices: 143 us -> none  [on_device(): mine = lax.psum_scatter(outputs, 'hid', scatter_dimension=1, tiled=True)]
    ppermute x0 -> x38, waiting for transfers between devices: none -> 103 us  [swap(): return lax.ppermute(value, axis, [(i, i ^ by) for i in range(size)])]
    all_to_all x1 -> x0, blocking collectives: 51.9 us -> none  [on_device(): lax.all_to_all(outgoing, 'sect', split_axis=0, concat_axis=0, tiled=True)]
    pallas_call x0 -> x8, Pallas kernels: none -> 43 us  [the longest x2 25.2 us: up_call(): pl.pallas_call(up_body, grid_spec=pltpu.PrefetchScalarGridSpec(num_scalar...]
    ppermute x0 -> x38, starting transfers between devices: none -> 40.5 us  [swap(): return lax.ppermute(value, axis, [(i, i ^ by) for i in range(size)])]
    dot_general x7 -> x0, matrix products: 35.4 us -> none  [the longest x1 19.1 us: on_device(): outputs = jnp.dot(hidden, down_w, preferred_element_type=jnp.float32)]
    all_to_all x1 -> x0, waiting for transfers between devices: 25.3 us -> none  [on_device(): lax.all_to_all(mine.reshape(sections, capacity, local_width), 'sect', spl...]
  transfers between devices with their start and end apart: 7 -> 38, of which waited for: 7 -> 17; matrix products, arithmetic and copies ran while one was open for 4% -> 4% of each run, Pallas kernels for 0% -> 16%
where the time goes in v1:
time: 216 us; the launch traced here: 215 us
  waiting for transfers between devices  103 us (48%)
  Pallas kernels  43 us (20%)
  starting transfers between devices  40.5 us (19%)
  local copies, waits for them, and re-layouts  19.8 us (9%)
  other arithmetic  7.44 us (3%)
    ppermute x38, waiting for transfers between devices, swap(): return lax.ppermute(value, axis, [(i, i ^ by) for i in range(size)])  103 us
    ppermute x38, starting transfers between devices, swap(): return lax.ppermute(value, axis, [(i, i ^ by) for i in range(size)])  40.5 us
    pallas_call x2, Pallas kernels, up_call(): pl.pallas_call(up_body, grid_spec=pltpu.PrefetchScalarGridSpec(num_scalar...  25.2 us
    unnamed x42, local copies, waits for them, and re-layouts  16.5 us
    pallas_call x5, Pallas kernels, down_call(): pl.pallas_call(functools.partial(down_body, first), grid_spec=pltpu.Prefe...  9.05 us
    pallas_call x1, Pallas kernels, attend_call(): pl.pallas_call(attend_body, in_specs=[pl.BlockSpec(memory_space=pltpu.SME...  8.71 us
  transfers between devices with their start and end apart: 38, of which 17 were waited for; matrix products, arithmetic and copies ran while one was open for 4% of the time, Pallas kernels for 16%

profile of v1, /device:TPU:0, one launch (start us, length us, event | category | flops | bytes accessed | tf_op | source)
XLA Modules:
  0.0 215.0 jit_solution(876200139311681481)
XLA Ops:
  6.0 2.9 %collective-permute-start.34 = (bf16[512,1536]{1,0:T(8,128)(2,1)}, bf16[512,1536]{1,0:T(8,128)(2,1)}, u32[]{:S(2)}, u32[]{:S(2)}) collective-permute-start(bf16[512,1536]{1,0:T(8,128)(2,1)} %constant_dynamic-slice_fusion), channel_id=1, source_target_pairs={{0,8},{4,12},{8,0},{12,4},{1,9},{5,13},{9,1},{13,5},{2,10},{6,14},... | collective-permute-start | bytes 4718600 | tf_op jit(solution)/shard_map/ppermute | solution.py:203
  8.9 3.6 %collective-permute-start.2 = (bf16[128,1024]{1,0:T(8,128)(2,1)S(1)}, bf16[128,1024]{1,0:T(8,128)(2,1)}, u32[]{:S(2)}, u32[]{:S(2)}) collective-permute-start(bf16[128,1024]{1,0:T(8,128)(2,1)S(1)} %copy-done.4), channel_id=1, source_target_pairs={{0,3},{1,2},{2,1},{3,0},{4,7},{5,6},{6,5},{7,4},{8,11},{9,10},{10,... | collective-permute-start | bytes 786440 | tf_op jit(solution)/shard_map/ppermute | solution.py:203
  14.8 28.8 %collective-permute-done.17 = f32[1,128]{1,0:T(1,128)S(1)} collective-permute-done((f32[1,128]{1,0:T(1,128)S(1)}, f32[1,128]{1,0:T(1,128)S(1)}, u32[]{:S(2)}, u32[]{:S(2)}) %collective-permute-start.17) | collective-permute-done | bytes 544 | tf_op jit(solution)/shard_map/ppermute | solution.py:203
  43.9 2.7 %collective-permute-done.18 = f32[1,128]{1,0:T(1,128)S(1)} collective-permute-done((f32[1,128]{1,0:T(1,128)S(1)}, f32[1,128]{1,0:T(1,128)S(1)}, u32[]{:S(2)}, u32[]{:S(2)}) %collective-permute-start.18) | collective-permute-done | bytes 544 | tf_op jit(solution)/shard_map/ppermute | solution.py:203
  50.6 5.1 %collective-permute-done.9.refs_0_ = bf16[128,1024]{1,0:T(8,128)(2,1)S(1)} collective-permute-done((bf16[128,1024]{1,0:T(8,128)(2,1)S(1)}, bf16[128,1024]{1,0:T(8,128)(2,1)S(1)}, u32[]{:S(2)}, u32[]{:S(2)}) %collective-permute-start.9) | collective-permute-done | bytes 262176 | tf_op jit(solution)/shard_map/ppermute | solution.py:203
  56.4 5.0 %collective-permute-done.12.refs_3_ = bf16[128,1024]{1,0:T(8,128)(2,1)} collective-permute-done((bf16[128,1024]{1,0:T(8,128)(2,1)}, bf16[128,1024]{1,0:T(8,128)(2,1)}, u32[]{:S(2)}, u32[]{:S(2)}) %collective-permute-start.12) | collective-permute-done | bytes 262176 | tf_op jit(solution)/shard_map/ppermute | solution.py:203
  61.5 5.6 %collective-permute-done.11.refs_2_ = bf16[128,1024]{1,0:T(8,128)(2,1)} collective-permute-done((bf16[128,1024]{1,0:T(8,128)(2,1)}, bf16[128,1024]{1,0:T(8,128)(2,1)}, u32[]{:S(2)}, u32[]{:S(2)}) %collective-permute-start.11) | collective-permute-done | bytes 262176 | tf_op jit(solution)/shard_map/ppermute | solution.py:203
  67.1 4.8 %collective-permute-done.10.refs_1_ = bf16[128,1024]{1,0:T(8,128)(2,1)} collective-permute-done((bf16[128,1024]{1,0:T(8,128)(2,1)}, bf16[128,1024]{1,0:T(8,128)(2,1)}, u32[]{:S(2)}, u32[]{:S(2)}) %collective-permute-start.10) | collective-permute-done | bytes 262176 | tf_op jit(solution)/shard_map/ppermute | solution.py:203
  73.9 3.5 %copy-done = bf16[1,4096,1024]{2,1,0:T(8,128)(2,1)S(1)} copy-done((bf16[1,4096,1024]{2,1,0:T(8,128)(2,1)S(1)}, bf16[1,4096,1024]{2,1,0:T(8,128)(2,1)}, u32[]{:S(2)}) %copy-start) | copy-done | bytes 8388632
  79.4 12.9 %up.3.hidden_ref = bf16[256,1024]{1,0:T(8,128)(2,1)S(1)} custom-call(s32[3]{0:T(128)S(1)} %pad_add_fusion.place_ref, bf16[128,1024]{1,0:T(8,128)(2,1)S(1)} %copy-done.8, bf16[128,1024]{1,0:T(8,128)(2,1)} %collective-permute-done.10.refs_1_, bf16[128,1024]{1,0:T(8,128)(2,1)} %collective-permute-done.11.refs_2_, ...), custom_call_target="tpu_custom_call" | custom-call | tf_op jit(solution)/shard_map/up/pallas_call | solution.py:70
  96.5 3.4 %copy-done.1 = bf16[1,4096,1024]{2,1,0:T(8,128)(2,1)S(1)} copy-done((bf16[1,4096,1024]{2,1,0:T(8,128)(2,1)S(1)}, bf16[1,4096,1024]{2,1,0:T(8,128)(2,1)}, u32[]{:S(2)}) %copy-start.1) | copy-done | bytes 8388632
  99.9 12.3 %up.2.hidden_ref = bf16[256,1024]{1,0:T(8,128)(2,1)S(1)} custom-call(s32[3]{0:T(128)S(1)} %pad_add_fusion.place_ref, bf16[128,1024]{1,0:T(8,128)(2,1)S(1)} %copy-done.4, bf16[128,1024]{1,0:T(8,128)(2,1)} %collective-permute-done.refs_1_, bf16[128,1024]{1,0:T(8,128)(2,1)} %collective-permute-done.1.refs_2_, bf16[128,1024]{1,0:T(8,128)(2,1)} %collective-permute-done.2.refs_3_, ...), custom_call_target="tpu_custom_call" | custom-call | tf_op jit(solution)/shard_map/up/pallas_call | solution.py:70
  114.1 4.0 %down.5 = (f32[4,128,1024]{2,1,0:T(8,128)S(1)}, bf16[4,128,1024]{2,1,0:T(8,128)(2,1)S(1)}) custom-call(s32[3]{0:T(128)S(1)} %pad_add_fusion.place_ref, bf16[256,1024]{1,0:T(8,128)(2,1)S(1)} %copy-done.3, bf16[1024,4096]{1,0:T(8,128)(2,1)S(1)} %bitcast.70, f32[256,128]{1,0:T(8,128)S(1)} %broadcast.16.share_ref), custom_call_target="tpu_custom_call" | custom-call | tf_op jit(solution)/shard_map/down/pallas_call | solution.py:104
  130.0 5.3 %collective-permute-done.28 = bf16[128,1024]{1,0:T(8,128)(2,1)S(1)} collective-permute-done((bf16[128,1024]{1,0:T(8,128)(2,1)S(1)}, bf16[128,1024]{1,0:T(8,128)(2,1)S(1)}, u32[]{:S(2)}, u32[]{:S(2)}) %collective-permute-start.28) | collective-permute-done | bytes 262176 | tf_op jit(solution)/shard_map/ppermute | solution.py:203
  135.8 5.0 %collective-permute-done.25 = bf16[128,1024]{1,0:T(8,128)(2,1)S(1)} collective-permute-done((bf16[128,1024]{1,0:T(8,128)(2,1)S(1)}, bf16[128,1024]{1,0:T(8,128)(2,1)S(1)}, u32[]{:S(2)}, u32[]{:S(2)}) %collective-permute-start.25) | collective-permute-done | bytes 262176 | tf_op jit(solution)/shard_map/ppermute | solution.py:203
  141.4 5.1 %collective-permute-done.22 = bf16[128,1024]{1,0:T(8,128)(2,1)S(1)} collective-permute-done((bf16[128,1024]{1,0:T(8,128)(2,1)S(1)}, bf16[128,1024]{1,0:T(8,128)(2,1)S(1)}, u32[]{:S(2)}, u32[]{:S(2)}) %collective-permute-start.22) | collective-permute-done | bytes 262176 | tf_op jit(solution)/shard_map/ppermute | solution.py:203
  151.6 3.6 %collective-permute-start.29 = (bf16[128,1024]{1,0:T(8,128)(2,1)}, bf16[128,1024]{1,0:T(8,128)(2,1)S(1)}, u32[]{:S(2)}, u32[]{:S(2)}) collective-permute-start(bf16[128,1024]{1,0:T(8,128)(2,1)} %get-tuple-element.29), channel_id=1, source_target_pairs={{0,3},{1,2},{2,1},{3,0},{4,7},{5,6},{6,5},{7,4},{8,11},{9,10},{10,... | collective-permute-start | bytes 786440 | tf_op jit(solution)/shard_map/ppermute | solution.py:203
  155.2 3.4 %collective-permute-start.26 = (bf16[128,1024]{1,0:T(8,128)(2,1)}, bf16[128,1024]{1,0:T(8,128)(2,1)S(1)}, u32[]{:S(2)}, u32[]{:S(2)}) collective-permute-start(bf16[128,1024]{1,0:T(8,128)(2,1)} %get-tuple-element.30), channel_id=1, source_target_pairs={{0,2},{1,3},{2,0},{3,1},{4,6},{5,7},{6,4},{7,5},{8,10},{9,11},{10,... | collective-permute-start | bytes 786440 | tf_op jit(solution)/shard_map/ppermute | solution.py:203
  159.2 4.5 %collective-permute-done.29 = bf16[128,1024]{1,0:T(8,128)(2,1)S(1)} collective-permute-done((bf16[128,1024]{1,0:T(8,128)(2,1)}, bf16[128,1024]{1,0:T(8,128)(2,1)S(1)}, u32[]{:S(2)}, u32[]{:S(2)}) %collective-permute-start.29) | collective-permute-done | bytes 262176 | tf_op jit(solution)/shard_map/ppermute | solution.py:203
  163.7 13.8 %collective-permute-done.26 = bf16[128,1024]{1,0:T(8,128)(2,1)S(1)} collective-permute-done((bf16[128,1024]{1,0:T(8,128)(2,1)}, bf16[128,1024]{1,0:T(8,128)(2,1)S(1)}, u32[]{:S(2)}, u32[]{:S(2)}) %collective-permute-start.26) | collective-permute-done | bytes 262176 | tf_op jit(solution)/shard_map/ppermute | solution.py:203
  182.5 8.4 %collective-permute-done.32.refs_3_ = bf16[128,1024]{1,0:T(8,128)(2,1)S(1)} collective-permute-done((bf16[128,1024]{1,0:T(8,128)(2,1)}, bf16[128,1024]{1,0:T(8,128)(2,1)S(1)}, u32[]{:S(2)}, u32[]{:S(2)}) %collective-permute-start.32) | collective-permute-done | bytes 262176 | tf_op jit(solution)/shard_map/ppermute | solution.py:203
  190.9 9.1 %collective-permute-start.30 = (bf16[128,1024]{1,0:T(8,128)(2,1)}, bf16[128,1024]{1,0:T(8,128)(2,1)}, u32[]{:S(2)}, u32[]{:S(2)}) collective-permute-start(bf16[128,1024]{1,0:T(8,128)(2,1)} %fusion.11.refs_0_), channel_id=1, source_target_pairs={{0,1},{1,0},{2,3},{3,2},{4,5},{5,4},{6,7},{7,6},{8,9},{9,8},{10,11... | collective-permute-start | bytes 786440 | tf_op jit(solution)/shard_map/ppermute | solution.py:203
  202.9 2.7 %collective-permute-done.30.refs_1_ = bf16[128,1024]{1,0:T(8,128)(2,1)} collective-permute-done((bf16[128,1024]{1,0:T(8,128)(2,1)}, bf16[128,1024]{1,0:T(8,128)(2,1)}, u32[]{:S(2)}, u32[]{:S(2)}) %collective-permute-start.30) | collective-permute-done | bytes 262176 | tf_op jit(solution)/shard_map/ppermute | solution.py:203
  206.3 8.7 %attend.1 = bf16[128,1024]{1,0:T(8,128)(2,1)} custom-call(s32[3]{0:T(128)S(1)} %copy-done.12, bf16[128,1024]{1,0:T(8,128)(2,1)} %fusion.11.refs_0_, bf16[128,1024]{1,0:T(8,128)(2,1)} %collective-permute-done.30.refs_1_, bf16[128,1024]{1,0:T(8,128)(2,1)} %collective-permute-done.31.refs_2_, bf16[128,1024]{1,0:T(8,128)(2,1)S(1)} %collective-permute-done.32.refs_3_, ...), custom_call_target="tpu_custom_call" | custom-call | tf_op jit(solution)/shard_map/attend/pallas_call | solution.py:187
  (127 shorter events, 49.7 us)
Async XLA Ops:
  6.0 89.0 %collective-permute-start.34 = (bf16[512,1536]{1,0:T(8,128)(2,1)}, bf16[512,1536]{1,0:T(8,128)(2,1)}, u32[]{:S(2)}, u32[]{:S(2)}) collective-permute-start(bf16[512,1536]{1,0:T(8,128)(2,1)} %constant_dynamic-slice_fusion), channel_id=1, source_target_pairs={{0,8},{4,12},{8,0},{12,4},{1,9},{5,13},{9,1},{13,5},{2,10},{6,14},... | collective-permute-start | bytes 4718600 | tf_op jit(solution)/shard_map/ppermute | solution.py:203
  8.9 39.4 %collective-permute-start.2 = (bf16[128,1024]{1,0:T(8,128)(2,1)S(1)}, bf16[128,1024]{1,0:T(8,128)(2,1)}, u32[]{:S(2)}, u32[]{:S(2)}) collective-permute-start(bf16[128,1024]{1,0:T(8,128)(2,1)S(1)} %copy-done.4), channel_id=1, source_target_pairs={{0,3},{1,2},{2,1},{3,0},{4,7},{5,6},{6,5},{7,4},{8,11},{9,10},{10,... | collective-permute-start | bytes 786440 | tf_op jit(solution)/shard_map/ppermute | solution.py:203
  12.5 36.1 %collective-permute-start.1 = (bf16[128,1024]{1,0:T(8,128)(2,1)S(1)}, bf16[128,1024]{1,0:T(8,128)(2,1)}, u32[]{:S(2)}, u32[]{:S(2)}) collective-permute-start(bf16[128,1024]{1,0:T(8,128)(2,1)S(1)} %copy-done.4), channel_id=1, source_target_pairs={{0,2},{1,3},{2,0},{3,1},{4,6},{5,7},{6,4},{7,5},{8,10},{9,11},{10,... | collective-permute-start | bytes 786440 | tf_op jit(solution)/shard_map/ppermute | solution.py:203
  12.5 37.9 %collective-permute-start = (bf16[128,1024]{1,0:T(8,128)(2,1)S(1)}, bf16[128,1024]{1,0:T(8,128)(2,1)}, u32[]{:S(2)}, u32[]{:S(2)}) collective-permute-start(bf16[128,1024]{1,0:T(8,128)(2,1)S(1)} %copy-done.4), channel_id=1, source_target_pairs={{0,1},{1,0},{2,3},{3,2},{4,5},{5,4},{6,7},{7,6},{8,9},{9,8},{10,11... | collective-permute-start | bytes 786440 | tf_op jit(solution)/shard_map/ppermute | solution.py:203
  14.5 29.1 %collective-permute-start.17 = (f32[1,128]{1,0:T(1,128)S(1)}, f32[1,128]{1,0:T(1,128)S(1)}, u32[]{:S(2)}, u32[]{:S(2)}) collective-permute-start(f32[1,128]{1,0:T(1,128)S(1)} %bitcast.83), channel_id=1, source_target_pairs={{0,8},{4,12},{8,0},{12,4},{1,9},{5,13},{9,1},{13,5},{2,10},{6,14},... | collective-permute-start | bytes 1544 | tf_op jit(solution)/shard_map/ppermute | solution.py:203
  48.3 13.1 %collective-permute-start.12 = (bf16[128,1024]{1,0:T(8,128)(2,1)}, bf16[128,1024]{1,0:T(8,128)(2,1)}, u32[]{:S(2)}, u32[]{:S(2)}) collective-permute-start(bf16[128,1024]{1,0:T(8,128)(2,1)} %collective-permute-done.2.refs_3_), channel_id=1, source_target_pairs={{0,8},{4,12},{8,0},{12,4},{1,9},{5,13},{9,1},{13,5},{2,10},{6,14},... | collective-permute-start | bytes 786440 | tf_op jit(solution)/shard_map/ppermute | solution.py:203
  48.6 18.5 %collective-permute-start.11 = (bf16[128,1024]{1,0:T(8,128)(2,1)}, bf16[128,1024]{1,0:T(8,128)(2,1)}, u32[]{:S(2)}, u32[]{:S(2)}) collective-permute-start(bf16[128,1024]{1,0:T(8,128)(2,1)} %collective-permute-done.1.refs_2_), channel_id=1, source_target_pairs={{0,8},{4,12},{8,0},{12,4},{1,9},{5,13},{9,1},{13,5},{2,10},{6,14},... | collective-permute-start | bytes 786440 | tf_op jit(solution)/shard_map/ppermute | solution.py:203
  50.4 21.5 %collective-permute-start.10 = (bf16[128,1024]{1,0:T(8,128)(2,1)}, bf16[128,1024]{1,0:T(8,128)(2,1)}, u32[]{:S(2)}, u32[]{:S(2)}) collective-permute-start(bf16[128,1024]{1,0:T(8,128)(2,1)} %collective-permute-done.refs_1_), channel_id=1, source_target_pairs={{0,8},{4,12},{8,0},{12,4},{1,9},{5,13},{9,1},{13,5},{2,10},{6,14},... | collective-permute-start | bytes 786440 | tf_op jit(solution)/shard_map/ppermute | solution.py:203
  55.7 16.1 %collective-permute-start.13 = (bf16[128,1024]{1,0:T(8,128)(2,1)S(1)}, bf16[128,1024]{1,0:T(8,128)(2,1)S(1)}, u32[]{:S(2)}, u32[]{:S(2)}) collective-permute-start(bf16[128,1024]{1,0:T(8,128)(2,1)S(1)} %collective-permute-done.9.refs_0_), channel_id=1, source_target_pairs={{0,4},{4,0},{8,12},{12,8},{1,5},{5,1},{9,13},{13,9},{2,6},{6,2},{1... | collective-permute-start | bytes 786440 | tf_op jit(solution)/shard_map/ppermute | solution.py:203
  72.6 22.0 %collective-permute-start.3 = (bf16[128,1024]{1,0:T(8,128)(2,1)S(1)}, bf16[128,1024]{1,0:T(8,128)(2,1)}, u32[]{:S(2)}, u32[]{:S(2)}) collective-permute-start(bf16[128,1024]{1,0:T(8,128)(2,1)S(1)} %copy-done.4), channel_id=1, source_target_pairs={{0,4},{4,0},{8,12},{12,8},{1,5},{5,1},{9,13},{13,9},{2,6},{6,2},{1... | collective-permute-start | bytes 786440 | tf_op jit(solution)/shard_map/ppermute | solution.py:203
  73.2 23.3 %collective-permute-start.6 = (bf16[128,1024]{1,0:T(8,128)(2,1)}, bf16[128,1024]{1,0:T(8,128)(2,1)S(1)}, u32[]{:S(2)}, u32[]{:S(2)}) collective-permute-start(bf16[128,1024]{1,0:T(8,128)(2,1)} %collective-permute-done.2.refs_3_), channel_id=1, source_target_pairs={{0,4},{4,0},{8,12},{12,8},{1,5},{5,1},{9,13},{13,9},{2,6},{6,2},{1... | collective-permute-start | bytes 786440 | tf_op jit(solution)/shard_map/ppermute | solution.py:203
  73.2 23.2 %collective-permute-start.5 = (bf16[128,1024]{1,0:T(8,128)(2,1)}, bf16[128,1024]{1,0:T(8,128)(2,1)S(1)}, u32[]{:S(2)}, u32[]{:S(2)}) collective-permute-start(bf16[128,1024]{1,0:T(8,128)(2,1)} %collective-permute-done.1.refs_2_), channel_id=1, source_target_pairs={{0,4},{4,0},{8,12},{12,8},{1,5},{5,1},{9,13},{13,9},{2,6},{6,2},{1... | collective-permute-start | bytes 786440 | tf_op jit(solution)/shard_map/ppermute | solution.py:203
  73.7 22.7 %collective-permute-start.4 = (bf16[128,1024]{1,0:T(8,128)(2,1)}, bf16[128,1024]{1,0:T(8,128)(2,1)S(1)}, u32[]{:S(2)}, u32[]{:S(2)}) collective-permute-start(bf16[128,1024]{1,0:T(8,128)(2,1)} %collective-permute-done.refs_1_), channel_id=1, source_target_pairs={{0,4},{4,0},{8,12},{12,8},{1,5},{5,1},{9,13},{13,9},{2,6},{6,2},{1... | collective-permute-start | bytes 786440 | tf_op jit(solution)/shard_map/ppermute | solution.py:203
  94.5 28.1 %collective-permute-start.27 = (bf16[128,1024]{1,0:T(8,128)(2,1)S(1)}, bf16[128,1024]{1,0:T(8,128)(2,1)}, u32[]{:S(2)}, u32[]{:S(2)}) collective-permute-start(bf16[128,1024]{1,0:T(8,128)(2,1)S(1)} %bitcast.76), channel_id=1, source_target_pairs={{0,4},{4,0},{8,12},{12,8},{1,5},{5,1},{9,13},{13,9},{2,6},{6,2},{1... | collective-permute-start | bytes 786440 | tf_op jit(solution)/shard_map/ppermute | solution.py:203
  94.9 46.0 %collective-permute-start.35 = (bf16[512,1536]{1,0:T(8,128)(2,1)}, bf16[512,1536]{1,0:T(8,128)(2,1)}, u32[]{:S(2)}, u32[]{:S(2)}) collective-permute-start(bf16[512,1536]{1,0:T(8,128)(2,1)} %collective-permute-done.34.refs_10_), channel_id=1, source_target_pairs={{0,16},{16,0},{1,17},{17,1},{2,18},{18,2},{3,19},{19,3},{4,20},{20... | collective-permute-start | bytes 4718600 | tf_op jit(solution)/shard_map/ppermute | solution.py:203
  120.1 85.6 %collective-permute-start.33 = (bf16[1024,1536]{1,0:T(8,128)(2,1)S(1)}, bf16[1024,1536]{1,0:T(8,128)(2,1)}, u32[]{:S(2)}, u32[]{:S(2)}) collective-permute-start(bf16[1024,1536]{1,0:T(8,128)(2,1)S(1)} %constant_dynamic-update-slice_fusion.refs_8_), channel_id=1, source_target_pairs={{0,4},{4,0},{8,12},{12,8},{1,5},{5,1},{9,13},{13,9},{2,6},{6,2},{1... | collective-permute-start | bytes 9437192 | tf_op jit(solution)/shard_map/ppermute | solution.py:203
  127.5 13.4 %collective-permute-start.25 = (bf16[128,1024]{1,0:T(8,128)(2,1)S(1)}, bf16[128,1024]{1,0:T(8,128)(2,1)S(1)}, u32[]{:S(2)}, u32[]{:S(2)}) collective-permute-start(bf16[128,1024]{1,0:T(8,128)(2,1)S(1)} %fusion.13), channel_id=1, source_target_pairs={{0,8},{4,12},{8,0},{12,4},{1,9},{5,13},{9,1},{13,5},{2,10},{6,14},... | collective-permute-start | bytes 786440 | tf_op jit(solution)/shard_map/ppermute | solution.py:203
  129.0 17.5 %collective-permute-start.22 = (bf16[128,1024]{1,0:T(8,128)(2,1)S(1)}, bf16[128,1024]{1,0:T(8,128)(2,1)S(1)}, u32[]{:S(2)}, u32[]{:S(2)}) collective-permute-start(bf16[128,1024]{1,0:T(8,128)(2,1)S(1)} %fusion.14), channel_id=1, source_target_pairs={{0,8},{4,12},{8,0},{12,4},{1,9},{5,13},{9,1},{13,5},{2,10},{6,14},... | collective-permute-start | bytes 786440 | tf_op jit(solution)/shard_map/ppermute | solution.py:203
  135.3 16.4 %collective-permute-start.20 = (bf16[128,1024]{1,0:T(8,128)(2,1)}, bf16[128,1024]{1,0:T(8,128)(2,1)}, u32[]{:S(2)}, u32[]{:S(2)}) collective-permute-start(bf16[128,1024]{1,0:T(8,128)(2,1)} %fusion.15), channel_id=1, source_target_pairs={{0,8},{4,12},{8,0},{12,4},{1,9},{5,13},{9,1},{13,5},{2,10},{6,14},... | collective-permute-start | bytes 786440 | tf_op jit(solution)/shard_map/ppermute | solution.py:203
  140.9 64.7 %collective-permute-start.36 = (bf16[512,1536]{1,0:T(8,128)(2,1)}, bf16[512,1536]{1,0:T(8,128)(2,1)}, u32[]{:S(2)}, u32[]{:S(2)}) collective-permute-start(bf16[512,1536]{1,0:T(8,128)(2,1)} %collective-permute-done.34.refs_10_), channel_id=1, source_target_pairs={{0,4},{4,0},{8,12},{12,8},{1,5},{5,1},{9,13},{13,9},{2,6},{6,2},{1... | collective-permute-start | bytes 4718600 | tf_op jit(solution)/shard_map/ppermute | solution.py:203
  140.9 64.7 %collective-permute-start.37 = (bf16[512,1536]{1,0:T(8,128)(2,1)}, bf16[512,1536]{1,0:T(8,128)(2,1)}, u32[]{:S(2)}, u32[]{:S(2)}) collective-permute-start(bf16[512,1536]{1,0:T(8,128)(2,1)} %collective-permute-done.35.refs_11_), channel_id=1, source_target_pairs={{0,4},{4,0},{8,12},{12,8},{1,5},{5,1},{9,13},{13,9},{2,6},{6,2},{1... | collective-permute-start | bytes 4718600 | tf_op jit(solution)/shard_map/ppermute | solution.py:203
  155.2 22.2 %collective-permute-start.26 = (bf16[128,1024]{1,0:T(8,128)(2,1)}, bf16[128,1024]{1,0:T(8,128)(2,1)S(1)}, u32[]{:S(2)}, u32[]{:S(2)}) collective-permute-start(bf16[128,1024]{1,0:T(8,128)(2,1)} %get-tuple-element.30), channel_id=1, source_target_pairs={{0,2},{1,3},{2,0},{3,1},{4,6},{5,7},{6,4},{7,5},{8,10},{9,11},{10,... | collective-permute-start | bytes 786440 | tf_op jit(solution)/shard_map/ppermute | solution.py:203
  182.4 20.5 %collective-permute-start.31 = (bf16[128,1024]{1,0:T(8,128)(2,1)}, bf16[128,1024]{1,0:T(8,128)(2,1)}, u32[]{:S(2)}, u32[]{:S(2)}) collective-permute-start(bf16[128,1024]{1,0:T(8,128)(2,1)} %fusion.11.refs_0_), channel_id=1, source_target_pairs={{0,2},{1,3},{2,0},{3,1},{4,6},{5,7},{6,4},{7,5},{8,10},{9,11},{10,... | collective-permute-start | bytes 786440 | tf_op jit(solution)/shard_map/ppermute | solution.py:203
  190.9 14.7 %collective-permute-start.30 = (bf16[128,1024]{1,0:T(8,128)(2,1)}, bf16[128,1024]{1,0:T(8,128)(2,1)}, u32[]{:S(2)}, u32[]{:S(2)}) collective-permute-start(bf16[128,1024]{1,0:T(8,128)(2,1)} %fusion.11.refs_0_), channel_id=1, source_target_pairs={{0,1},{1,0},{2,3},{3,2},{4,5},{5,4},{6,7},{7,6},{8,9},{9,8},{10,11... | collective-permute-start | bytes 786440 | tf_op jit(solution)/shard_map/ppermute | solution.py:203
  (34 other events, 321.0 us)

commit v2 on v0

--- a/solution.py
+++ b/solution.py
@@ -3,11 +3,441 @@
 import jax
 import jax.numpy as jnp
 from jax import lax
+from jax.experimental import pallas as pl
+from jax.experimental.pallas import tpu as pltpu
 from jax.sharding import PartitionSpec as P
 
 H = 32
 KVH = 8
 HD = 128
+F32 = jnp.float32
+BF16 = jnp.bfloat16
+LIMIT = 16
+SLOTS = 4
+DEEP = 1024
+ORDER = (3, 1, 2, 0)
+TINY = pl.CostEstimate(flops=1, transcendentals=0, bytes_accessed=1)
+STEP = pl.CostEstimate(flops=1 << 22, transcendentals=0, bytes_accessed=1 << 10)
+VMEM = pl.BlockSpec(memory_space=pltpu.VMEM)
+SMEM = pl.BlockSpec(memory_space=pltpu.SMEM)
+
+
+def reads(count):
+    return pl.CostEstimate(flops=1, transcendentals=0, bytes_accessed=count)
+
+
+def features(piece):
+    return pl.BlockSpec((piece.shape[0], piece.shape[1] // 1024 * 1024), lambda *_: (0, 0))
+
+
+def routing(piece):
+    return pl.BlockSpec((piece.shape[0], 128), lambda *_: (0, piece.shape[1] // 128 - 1))
+
+
+def whole(shape):
+    return pl.BlockSpec(shape, lambda *_: (0,) * len(shape))
+
+
+def stats_body(before, first_ref, *refs):
+    pieces = [first_ref] + list(refs[:-4]) if before else [first_ref] + list(refs[:-2])
+    rows, local = first_ref.shape
+    mean_ref, spread_ref = refs[-2], refs[-1]
+    for j, p in enumerate(pieces):
+        here = slice(j * rows, (j + 1) * rows)
+        values = p[...].astype(F32)
+        mean = jnp.sum(values, axis=1, keepdims=True) / local
+        values = values - mean
+        spread = jnp.sum(values * values, axis=1, keepdims=True)
+        if before:
+            seen = before * local
+            old = refs[-4][here, :]
+            gap = mean - old
+            spread = refs[-3][here, :] + spread + gap * gap * (seen * local / (seen + local))
+            mean = old + gap * (local / (seen + local))
+        mean_ref[here, :] = mean
+        spread_ref[here, :] = spread
+
+
+def stats_call(pieces, seen, before, cost, name):
+    rows = sum(p.shape[0] for p in pieces)
+    operands = list(pieces) + list(before or ())
+    return pl.pallas_call(
+        lambda *refs: stats_body(seen, *refs),
+        grid=(1,),
+        in_specs=[features(v) for v in pieces] + [whole(v.shape) for v in before or ()],
+        out_specs=[whole((rows, 1))] * 2,
+        out_shape=[jax.ShapeDtypeStruct((rows, 1), F32)] * 2,
+        compiler_params=pltpu.CompilerParams(vmem_limit_bytes=LIMIT << 20),
+        cost_estimate=cost,
+        name=name,
+    )(*operands)
+
+
+def stats_chain(groups, name):
+    before = None
+    for seen, pieces in enumerate(groups):
+        before = list(stats_call(pieces, seen, before, STEP, name))
+    return before
+
+
+def full_norm_rows(pieces, gain_ref, hid, out_ref, first, step):
+    rows, local = pieces[0].shape
+    width = local * len(pieces)
+
+    def body(i, carry):
+        at = pl.multiple_of(i * step, step)
+        values = [p[pl.ds(at, step), :].astype(F32) for p in pieces]
+        total = values[0]
+        for v in values[1:]:
+            total = total + v
+        mean = jnp.sum(total, axis=1, keepdims=True) / width
+        centered = [v - mean for v in values]
+        squares = centered[0] * centered[0]
+        for c in centered[1:]:
+            squares = squares + c * c
+        spread = jnp.sum(squares, axis=1, keepdims=True) / width
+        scale = lax.rsqrt(spread + 1e-05)
+        for k, c in enumerate(centered):
+            cols = pl.ds(pl.multiple_of((hid ^ k) * local, local), local)
+            gain = gain_ref[:, cols].astype(F32)
+            out_ref[pl.ds(first + at, step), cols] = (c * scale * gain).astype(BF16)
+        return carry
+
+    lax.fori_loop(0, rows // step, body, 0)
+
+
+def norm_rows(pieces, gain_ref, mean_ref, spread_ref, hid, out_ref, first, step):
+    rows, local = pieces[0].shape
+    width = local * len(pieces)
+    for k, p in enumerate(pieces):
+        cols = pl.ds(pl.multiple_of((hid ^ k) * local, local), local)
+        gain = gain_ref[:, cols].astype(F32)
+        for at in range(0, rows, step):
+            here = slice(first + at, first + at + step)
+            scale = lax.rsqrt(spread_ref[here, :] / width + 1e-05)
+            values = p[at : at + step, :].astype(F32) - mean_ref[here, :]
+            out_ref[here, cols] = (values * scale * gain).astype(BF16)
+
+
+def expert_body(place_ref, *refs):
+    pieces = refs[:8]
+    gain_ref, gate_hbm, up_hbm, down_hbm = refs[8:12]
+    routed, keep_ref, send_ref = refs[12:14], refs[14], refs[15]
+    normed, sums, hidden, ring, sems = refs[16:]
+    rows, local = pieces[1].shape
+    slots, deep = ring.shape[:2]
+    width, units = gate_hbm.shape
+    ups = 2 * (width // deep)
+    hid, sect = place_ref[1], place_ref[2]
+
+    def copy(n):
+        if n < ups:
+            src = (gate_hbm, up_hbm)[n % 2].at[n // 2 * deep : (n // 2 + 1) * deep, :]
+        else:
+            at = pl.multiple_of((hid ^ ORDER[n - ups]) * local, local)
+            src = down_hbm.at[:, pl.ds(at, local)]
+        return pltpu.make_async_copy(src, ring.at[n % slots], sems.at[n % slots])
+
+    for n in range(slots):
+        copy(n).start()
+    for j in range(2):
+        mine = pieces[4 * j : 4 * j + 4]
+        full_norm_rows(mine, gain_ref, hid, normed, j * rows, 64)
+    shares = []
+    for ref in routed:
+        chosen = lax.broadcasted_iota(jnp.int32, ref.shape, 1) == sect
+        units_of = jnp.sum(jnp.where(chosen, ref[...].astype(F32), 0.0), axis=1, keepdims=True)
+        shares.append(units_of / 256.0)
+    for n in range(ups + 4):
+        copy(n).wait()
+        if n < ups:
+            lhs = normed[:, n // 2 * deep : (n // 2 + 1) * deep]
+            term = jnp.dot(lhs, ring[n % slots], preferred_element_type=F32)
+            sums[n % 2] = term if n < 2 else sums[n % 2] + term
+        else:
+            if n == ups:
+                for b in range(0, units, 128):
+                    gate = sums[0, :, b : b + 128]
+                    up = sums[1, :, b : b + 128]
+                    hidden[:, b : b + 128] = (gate / (1.0 + jnp.exp(-gate)) * up).astype(BF16)
+            out = jnp.dot(hidden[...], ring[n % slots], preferred_element_type=F32)
+            keep_ref[n - ups] = out[:rows] * shares[0]
+            send_ref[n - ups] = (out[rows:] * shares[1]).astype(BF16)
+        if n + slots < ups + 4:
+            copy(n + slots).start()
+
+
+def expert_call(place, pieces, gain, gate_w, up_w, down_w, name):
+    rows, local = pieces[1].shape
+    width, units = gate_w.shape
+    once = pl.Buffered(1)
+    held = [pl.BlockSpec((rows, local), lambda *_: (0, 0), pipeline_mode=once)] * 8
+    pieces = [pltpu.with_memory_space_constraint(p, pltpu.HBM) for p in pieces]
+    routed = [pieces[0], pieces[4]]
+    shape = (4, rows, local)
+    return pl.pallas_call(
+        expert_body,
+        grid=(1,),
+        in_specs=[SMEM]
+        + held
+        + [whole(gain.shape)]
+        + [pl.BlockSpec(memory_space=pl.ANY)] * 3
+        + [routing(v) for v in routed],
+        out_specs=[whole(shape)] * 2,
+        out_shape=[jax.ShapeDtypeStruct(shape, F32), jax.ShapeDtypeStruct(shape, BF16)],
+        scratch_shapes=[
+            pltpu.VMEM((2 * rows, width), BF16),
+            pltpu.VMEM((2, 2 * rows, units), F32),
+            pltpu.VMEM((2 * rows, units), BF16),
+            pltpu.VMEM((SLOTS, DEEP, units), BF16),
+            pltpu.SemaphoreType.DMA((SLOTS,)),
+        ],
+        compiler_params=pltpu.CompilerParams(vmem_limit_bytes=26 << 20),
+        cost_estimate=TINY,
+        name=name,
+    )(place, *pieces, gain, gate_w, up_w, down_w, *routed)
+
+
+def sums_call(body, operands, outs, name):
+    return pl.pallas_call(
+        body,
+        grid=(1,),
+        in_specs=[whole(v.shape) for v in operands],
+        out_specs=[whole(shape) for shape, _ in outs],
+        out_shape=[jax.ShapeDtypeStruct(*o) for o in outs],
+        compiler_params=pltpu.CompilerParams(vmem_limit_bytes=LIMIT << 20),
+        cost_estimate=TINY,
+        name=name,
+    )(*operands)
+
+
+def core_body(keep_ref, got_ref, first_ref, second_ref):
+    for n in range(4):
+        out_ref = (first_ref, second_ref)[n // 2]
+        out_ref[n % 2] = (keep_ref[n] + got_ref[n].astype(F32)).astype(BF16)
+
+
+def chip_body(keep_ref, near_ref, far_ref, out_ref):
+    for n in range(2):
+        total = keep_ref[n] + near_ref[n].astype(F32) + far_ref[n].astype(F32)
+        out_ref[n] = total.astype(BF16)
+
+
+def pair_body(keep_ref, near_ref, far_ref, hid_ref, resid_ref, send_ref, own_ref):
+    both = []
+    for n in range(2):
+        total = keep_ref[n + 2] + near_ref[n + 2].astype(F32) + far_ref[n].astype(F32)
+        both.append(total + hid_ref[n].astype(F32))
+    send_ref[...] = both[0].astype(BF16)
+    own_ref[...] = resid_ref[...].astype(F32) + both[1]
+
+
+def last_body(own_ref, got_ref, out_ref):
+    out_ref[...] = (own_ref[...] + got_ref[...].astype(F32)).astype(BF16)
+
+
+def attend_body(place_ref, *refs):
+    pieces = refs[:4]
+    mean_ref, spread_ref, gain_ref, cos_ref, sin_ref, bias_ref = refs[4:10]
+    sources = refs[10:26]
+    out_ref, normed, total = refs[26:29]
+    weights = refs[29:45]
+    sems = refs[45]
+    rows, local = pieces[0].shape
+    half = local // 2
+    group, hid, sect = place_ref[0], place_ref[1], place_ref[2]
+    copies = [
+        pltpu.make_async_copy(src, dst, sems.at[i])
+        for i, (src, dst) in enumerate(zip(sources, weights))
+    ]
+    for c in copies:
+        c.start()
+    norm_rows(pieces, gain_ref, mean_ref, spread_ref, hid, normed, 0, 64)
+
+    def rows_of(at, count):
+        return normed[:, pl.ds(pl.multiple_of(at, 512), count)]
+
+    starts = [(sect ^ j) * local for j in range(4)]
+    mine, other = group * half, (1 - group) * half
+    halves = [rows_of(starts[j] + o, half) for j in (2, 3) for o in (mine, other)]
+    wholes = [rows_of(at, local) for at in starts]
+    plan = []
+    for c in range(2):
+        cols = slice(c * half, (c + 1) * half)
+        plan.append([(wholes[i], i, cols) for i in range(2)])
+        plan[c] += [(halves[i], 2 + 4 * c + i, slice(0, half)) for i in range(4)]
+    plan.append([(wholes[i], 10 + i, slice(0, half)) for i in range(2)])
+    plan[2] += [(halves[i], 12 + i, slice(0, half)) for i in range(4)]
+    waited = set()
+    for c, terms in enumerate(plan):
+        acc = None
+        for lhs, n, cols in terms:
+            if n not in waited:
+                copies[n].wait()
+                waited.add(n)
+            term = jnp.dot(lhs, weights[n][:, cols], preferred_element_type=F32)
+            acc = term if acc is None else acc + term
+        total[:, c * half : (c + 1) * half] = acc
+    heads = local // HD
+    kv_heads = (total.shape[1] - local) // (2 * HD)
+    cos, sin, bias = cos_ref[...], sin_ref[...], bias_ref[...]
+
+    def turned(at):
+        x = total[:, at : at + HD]
+        return (x * cos + pltpu.roll(x, HD // 2, 1) * sin).astype(BF16)
+
+    for g in range(kv_heads):
+        key = turned(local + g * HD)
+        at = local + (kv_heads + g) * HD
+        val = total[:, at : at + HD].astype(BF16)
+        for r in range(heads // kv_heads):
+            at = (g * (heads // kv_heads) + r) * HD
+            scores = lax.dot_general(
+                turned(at), key, (((1,), (1,)), ((), ())), preferred_element_type=F32
+            ) * (1.0 / math.sqrt(HD)) + bias
+            weight = jnp.exp(scores - jnp.max(scores, axis=1, keepdims=True))
+            probs = (weight / jnp.sum(weight, axis=1, keepdims=True)).astype(BF16)
+            mixed = jnp.dot(probs, val, preferred_element_type=F32)
+            out_ref[:, at : at + HD] = mixed.astype(BF16)
+
+
+def attend_call(place, pieces, stats, gain, cos, sin, bias, weights):
+    rows, local = pieces[0].shape
+    return pl.pallas_call(
+        attend_body,
+        grid=(1,),
+        in_specs=[SMEM]
+        + [whole(v.shape) for v in (*pieces, *stats, gain, cos, sin, bias)]
+        + [pl.BlockSpec(memory_space=pl.ANY)] * len(weights),
+        out_specs=whole((rows, local)),
+        out_shape=jax.ShapeDtypeStruct((rows, local), BF16),
+        scratch_shapes=[pltpu.VMEM((rows, 4 * local), BF16), pltpu.VMEM((rows, 3 * local // 2), F32)]
+        + [pltpu.VMEM(w.shape, BF16) for w in weights]
+        + [pltpu.SemaphoreType.DMA((len(weights),))],
+        compiler_params=pltpu.CompilerParams(vmem_limit_bytes=20 << 20),
+        cost_estimate=TINY,
+        name="attend",
+    )(place, *pieces, *stats, gain, cos, sin, bias, *weights)
+
+
+def swap(value, axis, size, by):
+    return lax.ppermute(value, axis, [(i, i ^ by) for i in range(size)])
+
+
+def tie(*values):
+    return lax.optimization_barrier(values)
+
+
+def position_tables(lengths, count):
+    ends = jnp.cumsum(lengths, dtype=jnp.int32)
+    places = jnp.arange(count, dtype=jnp.int32)
+    past = (places[:, None] >= ends[None, :]).astype(jnp.int32)
+    doc_ids = jnp.sum(past, axis=1, dtype=jnp.int32)
+    starts = jnp.sum(past * lengths[None, :], axis=1, dtype=jnp.int32)
+    position = (places - starts).astype(F32)
+    half = HD // 2
+    freqs = jnp.exp(jnp.arange(half, dtype=F32) * (-2.0 * math.log(10000.0) / HD))
+    angles = position[:, None] * freqs[None, :]
+    cosine = jnp.cos(angles)
+    sine = jnp.sin(angles)
+    allowed = (doc_ids[:, None] == doc_ids[None, :]) & (places[None, :] <= places[:, None])
+    bias = jnp.where(allowed, 0.0, -jnp.inf).astype(F32)
+    return (
+        jnp.concatenate([cosine, cosine], axis=1),
+        jnp.concatenate([-sine, sine], axis=1),
+        bias,
+    )
+
+
+def on_grid(
+    resid, moe_gain, routes, gate_q, doc_lengths, w_gate, w_up, w_down, attn_gain, w_q, w_k, w_v
+):
+    tokens, local = resid.shape
+    half = local // 2
+    group = lax.axis_index("groups")
+    sect = lax.axis_index("sect")
+    hid = lax.axis_index("hid")
+    place = jnp.stack([group, hid, sect]).astype(jnp.int32)
+
+    over_hid = lambda v, by: swap(v, "hid", 4, by)
+    over_core = lambda v: swap(v, "sect", 4, 1)
+    over_chip = lambda v: swap(v, "sect", 4, 2)
+    over_group = lambda v: swap(v, "groups", 2, 1)
+
+    def half_of(w, c):
+        return lax.dynamic_slice(w, (group * half, c * half), (half, half))
+
+    here, there, here_core, there_core = ([None] * 3 for _ in range(4))
+    gate_w, up_w, down_w = (
+        pltpu.with_memory_space_constraint(w[0], pltpu.HBM) for w in (w_gate, w_up, w_down)
+    )
+
+    first, second, third = (over_hid(resid, k) for k in (1, 2, 3))
+    experts = jnp.arange(128, dtype=jnp.int32)
+    units = jnp.sum(jnp.where(routes[:, :, None] == experts, gate_q[:, :, None], 0), axis=1)
+    marked = jnp.concatenate([resid, units.astype(BF16)], axis=1)
+    far_own = over_chip(marked)
+    here[0] = over_chip(half_of(w_q, 0))
+    w_kv = jnp.concatenate([w_k, w_v], axis=1)
+    waiting = [half_of(w_q, 1), half_of(w_kv, 0)]
+    tables = position_tables(doc_lengths[0], tokens)
+    first, second, far_own, here[0], marked, w_q, w_kv, *held = tie(
+        first, second, far_own, here[0], marked, w_q, w_kv, *waiting, *tables
+    )
+    waiting, tables = held[:2], held[2:]
+    near = [marked, first, second, third]
+    near_pair = [over_core(v) for v in near]
+    far = [far_own] + [over_chip(v) for v in near[1:]]
+
+    gain = moe_gain.reshape(1, -1)
+    weights = (gate_w, up_w, down_w)
+    near_keep, near_send = expert_call(place, near + near_pair, gain, *weights, "near")
+    near_send, *far = tie(near_send, *far)
+    far[3], waiting[0] = tie(far[3], waiting[0])
+    here[1] = over_chip(waiting[0])
+    far_pair = [over_core(v) for v in far]
+    far_keep, far_send = expert_call(place, far + far_pair, gain, *weights, "far")
+    far_send, near_send, here[0], here[1] = tie(far_send, near_send, here[0], here[1])
+
+    rows_of = (2, tokens, local)
+    near_got, there[0] = over_core(near_send), over_group(here[0])
+    operands = [far_keep, over_core(far_send)]
+    summed = list(sums_call(core_body, operands, [(rows_of, BF16)] * 2, "sum_core"))
+    got = over_chip(summed[0])
+    got, near_got, there[0], here[0], here[1], summed[1] = tie(
+        got, near_got, there[0], here[0], here[1], summed[1]
+    )
+    got_rest, there[1] = over_chip(summed[1]), over_group(here[1])
+    here_core[0], there_core[0] = over_core(here[0]), over_core(there[0])
+    operands = [near_keep, near_got, got]
+    (part,) = sums_call(chip_body, operands, [(rows_of, BF16)], "sum_chip")
+    part = over_hid(part, 1)
+    part, got_rest, there[1], here_core[0], there_core[0], here[1], w_q, waiting[1] = tie(
+        part, got_rest, there[1], here_core[0], there_core[0], here[1], w_q, waiting[1]
+    )
+    here[2], q_near = over_chip(waiting[1]), over_core(w_q)
+    here_core[1], there_core[1] = over_core(here[1]), over_core(there[1])
+    operands = [near_keep, near_got, got_rest, part, resid]
+    one = (tokens, local)
+    send, own = sums_call(pair_body, operands, [(one, BF16), (one, F32)], "sum_pair")
+    send = over_hid(send, 2)
+    send, here[2], q_near, here_core[1], there_core[1], w_kv = tie(
+        send, here[2], q_near, here_core[1], there_core[1], w_kv
+    )
+    (new_local,) = sums_call(last_body, [own, send], [(one, BF16)], "sum_hid")
+
+    there[2], here_core[2], kv_near = over_group(here[2]), over_core(here[2]), over_core(w_kv)
+    rows = [new_local, over_hid(new_local, 1), over_hid(new_local, 2), None]
+    rows[1], rows[2], there[2], here_core[2], kv_near = tie(
+        rows[1], rows[2], there[2], here_core[2], kv_near
+    )
+    rows[3], there_core[2] = over_hid(rows[2], 1), over_core(there[2])
+    moved = [(here[c], there[c], here_core[c], there_core[c]) for c in range(3)]
+    proj = [w_q, q_near, *moved[0], *moved[1], w_kv, kv_near, *moved[2]]
+    stats = stats_chain([[r] for r in rows], "stats_next")
+    gain = attn_gain.reshape(1, -1)
+    context = attend_call(place, rows, stats, gain, *tables, proj)
+    return (new_local, context)
 
 
 def layer_norm(values, gain):
@@ -145,6 +575,9 @@
         P("sect", "hid"),
     )
     out_specs = (P(("groups", "sect"), "hid"), P(("groups", "sect"), "hid"))
+    plan = on_device
+    if dict(mesh.shape) == {"groups": 2, "sect": 4, "hid": 4}:
+        plan = on_grid
     return jax.shard_map(
-        on_device, mesh=mesh, in_specs=in_specs, out_specs=out_specs, check_vma=False
-    )
+        plan, mesh=mesh, in_specs=in_specs, out_specs=out_specs, check_vma=False
+    )

time: 451 us -> 151 us (0.33)
  waiting for transfers between devices: 318 us -> 73.7 us
  blocking collectives: 51.9 us -> 0 us
  matrix products: 35.8 us -> 0 us
  Pallas kernels: 0 us -> 33.2 us
  starting transfers between devices: 4.15 us -> 32.1 us
  between operations: 14.4 us -> 1.13 us
  other arithmetic: 12.8 us -> 2.67 us
  local copies, waits for them, and re-layouts: 12.6 us -> 8.06 us
    all_gather x5 -> x0, waiting for transfers between devices: 148 us -> none  [the longest x1 57.5 us: on_device(): lax.all_gather(w_q, 'sect', axis=0, tiled=True)]
    reduce_scatter x1 -> x0, waiting for transfers between devices: 143 us -> none  [on_device(): mine = lax.psum_scatter(outputs, 'hid', scatter_dimension=1, tiled=True)]
    ppermute x0 -> x38, waiting for transfers between devices: none -> 73.7 us  [swap(): return lax.ppermute(value, axis, [(i, i ^ by) for i in range(size)])]
    all_to_all x1 -> x0, blocking collectives: 51.9 us -> none  [on_device(): lax.all_to_all(outgoing, 'sect', split_axis=0, concat_axis=0, tiled=True)]
    dot_general x7 -> x0, matrix products: 35.4 us -> none  [the longest x1 19.1 us: on_device(): outputs = jnp.dot(hidden, down_w, preferred_element_type=jnp.float32)]
    pallas_call x0 -> x11, Pallas kernels: none -> 33.2 us  [the longest x2 22.9 us: expert_call(): pl.pallas_call(expert_body, grid=(1,), in_specs=[SMEM] + held + [whole(ga...]
    ppermute x0 -> x38, starting transfers between devices: none -> 32.1 us  [swap(): return lax.ppermute(value, axis, [(i, i ^ by) for i in range(size)])]
    all_to_all x1 -> x0, waiting for transfers between devices: 25.3 us -> none  [on_device(): lax.all_to_all(mine.reshape(sections, capacity, local_width), 'sect', spl...]
  transfers between devices with their start and end apart: 7 -> 38, of which waited for: 7 -> 16; matrix products, arithmetic and copies ran while one was open for 4% -> 4% of each run, Pallas kernels for 0% -> 17%
where the time goes in v2:
time: 151 us
  waiting for transfers between devices  73.7 us (49%)
  Pallas kernels  33.2 us (22%)
  starting transfers between devices  32.1 us (21%)
  local copies, waits for them, and re-layouts  8.06 us (5%)
  other arithmetic  2.67 us (2%)
    ppermute x38, waiting for transfers between devices, swap(): return lax.ppermute(value, axis, [(i, i ^ by) for i in range(size)])  73.7 us
    ppermute x38, starting transfers between devices, swap(): return lax.ppermute(value, axis, [(i, i ^ by) for i in range(size)])  32.1 us
    pallas_call x2, Pallas kernels, expert_call(): pl.pallas_call(expert_body, grid=(1,), in_specs=[SMEM] + held + [whole(ga...  22.9 us
    pallas_call x1, Pallas kernels, attend_call(): pl.pallas_call(attend_body, grid=(1,), in_specs=[SMEM] + [whole(v.shape)...  8 us
    unnamed x35, local copies, waits for them, and re-layouts  4.06 us
  transfers between devices with their start and end apart: 38, of which 16 were waited for; matrix products, arithmetic and copies ran while one was open for 4% of the time, Pallas kernels for 17%

profile of v2, /device:TPU:0, one launch (start us, length us, event | category | flops | bytes accessed | tf_op | source)
XLA Modules:
  0.0 151.0 jit_solution(6928809185457284200)
XLA Ops:
  0.7 4.1 %collective-permute-start.1 = (bf16[128,1024]{1,0:T(8,128)(2,1)}, bf16[128,1024]{1,0:T(8,128)(2,1)}, u32[]{:S(2)}, u32[]{:S(2)}) collective-permute-start(bf16[128,1024]{1,0:T(8,128)(2,1)} %resid_ref.1), channel_id=1, source_target_pairs={{0,2},{1,3},{2,0},{3,1},{4,6},{5,7},{6,4},{7,5},{8,10},{9,11},{10,... | collective-permute-start | bytes 786440 | tf_op jit(solution)/shard_map/ppermute | solution.py:324
  4.8 1.6 %collective-permute-start = (bf16[128,1024]{1,0:T(8,128)(2,1)}, bf16[128,1024]{1,0:T(8,128)(2,1)}, u32[]{:S(2)}, u32[]{:S(2)}) collective-permute-start(bf16[128,1024]{1,0:T(8,128)(2,1)} %resid_ref.1), channel_id=1, source_target_pairs={{0,1},{1,0},{2,3},{3,2},{4,5},{5,4},{6,7},{7,6},{8,9},{9,8},{10,11... | collective-permute-start | bytes 786440 | tf_op jit(solution)/shard_map/ppermute | solution.py:324
  8.2 1.8 %collective-permute-start.2 = (bf16[128,1152]{1,0:T(8,128)(2,1)S(1)}, bf16[128,1152]{1,0:T(8,128)(2,1)S(1)}, u32[]{:S(2)}, u32[]{:S(2)}) collective-permute-start(bf16[128,1152]{1,0:T(8,128)(2,1)S(1)} %pad_maximum_fusion.refs_0_.refs_12_), channel_id=1, source_target_pairs={{0,8},{4,12},{8,0},{12,4},{1,9},{5,13},{9,1},{13,5},{2,10},{6,14},... | collective-permute-start | bytes 884744 | tf_op jit(solution)/shard_map/ppermute | solution.py:324
  9.9 2.1 %constant_dynamic-slice_fusion.2 = (bf16[512,512]{1,0:T(8,128)(2,1)S(1)}, bf16[512,512]{1,0:T(8,128)(2,1)}) fusion(bf16[1024,1024]{1,0:T(8,128)(2,1)} %refs_10_, s32[]{:T(128)S(6)} %select_n.14), kind=kLoop, calls=%fused_computation.21 | loop fusion | bytes 2097156 | tf_op jit(solution)/shard_map/dynamic_slice | solution.py:368
  15.1 8.7 %collective-permute-done.4.refs_3_ = bf16[128,1024]{1,0:T(8,128)(2,1)} collective-permute-done((bf16[128,1024]{1,0:T(8,128)(2,1)}, bf16[128,1024]{1,0:T(8,128)(2,1)}, u32[]{:S(2)}, u32[]{:S(2)}) %collective-permute-start.4) | collective-permute-done | bytes 262176 | tf_op jit(solution)/shard_map/ppermute | solution.py:324
  23.9 3.8 %collective-permute-done.3.refs_12_ = bf16[512,512]{1,0:T(8,128)(2,1)S(1)} collective-permute-done((bf16[512,512]{1,0:T(8,128)(2,1)}, bf16[512,512]{1,0:T(8,128)(2,1)S(1)}, u32[]{:S(2)}, u32[]{:S(2)}) %collective-permute-start.3) | collective-permute-done | bytes 524320 | tf_op jit(solution)/shard_map/ppermute | solution.py:324
  30.2 1.5 collective-permute-start.10
  32.5 11.4 %near.1 = (f32[4,128,1024]{2,1,0:T(8,128)S(1)}, bf16[4,128,1024]{2,1,0:T(8,128)(2,1)S(1)}) custom-call(s32[3]{0:T(128)S(1)} %pad_add_fusion.place_ref, bf16[128,1152]{1,0:T(8,128)(2,1)} %copy-done.4, bf16[128,1024]{1,0:T(8,128)(2,1)} %collective-permute-done.refs_1_, bf16[128,1024]{1,0:T(8,128)(2,1)} %collective-permute-done.1.refs_2_, ...), custom_call_target="tpu_custom_call" | custom-call | flops 1 | bytes 1 | tf_op jit(solution)/shard_map/near/pallas_call | solution.py:178
  44.0 4.5 %collective-permute-done.10.refs_2_ = bf16[128,1024]{1,0:T(8,128)(2,1)} collective-permute-done((bf16[128,1024]{1,0:T(8,128)(2,1)}, bf16[128,1024]{1,0:T(8,128)(2,1)}, u32[]{:S(2)}, u32[]{:S(2)}) %collective-permute-start.10) | collective-permute-done | bytes 262176 | tf_op jit(solution)/shard_map/ppermute | solution.py:324
  54.3 11.4 %far.1 = (f32[4,128,1024]{2,1,0:T(8,128)S(1)}, bf16[4,128,1024]{2,1,0:T(8,128)(2,1)S(1)}) custom-call(s32[3]{0:T(128)S(1)} %pad_add_fusion.place_ref, bf16[128,1152]{1,0:T(8,128)(2,1)} %copy-done.5, bf16[128,1024]{1,0:T(8,128)(2,1)} %collective-permute-done.9.refs_1_, bf16[128,1024]{1,0:T(8,128)(2,1)} %collective-permute-done.10.refs_2_, ...), custom_call_target="tpu_custom_call" | custom-call | flops 1 | bytes 1 | tf_op jit(solution)/shard_map/far/pallas_call | solution.py:178
  66.3 1.5 %collective-permute-start.20 = (bf16[512,512]{1,0:T(8,128)(2,1)S(1)}, bf16[512,512]{1,0:T(8,128)(2,1)S(1)}, u32[]{:S(2)}, u32[]{:S(2)}) collective-permute-start(bf16[512,512]{1,0:T(8,128)(2,1)S(1)} %collective-permute-done.3.refs_12_), channel_id=1, source_target_pairs={{0,16},{16,0},{1,17},{17,1},{2,18},{18,2},{3,19},{19,3},{4,20},{20... | collective-permute-start | bytes 1572872 | tf_op jit(solution)/shard_map/ppermute | solution.py:324
  69.3 11.0 %collective-permute-done.20.refs_13_ = bf16[512,512]{1,0:T(8,128)(2,1)S(1)} collective-permute-done((bf16[512,512]{1,0:T(8,128)(2,1)S(1)}, bf16[512,512]{1,0:T(8,128)(2,1)S(1)}, u32[]{:S(2)}, u32[]{:S(2)}) %collective-permute-start.20) | collective-permute-done | bytes 524320 | tf_op jit(solution)/shard_map/ppermute | solution.py:324
  80.3 2.4 %collective-permute-done.18.far_ref = bf16[2,128,1024]{2,1,0:T(8,128)(2,1)S(1)} collective-permute-done((bf16[2,128,1024]{2,1,0:T(8,128)(2,1)S(1)}, bf16[2,128,1024]{2,1,0:T(8,128)(2,1)S(1)}, u32[]{:S(2)}, u32[]{:S(2)}) %collective-permute-start.18) | collective-permute-done | bytes 524320 | tf_op jit(solution)/shard_map/ppermute | solution.py:324
  82.9 1.5 %collective-permute-start.21 = (bf16[2,128,1024]{2,1,0:T(8,128)(2,1)S(1)}, bf16[2,128,1024]{2,1,0:T(8,128)(2,1)S(1)}, u32[]{:S(2)}, u32[]{:S(2)}) collective-permute-start(bf16[2,128,1024]{2,1,0:T(8,128)(2,1)S(1)} %sum_chip.1), channel_id=1, source_target_pairs={{0,1},{1,0},{2,3},{3,2},{4,5},{5,4},{6,7},{7,6},{8,9},{9,8},{10,11... | collective-permute-start | bytes 1572872 | tf_op jit(solution)/shard_map/ppermute | solution.py:324
  85.0 1.5 %collective-permute-start.23 = (bf16[512,512]{1,0:T(8,128)(2,1)S(1)}, bf16[512,512]{1,0:T(8,128)(2,1)S(1)}, u32[]{:S(2)}, u32[]{:S(2)}) collective-permute-start(bf16[512,512]{1,0:T(8,128)(2,1)S(1)} %collective-permute-done.16.refs_16_), channel_id=1, source_target_pairs={{0,16},{16,0},{1,17},{17,1},{2,18},{18,2},{3,19},{19,3},{4,20},{20... | collective-permute-start | bytes 1572872 | tf_op jit(solution)/shard_map/ppermute | solution.py:324
  87.0 9.1 %collective-permute-done.21.hid_ref = bf16[2,128,1024]{2,1,0:T(8,128)(2,1)S(1)} collective-permute-done((bf16[2,128,1024]{2,1,0:T(8,128)(2,1)S(1)}, bf16[2,128,1024]{2,1,0:T(8,128)(2,1)S(1)}, u32[]{:S(2)}, u32[]{:S(2)}) %collective-permute-start.21) | collective-permute-done | bytes 524320 | tf_op jit(solution)/shard_map/ppermute | solution.py:324
  97.7 1.6 %collective-permute-start.27 = (bf16[512,512]{1,0:T(8,128)(2,1)S(1)}, bf16[512,512]{1,0:T(8,128)(2,1)S(1)}, u32[]{:S(2)}, u32[]{:S(2)}) collective-permute-start(bf16[512,512]{1,0:T(8,128)(2,1)S(1)} %copy-done.9), channel_id=1, source_target_pairs={{0,8},{4,12},{8,0},{12,4},{1,9},{5,13},{9,1},{13,5},{2,10},{6,14},... | collective-permute-start | bytes 1572872 | tf_op jit(solution)/shard_map/ppermute | solution.py:324
  100.0 2.7 %collective-permute-start.26 = (bf16[128,1024]{1,0:T(8,128)(2,1)S(1)}, bf16[128,1024]{1,0:T(8,128)(2,1)S(1)}, u32[]{:S(2)}, u32[]{:S(2)}) collective-permute-start(bf16[128,1024]{1,0:T(8,128)(2,1)S(1)} %get-tuple-element.100), channel_id=1, source_target_pairs={{0,2},{1,3},{2,0},{3,1},{4,6},{5,7},{6,4},{7,5},{8,10},{9,11},{10,... | collective-permute-start | bytes 786440 | tf_op jit(solution)/shard_map/ppermute | solution.py:324
  102.7 12.3 %collective-permute-done.26.got_ref = bf16[128,1024]{1,0:T(8,128)(2,1)S(1)} collective-permute-done((bf16[128,1024]{1,0:T(8,128)(2,1)S(1)}, bf16[128,1024]{1,0:T(8,128)(2,1)S(1)}, u32[]{:S(2)}, u32[]{:S(2)}) %collective-permute-start.26) | collective-permute-done | bytes 262176 | tf_op jit(solution)/shard_map/ppermute | solution.py:324
  115.6 1.5 %collective-permute-start.33 = (bf16[512,512]{1,0:T(8,128)(2,1)S(1)}, bf16[512,512]{1,0:T(8,128)(2,1)S(1)}, u32[]{:S(2)}, u32[]{:S(2)}) collective-permute-start(bf16[512,512]{1,0:T(8,128)(2,1)S(1)} %collective-permute-done.27.refs_22_), channel_id=1, source_target_pairs={{0,16},{16,0},{1,17},{17,1},{2,18},{18,2},{3,19},{19,3},{4,20},{20... | collective-permute-start | bytes 1572872 | tf_op jit(solution)/shard_map/ppermute | solution.py:324
  117.8 3.9 %collective-permute-start.31 = (bf16[128,1024]{1,0:T(8,128)(2,1)}, bf16[128,1024]{1,0:T(8,128)(2,1)S(1)}, u32[]{:S(2)}, u32[]{:S(2)}) collective-permute-start(bf16[128,1024]{1,0:T(8,128)(2,1)} %sum_hid.1.refs_0_), channel_id=1, source_target_pairs={{0,1},{1,0},{2,3},{3,2},{4,5},{5,4},{6,7},{7,6},{8,9},{9,8},{10,11... | collective-permute-start | bytes 786440 | tf_op jit(solution)/shard_map/ppermute | solution.py:324
  121.8 10.9 %collective-permute-done.32.refs_0_.refs_2_ = bf16[128,1024]{1,0:T(8,128)(2,1)S(1)} collective-permute-done((bf16[128,1024]{1,0:T(8,128)(2,1)}, bf16[128,1024]{1,0:T(8,128)(2,1)S(1)}, u32[]{:S(2)}, u32[]{:S(2)}) %collective-permute-start.32) | collective-permute-done | bytes 262176 | tf_op jit(solution)/shard_map/ppermute | solution.py:324
  134.6 7.0 %collective-permute-done.36.refs_0_.refs_3_ = bf16[128,1024]{1,0:T(8,128)(2,1)S(1)} collective-permute-done((bf16[128,1024]{1,0:T(8,128)(2,1)S(1)}, bf16[128,1024]{1,0:T(8,128)(2,1)S(1)}, u32[]{:S(2)}, u32[]{:S(2)}) %collective-permute-start.36) | collective-permute-done | bytes 262176 | tf_op jit(solution)/shard_map/ppermute | solution.py:324
  142.8 8.0 %attend.1 = bf16[128,1024]{1,0:T(8,128)(2,1)} custom-call(s32[3]{0:T(128)S(1)} %pad_add_fusion.place_ref, bf16[128,1024]{1,0:T(8,128)(2,1)S(1)} %copy-done.2, bf16[128,1024]{1,0:T(8,128)(2,1)S(1)} %collective-permute-done.31.refs_0_.refs_1_, bf16[128,1024]{1,0:T(8,128)(2,1)S(1)} %collective-permute-done.32.refs_0_.refs_2_, ...), custom_call_target="tpu_custom_call" | custom-call | flops 1 | bytes 1 | tf_op jit(solution)/shard_map/attend/pallas_call | solution.py:306
  (114 shorter events, 24.0 us)
Async XLA Ops:
  0.7 23.2 %collective-permute-start.1 = (bf16[128,1024]{1,0:T(8,128)(2,1)}, bf16[128,1024]{1,0:T(8,128)(2,1)}, u32[]{:S(2)}, u32[]{:S(2)}) collective-permute-start(bf16[128,1024]{1,0:T(8,128)(2,1)} %resid_ref.1), channel_id=1, source_target_pairs={{0,2},{1,3},{2,0},{3,1},{4,6},{5,7},{6,4},{7,5},{8,10},{9,11},{10,... | collective-permute-start | bytes 786440 | tf_op jit(solution)/shard_map/ppermute | solution.py:324
  4.8 19.1 %collective-permute-start = (bf16[128,1024]{1,0:T(8,128)(2,1)}, bf16[128,1024]{1,0:T(8,128)(2,1)}, u32[]{:S(2)}, u32[]{:S(2)}) collective-permute-start(bf16[128,1024]{1,0:T(8,128)(2,1)} %resid_ref.1), channel_id=1, source_target_pairs={{0,1},{1,0},{2,3},{3,2},{4,5},{5,4},{6,7},{7,6},{8,9},{9,8},{10,11... | collective-permute-start | bytes 786440 | tf_op jit(solution)/shard_map/ppermute | solution.py:324
  6.3 17.5 %collective-permute-start.4 = (bf16[128,1024]{1,0:T(8,128)(2,1)}, bf16[128,1024]{1,0:T(8,128)(2,1)}, u32[]{:S(2)}, u32[]{:S(2)}) collective-permute-start(bf16[128,1024]{1,0:T(8,128)(2,1)} %resid_ref.1), channel_id=1, source_target_pairs={{0,3},{1,2},{2,1},{3,0},{4,7},{5,6},{6,5},{7,4},{8,11},{9,10},{10,... | collective-permute-start | bytes 786440 | tf_op jit(solution)/shard_map/ppermute | solution.py:324
  8.2 15.7 %collective-permute-start.2 = (bf16[128,1152]{1,0:T(8,128)(2,1)S(1)}, bf16[128,1152]{1,0:T(8,128)(2,1)S(1)}, u32[]{:S(2)}, u32[]{:S(2)}) collective-permute-start(bf16[128,1152]{1,0:T(8,128)(2,1)S(1)} %pad_maximum_fusion.refs_0_.refs_12_), channel_id=1, source_target_pairs={{0,8},{4,12},{8,0},{12,4},{1,9},{5,13},{9,1},{13,5},{2,10},{6,14},... | collective-permute-start | bytes 884744 | tf_op jit(solution)/shard_map/ppermute | solution.py:324
  12.0 15.7 %collective-permute-start.3 = (bf16[512,512]{1,0:T(8,128)(2,1)}, bf16[512,512]{1,0:T(8,128)(2,1)S(1)}, u32[]{:S(2)}, u32[]{:S(2)}) collective-permute-start(bf16[512,512]{1,0:T(8,128)(2,1)} %get-tuple-element.133), channel_id=1, source_target_pairs={{0,8},{4,12},{8,0},{12,4},{1,9},{5,13},{9,1},{13,5},{2,10},{6,14},... | collective-permute-start | bytes 1572872 | tf_op jit(solution)/shard_map/ppermute | solution.py:324
  28.2 15.8 %collective-permute-start.11 = (bf16[128,1024]{1,0:T(8,128)(2,1)}, bf16[128,1024]{1,0:T(8,128)(2,1)S(1)}, u32[]{:S(2)}, u32[]{:S(2)}) collective-permute-start(bf16[128,1024]{1,0:T(8,128)(2,1)} %collective-permute-done.4.refs_3_), channel_id=1, source_target_pairs={{0,8},{4,12},{8,0},{12,4},{1,9},{5,13},{9,1},{13,5},{2,10},{6,14},... | collective-permute-start | bytes 786440 | tf_op jit(solution)/shard_map/ppermute | solution.py:324
  29.7 14.3 %collective-permute-start.9 = (bf16[128,1024]{1,0:T(8,128)(2,1)}, bf16[128,1024]{1,0:T(8,128)(2,1)}, u32[]{:S(2)}, u32[]{:S(2)}) collective-permute-start(bf16[128,1024]{1,0:T(8,128)(2,1)} %collective-permute-done.refs_1_), channel_id=1, source_target_pairs={{0,8},{4,12},{8,0},{12,4},{1,9},{5,13},{9,1},{13,5},{2,10},{6,14},... | collective-permute-start | bytes 786440 | tf_op jit(solution)/shard_map/ppermute | solution.py:324
  30.2 18.2 %collective-permute-start.10 = (bf16[128,1024]{1,0:T(8,128)(2,1)}, bf16[128,1024]{1,0:T(8,128)(2,1)}, u32[]{:S(2)}, u32[]{:S(2)}) collective-permute-start(bf16[128,1024]{1,0:T(8,128)(2,1)} %collective-permute-done.1.refs_2_), channel_id=1, source_target_pairs={{0,8},{4,12},{8,0},{12,4},{1,9},{5,13},{9,1},{13,5},{2,10},{6,14},... | collective-permute-start | bytes 786440 | tf_op jit(solution)/shard_map/ppermute | solution.py:324
  48.5 17.3 %collective-permute-start.16 = (bf16[512,512]{1,0:T(8,128)(2,1)S(1)}, bf16[512,512]{1,0:T(8,128)(2,1)S(1)}, u32[]{:S(2)}, u32[]{:S(2)}) collective-permute-start(bf16[512,512]{1,0:T(8,128)(2,1)S(1)} %get-tuple-element.82), channel_id=1, source_target_pairs={{0,8},{4,12},{8,0},{12,4},{1,9},{5,13},{9,1},{13,5},{2,10},{6,14},... | collective-permute-start | bytes 1572872 | tf_op jit(solution)/shard_map/ppermute | solution.py:324
  65.9 14.3 %collective-permute-start.19 = (bf16[4,128,1024]{2,1,0:T(8,128)(2,1)S(1)}, bf16[4,128,1024]{2,1,0:T(8,128)(2,1)S(1)}, u32[]{:S(2)}, u32[]{:S(2)}) collective-permute-start(bf16[4,128,1024]{2,1,0:T(8,128)(2,1)S(1)} %get-tuple-element.85), channel_id=1, source_target_pairs={{0,4},{4,0},{8,12},{12,8},{1,5},{5,1},{9,13},{13,9},{2,6},{6,2},{1... | collective-permute-start | bytes 3145736 | tf_op jit(solution)/shard_map/ppermute | solution.py:324
  66.3 14.0 %collective-permute-start.20 = (bf16[512,512]{1,0:T(8,128)(2,1)S(1)}, bf16[512,512]{1,0:T(8,128)(2,1)S(1)}, u32[]{:S(2)}, u32[]{:S(2)}) collective-permute-start(bf16[512,512]{1,0:T(8,128)(2,1)S(1)} %collective-permute-done.3.refs_12_), channel_id=1, source_target_pairs={{0,16},{16,0},{1,17},{17,1},{2,18},{18,2},{3,19},{19,3},{4,20},{20... | collective-permute-start | bytes 1572872 | tf_op jit(solution)/shard_map/ppermute | solution.py:324
  68.7 14.0 %collective-permute-start.18 = (bf16[2,128,1024]{2,1,0:T(8,128)(2,1)S(1)}, bf16[2,128,1024]{2,1,0:T(8,128)(2,1)S(1)}, u32[]{:S(2)}, u32[]{:S(2)}) collective-permute-start(bf16[2,128,1024]{2,1,0:T(8,128)(2,1)S(1)} %get-tuple-element.84), channel_id=1, source_target_pairs={{0,8},{4,12},{8,0},{12,4},{1,9},{5,13},{9,1},{13,5},{2,10},{6,14},... | collective-permute-start | bytes 1572872 | tf_op jit(solution)/shard_map/ppermute | solution.py:324
  82.9 13.2 %collective-permute-start.21 = (bf16[2,128,1024]{2,1,0:T(8,128)(2,1)S(1)}, bf16[2,128,1024]{2,1,0:T(8,128)(2,1)S(1)}, u32[]{:S(2)}, u32[]{:S(2)}) collective-permute-start(bf16[2,128,1024]{2,1,0:T(8,128)(2,1)S(1)} %sum_chip.1), channel_id=1, source_target_pairs={{0,1},{1,0},{2,3},{3,2},{4,5},{5,4},{6,7},{7,6},{8,9},{9,8},{10,11... | collective-permute-start | bytes 1572872 | tf_op jit(solution)/shard_map/ppermute | solution.py:324
  84.4 12.9 %collective-permute-start.22 = (bf16[2,128,1024]{2,1,0:T(8,128)(2,1)S(1)}, bf16[2,128,1024]{2,1,0:T(8,128)(2,1)S(1)}, u32[]{:S(2)}, u32[]{:S(2)}) collective-permute-start(bf16[2,128,1024]{2,1,0:T(8,128)(2,1)S(1)} %get-tuple-element.91), channel_id=1, source_target_pairs={{0,8},{4,12},{8,0},{12,4},{1,9},{5,13},{9,1},{13,5},{2,10},{6,14},... | collective-permute-start | bytes 1572872 | tf_op jit(solution)/shard_map/ppermute | solution.py:324
  97.6 17.4 %collective-permute-start.28 = (bf16[1024,1024]{1,0:T(8,128)(2,1)S(1)}, bf16[1024,1024]{1,0:T(8,128)(2,1)S(1)}, u32[]{:S(2)}, u32[]{:S(2)}) collective-permute-start(bf16[1024,1024]{1,0:T(8,128)(2,1)S(1)} %copy-done), channel_id=1, source_target_pairs={{0,4},{4,0},{8,12},{12,8},{1,5},{5,1},{9,13},{13,9},{2,6},{6,2},{1... | collective-permute-start | bytes 6291464 | tf_op jit(solution)/shard_map/ppermute | solution.py:324
  97.7 17.3 %collective-permute-start.27 = (bf16[512,512]{1,0:T(8,128)(2,1)S(1)}, bf16[512,512]{1,0:T(8,128)(2,1)S(1)}, u32[]{:S(2)}, u32[]{:S(2)}) collective-permute-start(bf16[512,512]{1,0:T(8,128)(2,1)S(1)} %copy-done.9), channel_id=1, source_target_pairs={{0,8},{4,12},{8,0},{12,4},{1,9},{5,13},{9,1},{13,5},{2,10},{6,14},... | collective-permute-start | bytes 1572872 | tf_op jit(solution)/shard_map/ppermute | solution.py:324
  99.2 15.8 %collective-permute-start.29 = (bf16[512,512]{1,0:T(8,128)(2,1)S(1)}, bf16[512,512]{1,0:T(8,128)(2,1)S(1)}, u32[]{:S(2)}, u32[]{:S(2)}) collective-permute-start(bf16[512,512]{1,0:T(8,128)(2,1)S(1)} %collective-permute-done.16.refs_16_), channel_id=1, source_target_pairs={{0,4},{4,0},{8,12},{12,8},{1,5},{5,1},{9,13},{13,9},{2,6},{6,2},{1... | collective-permute-start | bytes 1572872 | tf_op jit(solution)/shard_map/ppermute | solution.py:324
  99.4 15.6 %collective-permute-start.30 = (bf16[512,512]{1,0:T(8,128)(2,1)S(1)}, bf16[512,512]{1,0:T(8,128)(2,1)S(1)}, u32[]{:S(2)}, u32[]{:S(2)}) collective-permute-start(bf16[512,512]{1,0:T(8,128)(2,1)S(1)} %collective-permute-done.23.refs_17_), channel_id=1, source_target_pairs={{0,4},{4,0},{8,12},{12,8},{1,5},{5,1},{9,13},{13,9},{2,6},{6,2},{1... | collective-permute-start | bytes 1572872 | tf_op jit(solution)/shard_map/ppermute | solution.py:324
  100.0 15.0 %collective-permute-start.26 = (bf16[128,1024]{1,0:T(8,128)(2,1)S(1)}, bf16[128,1024]{1,0:T(8,128)(2,1)S(1)}, u32[]{:S(2)}, u32[]{:S(2)}) collective-permute-start(bf16[128,1024]{1,0:T(8,128)(2,1)S(1)} %get-tuple-element.100), channel_id=1, source_target_pairs={{0,2},{1,3},{2,0},{3,1},{4,6},{5,7},{6,4},{7,5},{8,10},{9,11},{10,... | collective-permute-start | bytes 786440 | tf_op jit(solution)/shard_map/ppermute | solution.py:324
  115.0 17.8 %collective-permute-start.35 = (bf16[1024,512]{1,0:T(8,128)(2,1)S(1)}, bf16[1024,512]{1,0:T(8,128)(2,1)S(1)}, u32[]{:S(2)}, u32[]{:S(2)}) collective-permute-start(bf16[1024,512]{1,0:T(8,128)(2,1)S(1)} %constant_dynamic-update-slice_fusion.refs_20_), channel_id=1, source_target_pairs={{0,4},{4,0},{8,12},{12,8},{1,5},{5,1},{9,13},{13,9},{2,6},{6,2},{1... | collective-permute-start | bytes 3145736 | tf_op jit(solution)/shard_map/ppermute | solution.py:324
  115.1 17.7 %collective-permute-start.34 = (bf16[512,512]{1,0:T(8,128)(2,1)S(1)}, bf16[512,512]{1,0:T(8,128)(2,1)S(1)}, u32[]{:S(2)}, u32[]{:S(2)}) collective-permute-start(bf16[512,512]{1,0:T(8,128)(2,1)S(1)} %collective-permute-done.27.refs_22_), channel_id=1, source_target_pairs={{0,4},{4,0},{8,12},{12,8},{1,5},{5,1},{9,13},{13,9},{2,6},{6,2},{1... | collective-permute-start | bytes 1572872 | tf_op jit(solution)/shard_map/ppermute | solution.py:324
  115.6 17.2 %collective-permute-start.33 = (bf16[512,512]{1,0:T(8,128)(2,1)S(1)}, bf16[512,512]{1,0:T(8,128)(2,1)S(1)}, u32[]{:S(2)}, u32[]{:S(2)}) collective-permute-start(bf16[512,512]{1,0:T(8,128)(2,1)S(1)} %collective-permute-done.27.refs_22_), channel_id=1, source_target_pairs={{0,16},{16,0},{1,17},{17,1},{2,18},{18,2},{3,19},{19,3},{4,20},{20... | collective-permute-start | bytes 1572872 | tf_op jit(solution)/shard_map/ppermute | solution.py:324
  117.8 14.8 %collective-permute-start.32 = (bf16[128,1024]{1,0:T(8,128)(2,1)}, bf16[128,1024]{1,0:T(8,128)(2,1)S(1)}, u32[]{:S(2)}, u32[]{:S(2)}) collective-permute-start(bf16[128,1024]{1,0:T(8,128)(2,1)} %sum_hid.1.refs_0_), channel_id=1, source_target_pairs={{0,2},{1,3},{2,0},{3,1},{4,6},{5,7},{6,4},{7,5},{8,10},{9,11},{10,... | collective-permute-start | bytes 786440 | tf_op jit(solution)/shard_map/ppermute | solution.py:324
  117.8 14.9 %collective-permute-start.31 = (bf16[128,1024]{1,0:T(8,128)(2,1)}, bf16[128,1024]{1,0:T(8,128)(2,1)S(1)}, u32[]{:S(2)}, u32[]{:S(2)}) collective-permute-start(bf16[128,1024]{1,0:T(8,128)(2,1)} %sum_hid.1.refs_0_), channel_id=1, source_target_pairs={{0,1},{1,0},{2,3},{3,2},{4,5},{5,4},{6,7},{7,6},{8,9},{9,8},{10,11... | collective-permute-start | bytes 786440 | tf_op jit(solution)/shard_map/ppermute | solution.py:324
  (31 other events, 281.1 us)

commit v3 on v2

--- a/solution.py
+++ b/solution.py
@@ -199,10 +199,18 @@
 
 
 def sums_call(body, operands, outs, name):
+    specs = []
+    for i, v in enumerate(operands):
+        if isinstance(v, tuple):
+            operands[i], n = v
+            half = (v[0].shape[0] // 2,) + v[0].shape[1:]
+            specs.append(pl.BlockSpec(half, lambda *_, n=n: (n, 0, 0)))
+        else:
+            specs.append(whole(v.shape))
     return pl.pallas_call(
         body,
         grid=(1,),
-        in_specs=[whole(v.shape) for v in operands],
+        in_specs=specs,
         out_specs=[whole(shape) for shape, _ in outs],
         out_shape=[jax.ShapeDtypeStruct(*o) for o in outs],
         compiler_params=pltpu.CompilerParams(vmem_limit_bytes=LIMIT << 20),
@@ -239,10 +247,10 @@
 def attend_body(place_ref, *refs):
     pieces = refs[:4]
     mean_ref, spread_ref, gain_ref, cos_ref, sin_ref, bias_ref = refs[4:10]
-    sources = refs[10:26]
-    out_ref, normed, total = refs[26:29]
-    weights = refs[29:45]
-    sems = refs[45]
+    sources = refs[10:24]
+    out_ref, normed, total = refs[24:27]
+    weights = refs[27:41]
+    sems = refs[41]
     rows, local = pieces[0].shape
     half = local // 2
     group, hid, sect = place_ref[0], place_ref[1], place_ref[2]
@@ -266,8 +274,7 @@
         cols = slice(c * half, (c + 1) * half)
         plan.append([(wholes[i], i, cols) for i in range(2)])
         plan[c] += [(halves[i], 2 + 4 * c + i, slice(0, half)) for i in range(4)]
-    plan.append([(wholes[i], 10 + i, slice(0, half)) for i in range(2)])
-    plan[2] += [(halves[i], 12 + i, slice(0, half)) for i in range(4)]
+    plan.append([(wholes[i], 10 + i, slice(0, half)) for i in range(4)])
     waited = set()
     for c, terms in enumerate(plan):
         acc = None
@@ -367,35 +374,39 @@
     def half_of(w, c):
         return lax.dynamic_slice(w, (group * half, c * half), (half, half))
 
-    here, there, here_core, there_core = ([None] * 3 for _ in range(4))
+    here, there, here_core, there_core = ([None] * 2 for _ in range(4))
     gate_w, up_w, down_w = (
         pltpu.with_memory_space_constraint(w[0], pltpu.HBM) for w in (w_gate, w_up, w_down)
     )
 
-    first, second, third = (over_hid(resid, k) for k in (1, 2, 3))
+    first, second = over_hid(resid, 1), over_hid(resid, 2)
     experts = jnp.arange(128, dtype=jnp.int32)
     units = jnp.sum(jnp.where(routes[:, :, None] == experts, gate_q[:, :, None], 0), axis=1)
     marked = jnp.concatenate([resid, units.astype(BF16)], axis=1)
     far_own = over_chip(marked)
     here[0] = over_chip(half_of(w_q, 0))
     w_kv = jnp.concatenate([w_k, w_v], axis=1)
-    waiting = [half_of(w_q, 1), half_of(w_kv, 0)]
+    waiting = [half_of(w_q, 1)]
     tables = position_tables(doc_lengths[0], tokens)
-    first, second, far_own, here[0], marked, w_q, w_kv, *held = tie(
-        first, second, far_own, here[0], marked, w_q, w_kv, *waiting, *tables
-    )
-    waiting, tables = held[:2], held[2:]
+    first, second, far_own, marked, w_q, w_kv, *held = tie(
+        first, second, far_own, marked, w_q, w_kv, *waiting, *tables
+    )
+    waiting, tables = held[:1], held[1:]
+    third = over_hid(second, 1)
+    far = [far_own, over_chip(first), over_chip(second), None]
+    near_pair = [over_core(marked), over_core(first), over_core(second), None]
+    third, far[1], here[0] = tie(third, far[1], here[0])
+    far[3], near_pair[3] = over_chip(third), over_core(third)
     near = [marked, first, second, third]
-    near_pair = [over_core(v) for v in near]
-    far = [far_own] + [over_chip(v) for v in near[1:]]
+    far_pair = [over_core(far[0]), over_core(far[1]), None, None]
 
     gain = moe_gain.reshape(1, -1)
     weights = (gate_w, up_w, down_w)
     near_keep, near_send = expert_call(place, near + near_pair, gain, *weights, "near")
-    near_send, *far = tie(near_send, *far)
+    near_send, far_pair[0], far_pair[1], *far = tie(near_send, far_pair[0], far_pair[1], *far)
+    far_pair[2:] = [over_core(v) for v in far[2:]]
     far[3], waiting[0] = tie(far[3], waiting[0])
     here[1] = over_chip(waiting[0])
-    far_pair = [over_core(v) for v in far]
     far_keep, far_send = expert_call(place, far + far_pair, gain, *weights, "far")
     far_send, near_send, here[0], here[1] = tie(far_send, near_send, here[0], here[1])
 
@@ -412,28 +423,26 @@
     operands = [near_keep, near_got, got]
     (part,) = sums_call(chip_body, operands, [(rows_of, BF16)], "sum_chip")
     part = over_hid(part, 1)
-    part, got_rest, there[1], here_core[0], there_core[0], here[1], w_q, waiting[1] = tie(
-        part, got_rest, there[1], here_core[0], there_core[0], here[1], w_q, waiting[1]
-    )
-    here[2], q_near = over_chip(waiting[1]), over_core(w_q)
+    part, got_rest, there[1], here_core[0], there_core[0], here[1], w_q, w_kv = tie(
+        part, got_rest, there[1], here_core[0], there_core[0], here[1], w_q, w_kv
+    )
+    kv_far, q_near = over_chip(w_kv), over_core(w_q)
     here_core[1], there_core[1] = over_core(here[1]), over_core(there[1])
     operands = [near_keep, near_got, got_rest, part, resid]
     one = (tokens, local)
     send, own = sums_call(pair_body, operands, [(one, BF16), (one, F32)], "sum_pair")
     send = over_hid(send, 2)
-    send, here[2], q_near, here_core[1], there_core[1], w_kv = tie(
-        send, here[2], q_near, here_core[1], there_core[1], w_kv
+    send, q_near, here_core[1], there_core[1], w_kv = tie(
+        send, q_near, here_core[1], there_core[1], w_kv
     )
     (new_local,) = sums_call(last_body, [own, send], [(one, BF16)], "sum_hid")
 
-    there[2], here_core[2], kv_near = over_group(here[2]), over_core(here[2]), over_core(w_kv)
+    kv_near = over_core(w_kv)
     rows = [new_local, over_hid(new_local, 1), over_hid(new_local, 2), None]
-    rows[1], rows[2], there[2], here_core[2], kv_near = tie(
-        rows[1], rows[2], there[2], here_core[2], kv_near
-    )
-    rows[3], there_core[2] = over_hid(rows[2], 1), over_core(there[2])
-    moved = [(here[c], there[c], here_core[c], there_core[c]) for c in range(3)]
-    proj = [w_q, q_near, *moved[0], *moved[1], w_kv, kv_near, *moved[2]]
+    rows[1], rows[2], kv_near, kv_far = tie(rows[1], rows[2], kv_near, kv_far)
+    rows[3] = over_hid(rows[2], 1)
+    moved = [(here[c], there[c], here_core[c], there_core[c]) for c in range(2)]
+    proj = [w_q, q_near, *moved[0], *moved[1], w_kv, kv_near, kv_far, over_core(kv_far)]
     stats = stats_chain([[r] for r in rows], "stats_next")
     gain = attn_gain.reshape(1, -1)
     context = attend_call(place, rows, stats, gain, *tables, proj)

time: 151 us -> 146 us (0.967)
  starting transfers between devices: 32.1 us -> 25.3 us
  waiting for transfers between devices: 73.7 us -> 75.7 us
  local copies, waits for them, and re-layouts: 8.06 us -> 6.18 us
    ppermute x38 -> x36, starting transfers between devices: 32.1 us -> 25.3 us  [swap(): return lax.ppermute(value, axis, [(i, i ^ by) for i in range(size)])]
    ppermute x38 -> x36, waiting for transfers between devices: 73.7 us -> 75.7 us  [swap(): return lax.ppermute(value, axis, [(i, i ^ by) for i in range(size)])]
    unnamed x35 -> x34, local copies, waits for them, and re-layouts: 4.06 us -> 4.08 us
  transfers between devices with their start and end apart: 38 -> 36, of which waited for: 16 -> 17; matrix products, arithmetic and copies ran while one was open for 4% -> 4% of each run, Pallas kernels for 17% -> 17%
where the time goes in v3:
time: 146 us; the launch traced here: 145 us
  waiting for transfers between devices  75.7 us (52%)
  Pallas kernels  33.1 us (23%)
  starting transfers between devices  25.3 us (17%)
  local copies, waits for them, and re-layouts  6.18 us (4%)
  other arithmetic  3.78 us (3%)
    ppermute x36, waiting for transfers between devices, swap(): return lax.ppermute(value, axis, [(i, i ^ by) for i in range(size)])  75.7 us
    ppermute x36, starting transfers between devices, swap(): return lax.ppermute(value, axis, [(i, i ^ by) for i in range(size)])  25.3 us
    pallas_call x2, Pallas kernels, expert_call(): pl.pallas_call(expert_body, grid=(1,), in_specs=[SMEM] + held + [whole(ga...  22.9 us
    pallas_call x1, Pallas kernels, attend_call(): pl.pallas_call(attend_body, grid=(1,), in_specs=[SMEM] + [whole(v.shape)...  7.9 us
    unnamed x34, local copies, waits for them, and re-layouts  4.08 us
  transfers between devices with their start and end apart: 36, of which 17 were waited for; matrix products, arithmetic and copies ran while one was open for 4% of the time, Pallas kernels for 17%

profile of v3, /device:TPU:0, one launch (start us, length us, event | category | flops | bytes accessed | tf_op | source)
XLA Modules:
  0.0 145.2 jit_solution(5335705407377788834)
XLA Ops:
  0.7 4.1 %collective-permute-start.1 = (bf16[128,1024]{1,0:T(8,128)(2,1)}, bf16[128,1024]{1,0:T(8,128)(2,1)}, u32[]{:S(2)}, u32[]{:S(2)}) collective-permute-start(bf16[128,1024]{1,0:T(8,128)(2,1)} %resid_ref.1), channel_id=1, source_target_pairs={{0,2},{1,3},{2,0},{3,1},{4,6},{5,7},{6,4},{7,5},{8,10},{9,11},{10,... | collective-permute-start | bytes 786440 | tf_op jit(solution)/shard_map/ppermute | solution.py:331
  4.8 1.6 %collective-permute-start = (bf16[128,1024]{1,0:T(8,128)(2,1)}, bf16[128,1024]{1,0:T(8,128)(2,1)}, u32[]{:S(2)}, u32[]{:S(2)}) collective-permute-start(bf16[128,1024]{1,0:T(8,128)(2,1)} %resid_ref.1), channel_id=1, source_target_pairs={{0,1},{1,0},{2,3},{3,2},{4,5},{5,4},{6,7},{7,6},{8,9},{9,8},{10,11... | collective-permute-start | bytes 786440 | tf_op jit(solution)/shard_map/ppermute | solution.py:331
  8.2 1.6 %collective-permute-start.2 = (bf16[128,1152]{1,0:T(8,128)(2,1)S(1)}, bf16[128,1152]{1,0:T(8,128)(2,1)S(1)}, u32[]{:S(2)}, u32[]{:S(2)}) collective-permute-start(bf16[128,1152]{1,0:T(8,128)(2,1)S(1)} %pad_maximum_fusion.1.refs_0_.refs_12_), channel_id=1, source_target_pairs={{0,8},{4,12},{8,0},{12,4},{1,9},{5,13},{9,1},{13,5},{2,10},{6,14},... | collective-permute-start | bytes 884744 | tf_op jit(solution)/shard_map/ppermute | solution.py:331
  9.7 2.1 %constant_dynamic-slice_fusion.1 = (bf16[512,512]{1,0:T(8,128)(2,1)}, bf16[512,512]{1,0:T(8,128)(2,1)S(1)}) fusion(bf16[1024,1024]{1,0:T(8,128)(2,1)} %refs_10_, s32[]{:T(128)S(6)} %select_n.13), kind=kLoop, calls=%fused_computation.19 | loop fusion | bytes 2097156 | tf_op jit(solution)/shard_map/dynamic_slice | solution.py:375
  14.3 2.8 %collective-permute-done.1.refs_2_ = bf16[128,1024]{1,0:T(8,128)(2,1)} collective-permute-done((bf16[128,1024]{1,0:T(8,128)(2,1)}, bf16[128,1024]{1,0:T(8,128)(2,1)}, u32[]{:S(2)}, u32[]{:S(2)}) %collective-permute-start.1) | collective-permute-done | bytes 262176 | tf_op jit(solution)/shard_map/ppermute | solution.py:331
  18.2 1.5 %collective-permute-start.4 = (bf16[128,1024]{1,0:T(8,128)(2,1)}, bf16[128,1024]{1,0:T(8,128)(2,1)}, u32[]{:S(2)}, u32[]{:S(2)}) collective-permute-start(bf16[128,1024]{1,0:T(8,128)(2,1)} %collective-permute-done.refs_1_), channel_id=1, source_target_pairs={{0,8},{4,12},{8,0},{12,4},{1,9},{5,13},{9,1},{13,5},{2,10},{6,14},... | collective-permute-start | bytes 786440 | tf_op jit(solution)/shard_map/ppermute | solution.py:331
  20.5 8.9 %collective-permute-done.5.refs_12_ = bf16[512,512]{1,0:T(8,128)(2,1)S(1)} collective-permute-done((bf16[512,512]{1,0:T(8,128)(2,1)}, bf16[512,512]{1,0:T(8,128)(2,1)S(1)}, u32[]{:S(2)}, u32[]{:S(2)}) %collective-permute-start.5) | collective-permute-done | bytes 524320 | tf_op jit(solution)/shard_map/ppermute | solution.py:331
  29.4 4.0 %collective-permute-done.4.refs_1_ = bf16[128,1024]{1,0:T(8,128)(2,1)} collective-permute-done((bf16[128,1024]{1,0:T(8,128)(2,1)}, bf16[128,1024]{1,0:T(8,128)(2,1)}, u32[]{:S(2)}, u32[]{:S(2)}) %collective-permute-start.4) | collective-permute-done | bytes 262176 | tf_op jit(solution)/shard_map/ppermute | solution.py:331
  33.9 1.5 %collective-permute-start.12 = (bf16[128,1024]{1,0:T(8,128)(2,1)}, bf16[128,1024]{1,0:T(8,128)(2,1)}, u32[]{:S(2)}, u32[]{:S(2)}) collective-permute-start(bf16[128,1024]{1,0:T(8,128)(2,1)} %collective-permute-done.1.refs_2_), channel_id=1, source_target_pairs={{0,8},{4,12},{8,0},{12,4},{1,9},{5,13},{9,1},{13,5},{2,10},{6,14},... | collective-permute-start | bytes 786440 | tf_op jit(solution)/shard_map/ppermute | solution.py:331
  36.8 11.4 %near.1 = (f32[4,128,1024]{2,1,0:T(8,128)S(1)}, bf16[4,128,1024]{2,1,0:T(8,128)(2,1)S(1)}) custom-call(s32[3]{0:T(128)S(1)} %pad_add_fusion.place_ref, bf16[128,1152]{1,0:T(8,128)(2,1)} %copy-done.4, bf16[128,1024]{1,0:T(8,128)(2,1)} %collective-permute-done.refs_1_, bf16[128,1024]{1,0:T(8,128)(2,1)} %collective-permute-done.1.refs_2_, ...), custom_call_target="tpu_custom_call" | custom-call | flops 1 | bytes 1 | tf_op jit(solution)/shard_map/near/pallas_call | solution.py:178
  48.3 1.5 %collective-permute-start.16 = (bf16[512,512]{1,0:T(8,128)(2,1)S(1)}, bf16[512,512]{1,0:T(8,128)(2,1)S(1)}, u32[]{:S(2)}, u32[]{:S(2)}) collective-permute-start(bf16[512,512]{1,0:T(8,128)(2,1)S(1)} %get-tuple-element.87), channel_id=1, source_target_pairs={{0,8},{4,12},{8,0},{12,4},{1,9},{5,13},{9,1},{13,5},{2,10},{6,14},... | collective-permute-start | bytes 1572872 | tf_op jit(solution)/shard_map/ppermute | solution.py:331
  50.3 1.6 %collective-permute-done.14.refs_6_ = bf16[128,1024]{1,0:T(8,128)(2,1)S(1)} collective-permute-done((bf16[128,1024]{1,0:T(8,128)(2,1)}, bf16[128,1024]{1,0:T(8,128)(2,1)S(1)}, u32[]{:S(2)}, u32[]{:S(2)}) %collective-permute-start.14) | collective-permute-done | bytes 262176 | tf_op jit(solution)/shard_map/ppermute | solution.py:331
  53.3 11.4 %far.1 = (f32[4,128,1024]{2,1,0:T(8,128)S(1)}, bf16[4,128,1024]{2,1,0:T(8,128)(2,1)S(1)}) custom-call(s32[3]{0:T(128)S(1)} %pad_add_fusion.place_ref, bf16[128,1152]{1,0:T(8,128)(2,1)} %copy-done.5, bf16[128,1024]{1,0:T(8,128)(2,1)} %collective-permute-done.4.refs_1_, bf16[128,1024]{1,0:T(8,128)(2,1)} %collective-permute-done.12.refs_2_, ...), custom_call_target="tpu_custom_call" | custom-call | flops 1 | bytes 1 | tf_op jit(solution)/shard_map/far/pallas_call | solution.py:178
  65.4 1.5 %collective-permute-start.20 = (bf16[512,512]{1,0:T(8,128)(2,1)S(1)}, bf16[512,512]{1,0:T(8,128)(2,1)S(1)}, u32[]{:S(2)}, u32[]{:S(2)}) collective-permute-start(bf16[512,512]{1,0:T(8,128)(2,1)S(1)} %collective-permute-done.5.refs_12_), channel_id=1, source_target_pairs={{0,16},{16,0},{1,17},{17,1},{2,18},{18,2},{3,19},{19,3},{4,20},{20... | collective-permute-start | bytes 1572872 | tf_op jit(solution)/shard_map/ppermute | solution.py:331
  68.4 10.9 %collective-permute-done.20.refs_13_ = bf16[512,512]{1,0:T(8,128)(2,1)S(1)} collective-permute-done((bf16[512,512]{1,0:T(8,128)(2,1)S(1)}, bf16[512,512]{1,0:T(8,128)(2,1)S(1)}, u32[]{:S(2)}, u32[]{:S(2)}) %collective-permute-start.20) | collective-permute-done | bytes 524320 | tf_op jit(solution)/shard_map/ppermute | solution.py:331
  79.3 2.4 %collective-permute-done.18.far_ref = bf16[2,128,1024]{2,1,0:T(8,128)(2,1)S(1)} collective-permute-done((bf16[2,128,1024]{2,1,0:T(8,128)(2,1)S(1)}, bf16[2,128,1024]{2,1,0:T(8,128)(2,1)S(1)}, u32[]{:S(2)}, u32[]{:S(2)}) %collective-permute-start.18) | collective-permute-done | bytes 524320 | tf_op jit(solution)/shard_map/ppermute | solution.py:331
  83.1 1.5 %collective-permute-start.23 = (bf16[512,512]{1,0:T(8,128)(2,1)S(1)}, bf16[512,512]{1,0:T(8,128)(2,1)S(1)}, u32[]{:S(2)}, u32[]{:S(2)}) collective-permute-start(bf16[512,512]{1,0:T(8,128)(2,1)S(1)} %collective-permute-done.16.refs_16_), channel_id=1, source_target_pairs={{0,16},{16,0},{1,17},{17,1},{2,18},{18,2},{3,19},{19,3},{4,20},{20... | collective-permute-start | bytes 1572872 | tf_op jit(solution)/shard_map/ppermute | solution.py:331
  85.1 10.1 %collective-permute-done.21.hid_ref = bf16[2,128,1024]{2,1,0:T(8,128)(2,1)S(1)} collective-permute-done((bf16[2,128,1024]{2,1,0:T(8,128)(2,1)S(1)}, bf16[2,128,1024]{2,1,0:T(8,128)(2,1)S(1)}, u32[]{:S(2)}, u32[]{:S(2)}) %collective-permute-start.21) | collective-permute-done | bytes 524320 | tf_op jit(solution)/shard_map/ppermute | solution.py:331
  98.5 13.4 %collective-permute-done.26.got_ref = bf16[128,1024]{1,0:T(8,128)(2,1)S(1)} collective-permute-done((bf16[128,1024]{1,0:T(8,128)(2,1)S(1)}, bf16[128,1024]{1,0:T(8,128)(2,1)S(1)}, u32[]{:S(2)}, u32[]{:S(2)}) %collective-permute-start.26) | collective-permute-done | bytes 262176 | tf_op jit(solution)/shard_map/ppermute | solution.py:331
  112.7 1.9 %collective-permute-start.30 = (bf16[128,1024]{1,0:T(8,128)(2,1)}, bf16[128,1024]{1,0:T(8,128)(2,1)S(1)}, u32[]{:S(2)}, u32[]{:S(2)}) collective-permute-start(bf16[128,1024]{1,0:T(8,128)(2,1)} %sum_hid.1.refs_0_), channel_id=1, source_target_pairs={{0,1},{1,0},{2,3},{3,2},{4,5},{5,4},{6,7},{7,6},{8,9},{9,8},{10,11... | collective-permute-start | bytes 786440 | tf_op jit(solution)/shard_map/ppermute | solution.py:331
  114.6 7.7 %collective-permute-done.33.refs_22_ = bf16[1024,512]{1,0:T(8,128)(2,1)S(1)} collective-permute-done((bf16[1024,512]{1,0:T(8,128)(2,1)S(1)}, bf16[1024,512]{1,0:T(8,128)(2,1)S(1)}, u32[]{:S(2)}, u32[]{:S(2)}) %collective-permute-start.33) | collective-permute-done | bytes 1048608 | tf_op jit(solution)/shard_map/ppermute | solution.py:331
  122.3 4.6 %collective-permute-done.31.refs_0_.refs_2_ = bf16[128,1024]{1,0:T(8,128)(2,1)S(1)} collective-permute-done((bf16[128,1024]{1,0:T(8,128)(2,1)}, bf16[128,1024]{1,0:T(8,128)(2,1)S(1)}, u32[]{:S(2)}, u32[]{:S(2)}) %collective-permute-start.31) | collective-permute-done | bytes 262176 | tf_op jit(solution)/shard_map/ppermute | solution.py:331
  129.2 6.7 %collective-permute-done.34.refs_0_.refs_3_ = bf16[128,1024]{1,0:T(8,128)(2,1)S(1)} collective-permute-done((bf16[128,1024]{1,0:T(8,128)(2,1)S(1)}, bf16[128,1024]{1,0:T(8,128)(2,1)S(1)}, u32[]{:S(2)}, u32[]{:S(2)}) %collective-permute-start.34) | collective-permute-done | bytes 262176 | tf_op jit(solution)/shard_map/ppermute | solution.py:331
  137.1 7.9 %attend.1 = bf16[128,1024]{1,0:T(8,128)(2,1)} custom-call(s32[3]{0:T(128)S(1)} %pad_add_fusion.place_ref, bf16[128,1024]{1,0:T(8,128)(2,1)S(1)} %copy-done.2, bf16[128,1024]{1,0:T(8,128)(2,1)S(1)} %collective-permute-done.30.refs_0_.refs_1_, bf16[128,1024]{1,0:T(8,128)(2,1)S(1)} %collective-permute-done.31.refs_0_.refs_2_, ...), custom_call_target="tpu_custom_call" | custom-call | flops 1 | bytes 1 | tf_op jit(solution)/shard_map/attend/pallas_call | solution.py:313
  (108 shorter events, 21.6 us)
Async XLA Ops:
  0.7 16.5 %collective-permute-start.1 = (bf16[128,1024]{1,0:T(8,128)(2,1)}, bf16[128,1024]{1,0:T(8,128)(2,1)}, u32[]{:S(2)}, u32[]{:S(2)}) collective-permute-start(bf16[128,1024]{1,0:T(8,128)(2,1)} %resid_ref.1), channel_id=1, source_target_pairs={{0,2},{1,3},{2,0},{3,1},{4,6},{5,7},{6,4},{7,5},{8,10},{9,11},{10,... | collective-permute-start | bytes 786440 | tf_op jit(solution)/shard_map/ppermute | solution.py:331
  11.8 17.6 %collective-permute-start.5 = (bf16[512,512]{1,0:T(8,128)(2,1)}, bf16[512,512]{1,0:T(8,128)(2,1)S(1)}, u32[]{:S(2)}, u32[]{:S(2)}) collective-permute-start(bf16[512,512]{1,0:T(8,128)(2,1)} %get-tuple-element.134), channel_id=1, source_target_pairs={{0,8},{4,12},{8,0},{12,4},{1,9},{5,13},{9,1},{13,5},{2,10},{6,14},... | collective-permute-start | bytes 1572872 | tf_op jit(solution)/shard_map/ppermute | solution.py:331
  18.2 15.2 %collective-permute-start.4 = (bf16[128,1024]{1,0:T(8,128)(2,1)}, bf16[128,1024]{1,0:T(8,128)(2,1)}, u32[]{:S(2)}, u32[]{:S(2)}) collective-permute-start(bf16[128,1024]{1,0:T(8,128)(2,1)} %collective-permute-done.refs_1_), channel_id=1, source_target_pairs={{0,8},{4,12},{8,0},{12,4},{1,9},{5,13},{9,1},{13,5},{2,10},{6,14},... | collective-permute-start | bytes 786440 | tf_op jit(solution)/shard_map/ppermute | solution.py:331
  19.7 15.7 %collective-permute-start.6 = (bf16[128,1152]{1,0:T(8,128)(2,1)S(1)}, bf16[128,1152]{1,0:T(8,128)(2,1)S(1)}, u32[]{:S(2)}, u32[]{:S(2)}) collective-permute-start(bf16[128,1152]{1,0:T(8,128)(2,1)S(1)} %pad_maximum_fusion.1.refs_0_.refs_12_), channel_id=1, source_target_pairs={{0,4},{4,0},{8,12},{12,8},{1,5},{5,1},{9,13},{13,9},{2,6},{6,2},{1... | collective-permute-start | bytes 884744 | tf_op jit(solution)/shard_map/ppermute | solution.py:331
  19.7 13.7 %collective-permute-start.3 = (bf16[128,1024]{1,0:T(8,128)(2,1)}, bf16[128,1024]{1,0:T(8,128)(2,1)}, u32[]{:S(2)}, u32[]{:S(2)}) collective-permute-start(bf16[128,1024]{1,0:T(8,128)(2,1)} %collective-permute-done.1.refs_2_), channel_id=1, source_target_pairs={{0,1},{1,0},{2,3},{3,2},{4,5},{5,4},{6,7},{7,6},{8,9},{9,8},{10,11... | collective-permute-start | bytes 786440 | tf_op jit(solution)/shard_map/ppermute | solution.py:331
  20.3 13.6 %collective-permute-start.7 = (bf16[128,1024]{1,0:T(8,128)(2,1)}, bf16[128,1024]{1,0:T(8,128)(2,1)S(1)}, u32[]{:S(2)}, u32[]{:S(2)}) collective-permute-start(bf16[128,1024]{1,0:T(8,128)(2,1)} %collective-permute-done.refs_1_), channel_id=1, source_target_pairs={{0,4},{4,0},{8,12},{12,8},{1,5},{5,1},{9,13},{13,9},{2,6},{6,2},{1... | collective-permute-start | bytes 786440 | tf_op jit(solution)/shard_map/ppermute | solution.py:331
  33.4 14.9 %collective-permute-start.10 = (bf16[128,1152]{1,0:T(8,128)(2,1)S(1)}, bf16[128,1152]{1,0:T(8,128)(2,1)S(1)}, u32[]{:S(2)}, u32[]{:S(2)}) collective-permute-start(bf16[128,1152]{1,0:T(8,128)(2,1)S(1)} %collective-permute-done.2.refs_0_.refs_12_), channel_id=1, source_target_pairs={{0,4},{4,0},{8,12},{12,8},{1,5},{5,1},{9,13},{13,9},{2,6},{6,2},{1... | collective-permute-start | bytes 884744 | tf_op jit(solution)/shard_map/ppermute | solution.py:331
  33.9 14.4 %collective-permute-start.12 = (bf16[128,1024]{1,0:T(8,128)(2,1)}, bf16[128,1024]{1,0:T(8,128)(2,1)}, u32[]{:S(2)}, u32[]{:S(2)}) collective-permute-start(bf16[128,1024]{1,0:T(8,128)(2,1)} %collective-permute-done.1.refs_2_), channel_id=1, source_target_pairs={{0,8},{4,12},{8,0},{12,4},{1,9},{5,13},{9,1},{13,5},{2,10},{6,14},... | collective-permute-start | bytes 786440 | tf_op jit(solution)/shard_map/ppermute | solution.py:331
  35.4 12.9 %collective-permute-start.11 = (bf16[128,1024]{1,0:T(8,128)(2,1)}, bf16[128,1024]{1,0:T(8,128)(2,1)}, u32[]{:S(2)}, u32[]{:S(2)}) collective-permute-start(bf16[128,1024]{1,0:T(8,128)(2,1)} %collective-permute-done.4.refs_1_), channel_id=1, source_target_pairs={{0,4},{4,0},{8,12},{12,8},{1,5},{5,1},{9,13},{13,9},{2,6},{6,2},{1... | collective-permute-start | bytes 786440 | tf_op jit(solution)/shard_map/ppermute | solution.py:331
  48.3 16.4 %collective-permute-start.16 = (bf16[512,512]{1,0:T(8,128)(2,1)S(1)}, bf16[512,512]{1,0:T(8,128)(2,1)S(1)}, u32[]{:S(2)}, u32[]{:S(2)}) collective-permute-start(bf16[512,512]{1,0:T(8,128)(2,1)S(1)} %get-tuple-element.87), channel_id=1, source_target_pairs={{0,8},{4,12},{8,0},{12,4},{1,9},{5,13},{9,1},{13,5},{2,10},{6,14},... | collective-permute-start | bytes 1572872 | tf_op jit(solution)/shard_map/ppermute | solution.py:331
  65.0 14.3 %collective-permute-start.19 = (bf16[4,128,1024]{2,1,0:T(8,128)(2,1)S(1)}, bf16[4,128,1024]{2,1,0:T(8,128)(2,1)S(1)}, u32[]{:S(2)}, u32[]{:S(2)}) collective-permute-start(bf16[4,128,1024]{2,1,0:T(8,128)(2,1)S(1)} %get-tuple-element.90), channel_id=1, source_target_pairs={{0,4},{4,0},{8,12},{12,8},{1,5},{5,1},{9,13},{13,9},{2,6},{6,2},{1... | collective-permute-start | bytes 3145736 | tf_op jit(solution)/shard_map/ppermute | solution.py:331
  65.4 14.0 %collective-permute-start.20 = (bf16[512,512]{1,0:T(8,128)(2,1)S(1)}, bf16[512,512]{1,0:T(8,128)(2,1)S(1)}, u32[]{:S(2)}, u32[]{:S(2)}) collective-permute-start(bf16[512,512]{1,0:T(8,128)(2,1)S(1)} %collective-permute-done.5.refs_12_), channel_id=1, source_target_pairs={{0,16},{16,0},{1,17},{17,1},{2,18},{18,2},{3,19},{19,3},{4,20},{20... | collective-permute-start | bytes 1572872 | tf_op jit(solution)/shard_map/ppermute | solution.py:331
  67.7 14.0 %collective-permute-start.18 = (bf16[2,128,1024]{2,1,0:T(8,128)(2,1)S(1)}, bf16[2,128,1024]{2,1,0:T(8,128)(2,1)S(1)}, u32[]{:S(2)}, u32[]{:S(2)}) collective-permute-start(bf16[2,128,1024]{2,1,0:T(8,128)(2,1)S(1)} %get-tuple-element.89), channel_id=1, source_target_pairs={{0,8},{4,12},{8,0},{12,4},{1,9},{5,13},{9,1},{13,5},{2,10},{6,14},... | collective-permute-start | bytes 1572872 | tf_op jit(solution)/shard_map/ppermute | solution.py:331
  81.9 13.2 %collective-permute-start.21 = (bf16[2,128,1024]{2,1,0:T(8,128)(2,1)S(1)}, bf16[2,128,1024]{2,1,0:T(8,128)(2,1)S(1)}, u32[]{:S(2)}, u32[]{:S(2)}) collective-permute-start(bf16[2,128,1024]{2,1,0:T(8,128)(2,1)S(1)} %sum_chip.1), channel_id=1, source_target_pairs={{0,1},{1,0},{2,3},{3,2},{4,5},{5,4},{6,7},{7,6},{8,9},{9,8},{10,11... | collective-permute-start | bytes 1572872 | tf_op jit(solution)/shard_map/ppermute | solution.py:331
  82.5 12.9 %collective-permute-start.22 = (bf16[2,128,1024]{2,1,0:T(8,128)(2,1)S(1)}, bf16[2,128,1024]{2,1,0:T(8,128)(2,1)S(1)}, u32[]{:S(2)}, u32[]{:S(2)}) collective-permute-start(bf16[2,128,1024]{2,1,0:T(8,128)(2,1)S(1)} %get-tuple-element.96), channel_id=1, source_target_pairs={{0,8},{4,12},{8,0},{12,4},{1,9},{5,13},{9,1},{13,5},{2,10},{6,14},... | collective-permute-start | bytes 1572872 | tf_op jit(solution)/shard_map/ppermute | solution.py:331
  83.1 12.6 %collective-permute-start.23 = (bf16[512,512]{1,0:T(8,128)(2,1)S(1)}, bf16[512,512]{1,0:T(8,128)(2,1)S(1)}, u32[]{:S(2)}, u32[]{:S(2)}) collective-permute-start(bf16[512,512]{1,0:T(8,128)(2,1)S(1)} %collective-permute-done.16.refs_16_), channel_id=1, source_target_pairs={{0,16},{16,0},{1,17},{17,1},{2,18},{18,2},{3,19},{19,3},{4,20},{20... | collective-permute-start | bytes 1572872 | tf_op jit(solution)/shard_map/ppermute | solution.py:331
  95.7 16.2 %collective-permute-start.27 = (bf16[1024,1024]{1,0:T(8,128)(2,1)S(1)}, bf16[1024,1024]{1,0:T(8,128)(2,1)S(1)}, u32[]{:S(2)}, u32[]{:S(2)}) collective-permute-start(bf16[1024,1024]{1,0:T(8,128)(2,1)S(1)} %copy-done), channel_id=1, source_target_pairs={{0,4},{4,0},{8,12},{12,8},{1,5},{5,1},{9,13},{13,9},{2,6},{6,2},{1... | collective-permute-start | bytes 6291464 | tf_op jit(solution)/shard_map/ppermute | solution.py:331
  95.7 16.1 %collective-permute-start.28 = (bf16[512,512]{1,0:T(8,128)(2,1)S(1)}, bf16[512,512]{1,0:T(8,128)(2,1)S(1)}, u32[]{:S(2)}, u32[]{:S(2)}) collective-permute-start(bf16[512,512]{1,0:T(8,128)(2,1)S(1)} %collective-permute-done.16.refs_16_), channel_id=1, source_target_pairs={{0,4},{4,0},{8,12},{12,8},{1,5},{5,1},{9,13},{13,9},{2,6},{6,2},{1... | collective-permute-start | bytes 1572872 | tf_op jit(solution)/shard_map/ppermute | solution.py:331
  96.2 15.6 %collective-permute-start.29 = (bf16[512,512]{1,0:T(8,128)(2,1)S(1)}, bf16[512,512]{1,0:T(8,128)(2,1)S(1)}, u32[]{:S(2)}, u32[]{:S(2)}) collective-permute-start(bf16[512,512]{1,0:T(8,128)(2,1)S(1)} %collective-permute-done.23.refs_17_), channel_id=1, source_target_pairs={{0,4},{4,0},{8,12},{12,8},{1,5},{5,1},{9,13},{13,9},{2,6},{6,2},{1... | collective-permute-start | bytes 1572872 | tf_op jit(solution)/shard_map/ppermute | solution.py:331
  96.6 15.2 %collective-permute-start.26 = (bf16[128,1024]{1,0:T(8,128)(2,1)S(1)}, bf16[128,1024]{1,0:T(8,128)(2,1)S(1)}, u32[]{:S(2)}, u32[]{:S(2)}) collective-permute-start(bf16[128,1024]{1,0:T(8,128)(2,1)S(1)} %get-tuple-element.105), channel_id=1, source_target_pairs={{0,2},{1,3},{2,0},{3,1},{4,6},{5,7},{6,4},{7,5},{8,10},{9,11},{10,... | collective-permute-start | bytes 786440 | tf_op jit(solution)/shard_map/ppermute | solution.py:331
  97.0 25.2 %collective-permute-start.33 = (bf16[1024,512]{1,0:T(8,128)(2,1)S(1)}, bf16[1024,512]{1,0:T(8,128)(2,1)S(1)}, u32[]{:S(2)}, u32[]{:S(2)}) collective-permute-start(bf16[1024,512]{1,0:T(8,128)(2,1)S(1)} %pad_maximum_fusion.refs_20_), channel_id=1, source_target_pairs={{0,8},{4,12},{8,0},{12,4},{1,9},{5,13},{9,1},{13,5},{2,10},{6,14},... | collective-permute-start | bytes 3145736 | tf_op jit(solution)/shard_map/ppermute | solution.py:331
  111.9 15.4 %collective-permute-start.32 = (bf16[1024,512]{1,0:T(8,128)(2,1)S(1)}, bf16[1024,512]{1,0:T(8,128)(2,1)S(1)}, u32[]{:S(2)}, u32[]{:S(2)}) collective-permute-start(bf16[1024,512]{1,0:T(8,128)(2,1)S(1)} %pad_maximum_fusion.refs_20_), channel_id=1, source_target_pairs={{0,4},{4,0},{8,12},{12,8},{1,5},{5,1},{9,13},{13,9},{2,6},{6,2},{1... | collective-permute-start | bytes 3145736 | tf_op jit(solution)/shard_map/ppermute | solution.py:331
  112.7 14.2 %collective-permute-start.31 = (bf16[128,1024]{1,0:T(8,128)(2,1)}, bf16[128,1024]{1,0:T(8,128)(2,1)S(1)}, u32[]{:S(2)}, u32[]{:S(2)}) collective-permute-start(bf16[128,1024]{1,0:T(8,128)(2,1)} %sum_hid.1.refs_0_), channel_id=1, source_target_pairs={{0,2},{1,3},{2,0},{3,1},{4,6},{5,7},{6,4},{7,5},{8,10},{9,11},{10,... | collective-permute-start | bytes 786440 | tf_op jit(solution)/shard_map/ppermute | solution.py:331
  112.7 14.5 %collective-permute-start.30 = (bf16[128,1024]{1,0:T(8,128)(2,1)}, bf16[128,1024]{1,0:T(8,128)(2,1)S(1)}, u32[]{:S(2)}, u32[]{:S(2)}) collective-permute-start(bf16[128,1024]{1,0:T(8,128)(2,1)} %sum_hid.1.refs_0_), channel_id=1, source_target_pairs={{0,1},{1,0},{2,3},{3,2},{4,5},{5,4},{6,7},{7,6},{8,9},{9,8},{10,11... | collective-permute-start | bytes 786440 | tf_op jit(solution)/shard_map/ppermute | solution.py:331
  (29 other events, 270.9 us)

commit v4 on v3

--- a/solution.py
+++ b/solution.py
@@ -172,7 +172,8 @@
     width, units = gate_w.shape
     once = pl.Buffered(1)
     held = [pl.BlockSpec((rows, local), lambda *_: (0, 0), pipeline_mode=once)] * 8
-    pieces = [pltpu.with_memory_space_constraint(p, pltpu.HBM) for p in pieces]
+    fixed = [pltpu.with_memory_space_constraint(p, pltpu.HBM) for p in pieces[:4]]
+    pieces = fixed + list(pieces[4:])
     routed = [pieces[0], pieces[4]]
     shape = (4, rows, local)
     return pl.pallas_call(
@@ -244,22 +245,43 @@
     out_ref[...] = (own_ref[...] + got_ref[...].astype(F32)).astype(BF16)
 
 
+def stage_body(*refs):
+    count = (len(refs) - 2) // 2
+    copies = [
+        pltpu.make_async_copy(refs[i], refs[count + i], refs[-1].at[i]) for i in range(count)
+    ]
+    for c in copies:
+        c.start()
+    refs[-2][...] = jnp.zeros_like(refs[-2])
+    for c in copies:
+        c.wait()
+
+
+def stage_call(arrays, name):
+    return pl.pallas_call(
+        stage_body,
+        in_specs=[pl.BlockSpec(memory_space=pl.ANY)] * len(arrays),
+        out_specs=[VMEM] * (len(arrays) + 1),
+        out_shape=[pltpu.VMEM(a.shape, a.dtype) for a in arrays]
+        + [jax.ShapeDtypeStruct((8, 128), F32)],
+        scratch_shapes=[pltpu.SemaphoreType.DMA((len(arrays),))],
+        compiler_params=pltpu.CompilerParams(vmem_limit_bytes=LIMIT << 20),
+        cost_estimate=TINY,
+        name=name,
+    )(*arrays)
+
+
 def attend_body(place_ref, *refs):
     pieces = refs[:4]
     mean_ref, spread_ref, gain_ref, cos_ref, sin_ref, bias_ref = refs[4:10]
-    sources = refs[10:24]
-    out_ref, normed, total = refs[24:27]
-    weights = refs[27:41]
-    sems = refs[41]
+    weights = list(refs[10:23])
+    last_hbm, out_ref, normed, total, last_ref, sem = refs[24:30]
+    weights.append(last_ref)
     rows, local = pieces[0].shape
     half = local // 2
     group, hid, sect = place_ref[0], place_ref[1], place_ref[2]
-    copies = [
-        pltpu.make_async_copy(src, dst, sems.at[i])
-        for i, (src, dst) in enumerate(zip(sources, weights))
-    ]
-    for c in copies:
-        c.start()
+    copy = pltpu.make_async_copy(last_hbm, last_ref, sem.at[0])
+    copy.start()
     norm_rows(pieces, gain_ref, mean_ref, spread_ref, hid, normed, 0, 64)
 
     def rows_of(at, count):
@@ -275,13 +297,11 @@
         plan.append([(wholes[i], i, cols) for i in range(2)])
         plan[c] += [(halves[i], 2 + 4 * c + i, slice(0, half)) for i in range(4)]
     plan.append([(wholes[i], 10 + i, slice(0, half)) for i in range(4)])
-    waited = set()
     for c, terms in enumerate(plan):
         acc = None
         for lhs, n, cols in terms:
-            if n not in waited:
-                copies[n].wait()
-                waited.add(n)
+            if n == 13:
+                copy.wait()
             term = jnp.dot(lhs, weights[n][:, cols], preferred_element_type=F32)
             acc = term if acc is None else acc + term
         total[:, c * half : (c + 1) * half] = acc
@@ -315,12 +335,13 @@
         grid=(1,),
         in_specs=[SMEM]
         + [whole(v.shape) for v in (*pieces, *stats, gain, cos, sin, bias)]
-        + [pl.BlockSpec(memory_space=pl.ANY)] * len(weights),
+        + [VMEM] * (len(weights) - 2)
+        + [whole((8, 128)), pl.BlockSpec(memory_space=pl.ANY)],
         out_specs=whole((rows, local)),
         out_shape=jax.ShapeDtypeStruct((rows, local), BF16),
         scratch_shapes=[pltpu.VMEM((rows, 4 * local), BF16), pltpu.VMEM((rows, 3 * local // 2), F32)]
-        + [pltpu.VMEM(w.shape, BF16) for w in weights]
-        + [pltpu.SemaphoreType.DMA((len(weights),))],
+        + [pltpu.VMEM(weights[-1].shape, BF16)]
+        + [pltpu.SemaphoreType.DMA((1,))],
         compiler_params=pltpu.CompilerParams(vmem_limit_bytes=20 << 20),
         cost_estimate=TINY,
         name="attend",
@@ -442,7 +463,10 @@
     rows[1], rows[2], kv_near, kv_far = tie(rows[1], rows[2], kv_near, kv_far)
     rows[3] = over_hid(rows[2], 1)
     moved = [(here[c], there[c], here_core[c], there_core[c]) for c in range(2)]
-    proj = [w_q, q_near, *moved[0], *moved[1], w_kv, kv_near, kv_far, over_core(kv_far)]
+    proj = [w_q, q_near, *moved[0], *moved[1], w_kv, kv_near, kv_far]
+    *proj, token = stage_call(proj, "stage")
+    rows[3], token = tie(rows[3], token)
+    proj += [token, over_core(kv_far)]
     stats = stats_chain([[r] for r in rows], "stats_next")
     gain = attn_gain.reshape(1, -1)
     context = attend_call(place, rows, stats, gain, *tables, proj)

time: 146 us -> 142 us (0.973)
  local copies, waits for them, and re-layouts: 6.18 us -> 3.08 us
  waiting for transfers between devices: 75.7 us -> 77.3 us
    unnamed x34 -> x18, local copies, waits for them, and re-layouts: 4.08 us -> 0.98 us
    pallas_call x1, Pallas kernels: 7.9 us -> 6.16 us  [attend_call(): pl.pallas_call(attend_body, grid=(1,), in_specs=[SMEM] + [whole(v.shape)...]
    ppermute x36, waiting for transfers between devices: 75.7 us -> 77.3 us  [swap(): return lax.ppermute(value, axis, [(i, i ^ by) for i in range(size)])]
  transfers between devices with their start and end apart: 36 -> 36, of which waited for: 17 -> 19; matrix products, arithmetic and copies ran while one was open for 4% -> 5% of each run, Pallas kernels for 17% -> 18%
where the time goes in v4:
time: 142 us
  waiting for transfers between devices  77.3 us (54%)
  Pallas kernels  31.7 us (22%)
  starting transfers between devices  24.6 us (17%)
  other arithmetic  4.49 us (3%)
  local copies, waits for them, and re-layouts  3.08 us (2%)
    ppermute x36, waiting for transfers between devices, swap(): return lax.ppermute(value, axis, [(i, i ^ by) for i in range(size)])  77.3 us
    ppermute x36, starting transfers between devices, swap(): return lax.ppermute(value, axis, [(i, i ^ by) for i in range(size)])  24.6 us
    pallas_call x2, Pallas kernels, expert_call(): pl.pallas_call(expert_body, grid=(1,), in_specs=[SMEM] + held + [whole(ga...  22.3 us
    pallas_call x1, Pallas kernels, attend_call(): pl.pallas_call(attend_body, grid=(1,), in_specs=[SMEM] + [whole(v.shape)...  6.16 us
  transfers between devices with their start and end apart: 36, of which 19 were waited for; matrix products, arithmetic and copies ran while one was open for 5% of the time, Pallas kernels for 18%

profile of v4, /device:TPU:0, one launch (start us, length us, event | category | flops | bytes accessed | tf_op | source)
XLA Modules:
  0.0 142.2 jit_solution(10318976439164763085)
XLA Ops:
  0.7 3.1 %collective-permute-start = (bf16[128,1024]{1,0:T(8,128)(2,1)}, bf16[128,1024]{1,0:T(8,128)(2,1)}, u32[]{:S(2)}, u32[]{:S(2)}) collective-permute-start(bf16[128,1024]{1,0:T(8,128)(2,1)} %resid_ref.1), channel_id=1, source_target_pairs={{0,1},{1,0},{2,3},{3,2},{4,5},{5,4},{6,7},{7,6},{8,9},{9,8},{10,11... | collective-permute-start | bytes 786440 | tf_op jit(solution)/shard_map/ppermute | solution.py:352
  3.7 2.6 %collective-permute-start.1 = (bf16[128,1024]{1,0:T(8,128)(2,1)}, bf16[128,1024]{1,0:T(8,128)(2,1)}, u32[]{:S(2)}, u32[]{:S(2)}) collective-permute-start(bf16[128,1024]{1,0:T(8,128)(2,1)} %resid_ref.1), channel_id=1, source_target_pairs={{0,2},{1,3},{2,0},{3,1},{4,6},{5,7},{6,4},{7,5},{8,10},{9,11},{10,... | collective-permute-start | bytes 786440 | tf_op jit(solution)/shard_map/ppermute | solution.py:352
  7.2 1.7 %pad_maximum_fusion.1.refs_0_.refs_12_ = bf16[128,1152]{1,0:T(8,128)(2,1)} fusion(bf16[128,128]{1,0:T(8,128)(2,1)S(1)} %convert_element_type.13, bf16[128,1024]{1,0:T(8,128)(2,1)} %resid_ref.1), kind=kLoop, calls=%fused_computation.1 | loop fusion | flops 589824 | bytes 589824 | tf_op jit(solution)/shard_map/concatenate | solution.py:406
  10.4 2.1 %constant_dynamic-slice_fusion.1 = (bf16[512,512]{1,0:T(8,128)(2,1)S(1)}, bf16[512,512]{1,0:T(8,128)(2,1)}) fusion(bf16[1024,1024]{1,0:T(8,128)(2,1)} %refs_0_, s32[]{:T(128)S(6)} %select_n.13), kind=kLoop, calls=%fused_computation.19 | loop fusion | bytes 2097156 | tf_op jit(solution)/shard_map/dynamic_slice | solution.py:396
  15.9 2.5 %collective-permute-done.1.refs_2_ = bf16[128,1024]{1,0:T(8,128)(2,1)} collective-permute-done((bf16[128,1024]{1,0:T(8,128)(2,1)}, bf16[128,1024]{1,0:T(8,128)(2,1)}, u32[]{:S(2)}, u32[]{:S(2)}) %collective-permute-start.1) | collective-permute-done | bytes 262176 | tf_op jit(solution)/shard_map/ppermute | solution.py:352
  21.3 9.0 %collective-permute-done.5.refs_2_ = bf16[512,512]{1,0:T(8,128)(2,1)S(1)} collective-permute-done((bf16[512,512]{1,0:T(8,128)(2,1)S(1)}, bf16[512,512]{1,0:T(8,128)(2,1)S(1)}, u32[]{:S(2)}, u32[]{:S(2)}) %collective-permute-start.5) | collective-permute-done | bytes 524320 | tf_op jit(solution)/shard_map/ppermute | solution.py:352
  30.8 3.4 %collective-permute-done.4.refs_1_ = bf16[128,1024]{1,0:T(8,128)(2,1)} collective-permute-done((bf16[128,1024]{1,0:T(8,128)(2,1)}, bf16[128,1024]{1,0:T(8,128)(2,1)}, u32[]{:S(2)}, u32[]{:S(2)}) %collective-permute-start.4) | collective-permute-done | bytes 262176 | tf_op jit(solution)/shard_map/ppermute | solution.py:352
  34.2 1.5 %collective-permute-start.12 = (bf16[128,1024]{1,0:T(8,128)(2,1)}, bf16[128,1024]{1,0:T(8,128)(2,1)}, u32[]{:S(2)}, u32[]{:S(2)}) collective-permute-start(bf16[128,1024]{1,0:T(8,128)(2,1)} %collective-permute-done.1.refs_2_), channel_id=1, source_target_pairs={{0,8},{4,12},{8,0},{12,4},{1,9},{5,13},{9,1},{13,5},{2,10},{6,14},... | collective-permute-start | bytes 786440 | tf_op jit(solution)/shard_map/ppermute | solution.py:352
  36.4 11.2 %near.1 = (f32[4,128,1024]{2,1,0:T(8,128)S(1)}, bf16[4,128,1024]{2,1,0:T(8,128)(2,1)S(1)}) custom-call(s32[3]{0:T(128)S(1)} %pad_add_fusion.place_ref, bf16[128,1152]{1,0:T(8,128)(2,1)} %pad_maximum_fusion.1.refs_0_.refs_12_, bf16[128,1024]{1,0:T(8,128)(2,1)} %collective-permute-done.refs_1_, bf16[128,1024]{1,0:T(8,128)(2,1)} %collective-permute-done.1.refs_2_, ...), custom_call_target="tpu_custom_call" | custom-call | flops 1 | bytes 1 | tf_op jit(solution)/shard_map/near/pallas_call | solution.py:179
  48.9 1.5 %collective-permute-start.16 = (bf16[512,512]{1,0:T(8,128)(2,1)S(1)}, bf16[512,512]{1,0:T(8,128)(2,1)S(1)}, u32[]{:S(2)}, u32[]{:S(2)}) collective-permute-start(bf16[512,512]{1,0:T(8,128)(2,1)S(1)} %copy-done.4), channel_id=1, source_target_pairs={{0,8},{4,12},{8,0},{12,4},{1,9},{5,13},{9,1},{13,5},{2,10},{6,14},... | collective-permute-start | bytes 1572872 | tf_op jit(solution)/shard_map/ppermute | solution.py:352
  52.5 11.1 %far.1 = (f32[4,128,1024]{2,1,0:T(8,128)S(1)}, bf16[4,128,1024]{2,1,0:T(8,128)(2,1)S(1)}) custom-call(s32[3]{0:T(128)S(1)} %pad_add_fusion.place_ref, bf16[128,1152]{1,0:T(8,128)(2,1)} %collective-permute-done.2.refs_0_.refs_12_, bf16[128,1024]{1,0:T(8,128)(2,1)} %collective-permute-done.4.refs_1_, bf16[128,1024]{1,0:T(8,128)(2,1)} %collective-permute-done.12.refs_2_, ...), custom_call_target="tpu_custom_call" | custom-call | flops 1 | bytes 1 | tf_op jit(solution)/shard_map/far/pallas_call | solution.py:179
  64.2 1.5 %collective-permute-start.20 = (bf16[512,512]{1,0:T(8,128)(2,1)S(1)}, bf16[512,512]{1,0:T(8,128)(2,1)S(1)}, u32[]{:S(2)}, u32[]{:S(2)}) collective-permute-start(bf16[512,512]{1,0:T(8,128)(2,1)S(1)} %collective-permute-done.5.refs_2_), channel_id=1, source_target_pairs={{0,16},{16,0},{1,17},{17,1},{2,18},{18,2},{3,19},{19,3},{4,20},{20... | collective-permute-start | bytes 1572872 | tf_op jit(solution)/shard_map/ppermute | solution.py:352
  67.2 11.0 %collective-permute-done.20.refs_3_ = bf16[512,512]{1,0:T(8,128)(2,1)S(1)} collective-permute-done((bf16[512,512]{1,0:T(8,128)(2,1)S(1)}, bf16[512,512]{1,0:T(8,128)(2,1)S(1)}, u32[]{:S(2)}, u32[]{:S(2)}) %collective-permute-start.20) | collective-permute-done | bytes 524320 | tf_op jit(solution)/shard_map/ppermute | solution.py:352
  78.2 2.4 %collective-permute-done.18.far_ref = bf16[2,128,1024]{2,1,0:T(8,128)(2,1)S(1)} collective-permute-done((bf16[2,128,1024]{2,1,0:T(8,128)(2,1)S(1)}, bf16[2,128,1024]{2,1,0:T(8,128)(2,1)S(1)}, u32[]{:S(2)}, u32[]{:S(2)}) %collective-permute-start.18) | collective-permute-done | bytes 524320 | tf_op jit(solution)/shard_map/ppermute | solution.py:352
  81.8 1.5 %collective-permute-start.23 = (bf16[512,512]{1,0:T(8,128)(2,1)S(1)}, bf16[512,512]{1,0:T(8,128)(2,1)S(1)}, u32[]{:S(2)}, u32[]{:S(2)}) collective-permute-start(bf16[512,512]{1,0:T(8,128)(2,1)S(1)} %collective-permute-done.16.refs_6_), channel_id=1, source_target_pairs={{0,16},{16,0},{1,17},{17,1},{2,18},{18,2},{3,19},{19,3},{4,20},{20... | collective-permute-start | bytes 1572872 | tf_op jit(solution)/shard_map/ppermute | solution.py:352
  83.8 10.1 %collective-permute-done.21.hid_ref = bf16[2,128,1024]{2,1,0:T(8,128)(2,1)S(1)} collective-permute-done((bf16[2,128,1024]{2,1,0:T(8,128)(2,1)S(1)}, bf16[2,128,1024]{2,1,0:T(8,128)(2,1)S(1)}, u32[]{:S(2)}, u32[]{:S(2)}) %collective-permute-start.21) | collective-permute-done | bytes 524320 | tf_op jit(solution)/shard_map/ppermute | solution.py:352
  95.7 1.5 %collective-permute-start.33 = (bf16[1024,512]{1,0:T(8,128)(2,1)S(1)}, bf16[1024,512]{1,0:T(8,128)(2,1)S(1)}, u32[]{:S(2)}, u32[]{:S(2)}) collective-permute-start(bf16[1024,512]{1,0:T(8,128)(2,1)S(1)} %pad_maximum_fusion.refs_10_), channel_id=1, source_target_pairs={{0,8},{4,12},{8,0},{12,4},{1,9},{5,13},{9,1},{13,5},{2,10},{6,14},... | collective-permute-start | bytes 3145736 | tf_op jit(solution)/shard_map/ppermute | solution.py:352
  97.2 13.3 %collective-permute-done.26.got_ref = bf16[128,1024]{1,0:T(8,128)(2,1)S(1)} collective-permute-done((bf16[128,1024]{1,0:T(8,128)(2,1)S(1)}, bf16[128,1024]{1,0:T(8,128)(2,1)S(1)}, u32[]{:S(2)}, u32[]{:S(2)}) %collective-permute-start.26) | collective-permute-done | bytes 262176 | tf_op jit(solution)/shard_map/ppermute | solution.py:352
  111.4 1.8 %collective-permute-start.31 = (bf16[128,1024]{1,0:T(8,128)(2,1)}, bf16[128,1024]{1,0:T(8,128)(2,1)S(1)}, u32[]{:S(2)}, u32[]{:S(2)}) collective-permute-start(bf16[128,1024]{1,0:T(8,128)(2,1)} %sum_hid.1.refs_0_), channel_id=1, source_target_pairs={{0,2},{1,3},{2,0},{3,1},{4,6},{5,7},{6,4},{7,5},{8,10},{9,11},{10,... | collective-permute-start | bytes 786440 | tf_op jit(solution)/shard_map/ppermute | solution.py:352
  113.2 7.8 %collective-permute-done.33.refs_12_ = bf16[1024,512]{1,0:T(8,128)(2,1)S(1)} collective-permute-done((bf16[1024,512]{1,0:T(8,128)(2,1)S(1)}, bf16[1024,512]{1,0:T(8,128)(2,1)S(1)}, u32[]{:S(2)}, u32[]{:S(2)}) %collective-permute-start.33) | collective-permute-done | bytes 1048608 | tf_op jit(solution)/shard_map/ppermute | solution.py:352
  121.0 3.6 %collective-permute-done.30.refs_0_.refs_1_ = bf16[128,1024]{1,0:T(8,128)(2,1)S(1)} collective-permute-done((bf16[128,1024]{1,0:T(8,128)(2,1)}, bf16[128,1024]{1,0:T(8,128)(2,1)S(1)}, u32[]{:S(2)}, u32[]{:S(2)}) %collective-permute-start.30) | collective-permute-done | bytes 262176 | tf_op jit(solution)/shard_map/ppermute | solution.py:352
  124.5 2.4 %collective-permute-done.31.refs_0_.refs_2_ = bf16[128,1024]{1,0:T(8,128)(2,1)S(1)} collective-permute-done((bf16[128,1024]{1,0:T(8,128)(2,1)}, bf16[128,1024]{1,0:T(8,128)(2,1)S(1)}, u32[]{:S(2)}, u32[]{:S(2)}) %collective-permute-start.31) | collective-permute-done | bytes 262176 | tf_op jit(solution)/shard_map/ppermute | solution.py:352
  129.5 6.1 %collective-permute-done.34.refs_0_.refs_3_ = bf16[128,1024]{1,0:T(8,128)(2,1)S(1)} collective-permute-done((bf16[128,1024]{1,0:T(8,128)(2,1)S(1)}, bf16[128,1024]{1,0:T(8,128)(2,1)S(1)}, u32[]{:S(2)}, u32[]{:S(2)}) %collective-permute-start.34) | collective-permute-done | bytes 262176 | tf_op jit(solution)/shard_map/ppermute | solution.py:352
  135.9 6.2 %attend.1 = bf16[128,1024]{1,0:T(8,128)(2,1)} custom-call(s32[3]{0:T(128)S(1)} %pad_add_fusion.place_ref, bf16[128,1024]{1,0:T(8,128)(2,1)S(1)} %copy-done.2, bf16[128,1024]{1,0:T(8,128)(2,1)S(1)} %collective-permute-done.30.refs_0_.refs_1_, bf16[128,1024]{1,0:T(8,128)(2,1)S(1)} %collective-permute-done.31.refs_0_.refs_2_, ...), custom_call_target="tpu_custom_call" | custom-call | flops 1 | bytes 1 | tf_op jit(solution)/shard_map/attend/pallas_call | solution.py:333
  (93 shorter events, 22.2 us)
Async XLA Ops:
  0.7 15.2 %collective-permute-start = (bf16[128,1024]{1,0:T(8,128)(2,1)}, bf16[128,1024]{1,0:T(8,128)(2,1)}, u32[]{:S(2)}, u32[]{:S(2)}) collective-permute-start(bf16[128,1024]{1,0:T(8,128)(2,1)} %resid_ref.1), channel_id=1, source_target_pairs={{0,1},{1,0},{2,3},{3,2},{4,5},{5,4},{6,7},{7,6},{8,9},{9,8},{10,11... | collective-permute-start | bytes 786440 | tf_op jit(solution)/shard_map/ppermute | solution.py:352
  3.7 14.7 %collective-permute-start.1 = (bf16[128,1024]{1,0:T(8,128)(2,1)}, bf16[128,1024]{1,0:T(8,128)(2,1)}, u32[]{:S(2)}, u32[]{:S(2)}) collective-permute-start(bf16[128,1024]{1,0:T(8,128)(2,1)} %resid_ref.1), channel_id=1, source_target_pairs={{0,2},{1,3},{2,0},{3,1},{4,6},{5,7},{6,4},{7,5},{8,10},{9,11},{10,... | collective-permute-start | bytes 786440 | tf_op jit(solution)/shard_map/ppermute | solution.py:352
  12.4 17.8 %collective-permute-start.5 = (bf16[512,512]{1,0:T(8,128)(2,1)S(1)}, bf16[512,512]{1,0:T(8,128)(2,1)S(1)}, u32[]{:S(2)}, u32[]{:S(2)}) collective-permute-start(bf16[512,512]{1,0:T(8,128)(2,1)S(1)} %get-tuple-element.166), channel_id=1, source_target_pairs={{0,8},{4,12},{8,0},{12,4},{1,9},{5,13},{9,1},{13,5},{2,10},{6,14},... | collective-permute-start | bytes 1572872 | tf_op jit(solution)/shard_map/ppermute | solution.py:352
  19.6 16.7 %collective-permute-start.6 = (bf16[128,1152]{1,0:T(8,128)(2,1)}, bf16[128,1152]{1,0:T(8,128)(2,1)S(1)}, u32[]{:S(2)}, u32[]{:S(2)}) collective-permute-start(bf16[128,1152]{1,0:T(8,128)(2,1)} %pad_maximum_fusion.1.refs_0_.refs_12_), channel_id=1, source_target_pairs={{0,4},{4,0},{8,12},{12,8},{1,5},{5,1},{9,13},{13,9},{2,6},{6,2},{1... | collective-permute-start | bytes 884744 | tf_op jit(solution)/shard_map/ppermute | solution.py:352
  19.6 14.6 %collective-permute-start.4 = (bf16[128,1024]{1,0:T(8,128)(2,1)}, bf16[128,1024]{1,0:T(8,128)(2,1)}, u32[]{:S(2)}, u32[]{:S(2)}) collective-permute-start(bf16[128,1024]{1,0:T(8,128)(2,1)} %collective-permute-done.refs_1_), channel_id=1, source_target_pairs={{0,8},{4,12},{8,0},{12,4},{1,9},{5,13},{9,1},{13,5},{2,10},{6,14},... | collective-permute-start | bytes 786440 | tf_op jit(solution)/shard_map/ppermute | solution.py:352
  21.1 13.2 %collective-permute-start.8 = (bf16[128,1024]{1,0:T(8,128)(2,1)}, bf16[128,1024]{1,0:T(8,128)(2,1)S(1)}, u32[]{:S(2)}, u32[]{:S(2)}) collective-permute-start(bf16[128,1024]{1,0:T(8,128)(2,1)} %collective-permute-done.1.refs_2_), channel_id=1, source_target_pairs={{0,4},{4,0},{8,12},{12,8},{1,5},{5,1},{9,13},{13,9},{2,6},{6,2},{1... | collective-permute-start | bytes 786440 | tf_op jit(solution)/shard_map/ppermute | solution.py:352
  30.3 17.3 %collective-permute-start.10 = (bf16[128,1152]{1,0:T(8,128)(2,1)}, bf16[128,1152]{1,0:T(8,128)(2,1)S(1)}, u32[]{:S(2)}, u32[]{:S(2)}) collective-permute-start(bf16[128,1152]{1,0:T(8,128)(2,1)} %collective-permute-done.2.refs_0_.refs_12_), channel_id=1, source_target_pairs={{0,4},{4,0},{8,12},{12,8},{1,5},{5,1},{9,13},{13,9},{2,6},{6,2},{1... | collective-permute-start | bytes 884744 | tf_op jit(solution)/shard_map/ppermute | solution.py:352
  34.2 13.3 %collective-permute-start.12 = (bf16[128,1024]{1,0:T(8,128)(2,1)}, bf16[128,1024]{1,0:T(8,128)(2,1)}, u32[]{:S(2)}, u32[]{:S(2)}) collective-permute-start(bf16[128,1024]{1,0:T(8,128)(2,1)} %collective-permute-done.1.refs_2_), channel_id=1, source_target_pairs={{0,8},{4,12},{8,0},{12,4},{1,9},{5,13},{9,1},{13,5},{2,10},{6,14},... | collective-permute-start | bytes 786440 | tf_op jit(solution)/shard_map/ppermute | solution.py:352
  35.7 13.2 %collective-permute-start.13 = (bf16[128,1024]{1,0:T(8,128)(2,1)}, bf16[128,1024]{1,0:T(8,128)(2,1)}, u32[]{:S(2)}, u32[]{:S(2)}) collective-permute-start(bf16[128,1024]{1,0:T(8,128)(2,1)} %collective-permute-done.3.refs_3_), channel_id=1, source_target_pairs={{0,8},{4,12},{8,0},{12,4},{1,9},{5,13},{9,1},{13,5},{2,10},{6,14},... | collective-permute-start | bytes 786440 | tf_op jit(solution)/shard_map/ppermute | solution.py:352
  36.3 12.6 %collective-permute-start.11 = (bf16[128,1024]{1,0:T(8,128)(2,1)}, bf16[128,1024]{1,0:T(8,128)(2,1)S(1)}, u32[]{:S(2)}, u32[]{:S(2)}) collective-permute-start(bf16[128,1024]{1,0:T(8,128)(2,1)} %collective-permute-done.4.refs_1_), channel_id=1, source_target_pairs={{0,4},{4,0},{8,12},{12,8},{1,5},{5,1},{9,13},{13,9},{2,6},{6,2},{1... | collective-permute-start | bytes 786440 | tf_op jit(solution)/shard_map/ppermute | solution.py:352
  48.9 14.8 %collective-permute-start.16 = (bf16[512,512]{1,0:T(8,128)(2,1)S(1)}, bf16[512,512]{1,0:T(8,128)(2,1)S(1)}, u32[]{:S(2)}, u32[]{:S(2)}) collective-permute-start(bf16[512,512]{1,0:T(8,128)(2,1)S(1)} %copy-done.4), channel_id=1, source_target_pairs={{0,8},{4,12},{8,0},{12,4},{1,9},{5,13},{9,1},{13,5},{2,10},{6,14},... | collective-permute-start | bytes 1572872 | tf_op jit(solution)/shard_map/ppermute | solution.py:352
  63.9 14.3 %collective-permute-start.19 = (bf16[4,128,1024]{2,1,0:T(8,128)(2,1)S(1)}, bf16[4,128,1024]{2,1,0:T(8,128)(2,1)S(1)}, u32[]{:S(2)}, u32[]{:S(2)}) collective-permute-start(bf16[4,128,1024]{2,1,0:T(8,128)(2,1)S(1)} %get-tuple-element.106), channel_id=1, source_target_pairs={{0,4},{4,0},{8,12},{12,8},{1,5},{5,1},{9,13},{13,9},{2,6},{6,2},{1... | collective-permute-start | bytes 3145736 | tf_op jit(solution)/shard_map/ppermute | solution.py:352
  64.2 14.0 %collective-permute-start.20 = (bf16[512,512]{1,0:T(8,128)(2,1)S(1)}, bf16[512,512]{1,0:T(8,128)(2,1)S(1)}, u32[]{:S(2)}, u32[]{:S(2)}) collective-permute-start(bf16[512,512]{1,0:T(8,128)(2,1)S(1)} %collective-permute-done.5.refs_2_), channel_id=1, source_target_pairs={{0,16},{16,0},{1,17},{17,1},{2,18},{18,2},{3,19},{19,3},{4,20},{20... | collective-permute-start | bytes 1572872 | tf_op jit(solution)/shard_map/ppermute | solution.py:352
  66.6 14.0 %collective-permute-start.18 = (bf16[2,128,1024]{2,1,0:T(8,128)(2,1)S(1)}, bf16[2,128,1024]{2,1,0:T(8,128)(2,1)S(1)}, u32[]{:S(2)}, u32[]{:S(2)}) collective-permute-start(bf16[2,128,1024]{2,1,0:T(8,128)(2,1)S(1)} %get-tuple-element.105), channel_id=1, source_target_pairs={{0,8},{4,12},{8,0},{12,4},{1,9},{5,13},{9,1},{13,5},{2,10},{6,14},... | collective-permute-start | bytes 1572872 | tf_op jit(solution)/shard_map/ppermute | solution.py:352
  80.8 13.2 %collective-permute-start.21 = (bf16[2,128,1024]{2,1,0:T(8,128)(2,1)S(1)}, bf16[2,128,1024]{2,1,0:T(8,128)(2,1)S(1)}, u32[]{:S(2)}, u32[]{:S(2)}) collective-permute-start(bf16[2,128,1024]{2,1,0:T(8,128)(2,1)S(1)} %sum_chip.1), channel_id=1, source_target_pairs={{0,1},{1,0},{2,3},{3,2},{4,5},{5,4},{6,7},{7,6},{8,9},{9,8},{10,11... | collective-permute-start | bytes 1572872 | tf_op jit(solution)/shard_map/ppermute | solution.py:352
  81.3 12.9 %collective-permute-start.22 = (bf16[2,128,1024]{2,1,0:T(8,128)(2,1)S(1)}, bf16[2,128,1024]{2,1,0:T(8,128)(2,1)S(1)}, u32[]{:S(2)}, u32[]{:S(2)}) collective-permute-start(bf16[2,128,1024]{2,1,0:T(8,128)(2,1)S(1)} %get-tuple-element.112), channel_id=1, source_target_pairs={{0,8},{4,12},{8,0},{12,4},{1,9},{5,13},{9,1},{13,5},{2,10},{6,14},... | collective-permute-start | bytes 1572872 | tf_op jit(solution)/shard_map/ppermute | solution.py:352
  94.4 16.2 %collective-permute-start.27 = (bf16[1024,1024]{1,0:T(8,128)(2,1)S(1)}, bf16[1024,1024]{1,0:T(8,128)(2,1)S(1)}, u32[]{:S(2)}, u32[]{:S(2)}) collective-permute-start(bf16[1024,1024]{1,0:T(8,128)(2,1)S(1)} %copy-done), channel_id=1, source_target_pairs={{0,4},{4,0},{8,12},{12,8},{1,5},{5,1},{9,13},{13,9},{2,6},{6,2},{1... | collective-permute-start | bytes 6291464 | tf_op jit(solution)/shard_map/ppermute | solution.py:352
  94.5 16.1 %collective-permute-start.28 = (bf16[512,512]{1,0:T(8,128)(2,1)S(1)}, bf16[512,512]{1,0:T(8,128)(2,1)S(1)}, u32[]{:S(2)}, u32[]{:S(2)}) collective-permute-start(bf16[512,512]{1,0:T(8,128)(2,1)S(1)} %collective-permute-done.16.refs_6_), channel_id=1, source_target_pairs={{0,4},{4,0},{8,12},{12,8},{1,5},{5,1},{9,13},{13,9},{2,6},{6,2},{1... | collective-permute-start | bytes 1572872 | tf_op jit(solution)/shard_map/ppermute | solution.py:352
  95.0 15.6 %collective-permute-start.29 = (bf16[512,512]{1,0:T(8,128)(2,1)S(1)}, bf16[512,512]{1,0:T(8,128)(2,1)S(1)}, u32[]{:S(2)}, u32[]{:S(2)}) collective-permute-start(bf16[512,512]{1,0:T(8,128)(2,1)S(1)} %collective-permute-done.23.refs_7_), channel_id=1, source_target_pairs={{0,4},{4,0},{8,12},{12,8},{1,5},{5,1},{9,13},{13,9},{2,6},{6,2},{1... | collective-permute-start | bytes 1572872 | tf_op jit(solution)/shard_map/ppermute | solution.py:352
  95.3 15.2 %collective-permute-start.26 = (bf16[128,1024]{1,0:T(8,128)(2,1)S(1)}, bf16[128,1024]{1,0:T(8,128)(2,1)S(1)}, u32[]{:S(2)}, u32[]{:S(2)}) collective-permute-start(bf16[128,1024]{1,0:T(8,128)(2,1)S(1)} %get-tuple-element.121), channel_id=1, source_target_pairs={{0,2},{1,3},{2,0},{3,1},{4,6},{5,7},{6,4},{7,5},{8,10},{9,11},{10,... | collective-permute-start | bytes 786440 | tf_op jit(solution)/shard_map/ppermute | solution.py:352
  95.7 25.3 %collective-permute-start.33 = (bf16[1024,512]{1,0:T(8,128)(2,1)S(1)}, bf16[1024,512]{1,0:T(8,128)(2,1)S(1)}, u32[]{:S(2)}, u32[]{:S(2)}) collective-permute-start(bf16[1024,512]{1,0:T(8,128)(2,1)S(1)} %pad_maximum_fusion.refs_10_), channel_id=1, source_target_pairs={{0,8},{4,12},{8,0},{12,4},{1,9},{5,13},{9,1},{13,5},{2,10},{6,14},... | collective-permute-start | bytes 3145736 | tf_op jit(solution)/shard_map/ppermute | solution.py:352
  110.6 16.3 %collective-permute-start.32 = (bf16[1024,512]{1,0:T(8,128)(2,1)S(1)}, bf16[1024,512]{1,0:T(8,128)(2,1)S(1)}, u32[]{:S(2)}, u32[]{:S(2)}) collective-permute-start(bf16[1024,512]{1,0:T(8,128)(2,1)S(1)} %pad_maximum_fusion.refs_10_), channel_id=1, source_target_pairs={{0,4},{4,0},{8,12},{12,8},{1,5},{5,1},{9,13},{13,9},{2,6},{6,2},{1... | collective-permute-start | bytes 3145736 | tf_op jit(solution)/shard_map/ppermute | solution.py:352
  111.4 13.1 %collective-permute-start.30 = (bf16[128,1024]{1,0:T(8,128)(2,1)}, bf16[128,1024]{1,0:T(8,128)(2,1)S(1)}, u32[]{:S(2)}, u32[]{:S(2)}) collective-permute-start(bf16[128,1024]{1,0:T(8,128)(2,1)} %sum_hid.1.refs_0_), channel_id=1, source_target_pairs={{0,1},{1,0},{2,3},{3,2},{4,5},{5,4},{6,7},{7,6},{8,9},{9,8},{10,11... | collective-permute-start | bytes 786440 | tf_op jit(solution)/shard_map/ppermute | solution.py:352
  111.4 15.5 %collective-permute-start.31 = (bf16[128,1024]{1,0:T(8,128)(2,1)}, bf16[128,1024]{1,0:T(8,128)(2,1)S(1)}, u32[]{:S(2)}, u32[]{:S(2)}) collective-permute-start(bf16[128,1024]{1,0:T(8,128)(2,1)} %sum_hid.1.refs_0_), channel_id=1, source_target_pairs={{0,2},{1,3},{2,0},{3,1},{4,6},{5,7},{6,4},{7,5},{8,10},{9,11},{10,... | collective-permute-start | bytes 786440 | tf_op jit(solution)/shard_map/ppermute | solution.py:352
  (21 other events, 234.8 us)

commit v5 on v4

--- a/solution.py
+++ b/solution.py
@@ -459,8 +459,9 @@
     (new_local,) = sums_call(last_body, [own, send], [(one, BF16)], "sum_hid")
 
     kv_near = over_core(w_kv)
-    rows = [new_local, over_hid(new_local, 1), over_hid(new_local, 2), None]
-    rows[1], rows[2], kv_near, kv_far = tie(rows[1], rows[2], kv_near, kv_far)
+    second = over_hid(new_local, 2)
+    rows = [new_local, over_hid(new_local, 1), second, None]
+    rows[2], rows[1], kv_near, kv_far = tie(rows[2], rows[1], kv_near, kv_far)
     rows[3] = over_hid(rows[2], 1)
     moved = [(here[c], there[c], here_core[c], there_core[c]) for c in range(2)]
     proj = [w_q, q_near, *moved[0], *moved[1], w_kv, kv_near, kv_far]

time: 142 us -> 142 us (level)
  no operation moved by 1% of the time
where the time goes in v5:
time: 142 us; the launch traced here: 141 us
  waiting for transfers between devices  76 us (54%)
  Pallas kernels  31.7 us (22%)
  starting transfers between devices  24.9 us (18%)
  other arithmetic  4.49 us (3%)
  local copies, waits for them, and re-layouts  3.08 us (2%)
    ppermute x36, waiting for transfers between devices, swap(): return lax.ppermute(value, axis, [(i, i ^ by) for i in range(size)])  76 us
    ppermute x36, starting transfers between devices, swap(): return lax.ppermute(value, axis, [(i, i ^ by) for i in range(size)])  24.9 us
    pallas_call x2, Pallas kernels, expert_call(): pl.pallas_call(expert_body, grid=(1,), in_specs=[SMEM] + held + [whole(ga...  22.3 us
    pallas_call x1, Pallas kernels, attend_call(): pl.pallas_call(attend_body, grid=(1,), in_specs=[SMEM] + [whole(v.shape)...  6.17 us
  transfers between devices with their start and end apart: 36, of which 19 were waited for; matrix products, arithmetic and copies ran while one was open for 5% of the time, Pallas kernels for 18%

profile of v5, /device:TPU:0, one launch (start us, length us, event | category | flops | bytes accessed | tf_op | source)
XLA Modules:
  0.0 141.2 jit_solution(2217440299600359369)
XLA Ops:
  0.7 3.1 %collective-permute-start = (bf16[128,1024]{1,0:T(8,128)(2,1)}, bf16[128,1024]{1,0:T(8,128)(2,1)}, u32[]{:S(2)}, u32[]{:S(2)}) collective-permute-start(bf16[128,1024]{1,0:T(8,128)(2,1)} %resid_ref.1), channel_id=1, source_target_pairs={{0,1},{1,0},{2,3},{3,2},{4,5},{5,4},{6,7},{7,6},{8,9},{9,8},{10,11... | collective-permute-start | bytes 786440 | tf_op jit(solution)/shard_map/ppermute | solution.py:352
  3.7 2.6 %collective-permute-start.1 = (bf16[128,1024]{1,0:T(8,128)(2,1)}, bf16[128,1024]{1,0:T(8,128)(2,1)}, u32[]{:S(2)}, u32[]{:S(2)}) collective-permute-start(bf16[128,1024]{1,0:T(8,128)(2,1)} %resid_ref.1), channel_id=1, source_target_pairs={{0,2},{1,3},{2,0},{3,1},{4,6},{5,7},{6,4},{7,5},{8,10},{9,11},{10,... | collective-permute-start | bytes 786440 | tf_op jit(solution)/shard_map/ppermute | solution.py:352
  7.2 1.7 %pad_maximum_fusion.1.refs_0_.refs_12_ = bf16[128,1152]{1,0:T(8,128)(2,1)} fusion(bf16[128,128]{1,0:T(8,128)(2,1)S(1)} %convert_element_type.13, bf16[128,1024]{1,0:T(8,128)(2,1)} %resid_ref.1), kind=kLoop, calls=%fused_computation.1 | loop fusion | flops 589824 | bytes 589824 | tf_op jit(solution)/shard_map/concatenate | solution.py:406
  8.9 1.5 %collective-permute-start.2 = (bf16[128,1152]{1,0:T(8,128)(2,1)}, bf16[128,1152]{1,0:T(8,128)(2,1)}, u32[]{:S(2)}, u32[]{:S(2)}) collective-permute-start(bf16[128,1152]{1,0:T(8,128)(2,1)} %pad_maximum_fusion.1.refs_0_.refs_12_), channel_id=1, source_target_pairs={{0,8},{4,12},{8,0},{12,4},{1,9},{5,13},{9,1},{13,5},{2,10},{6,14},... | collective-permute-start | bytes 884744 | tf_op jit(solution)/shard_map/ppermute | solution.py:352
  10.4 2.1 %constant_dynamic-slice_fusion.1 = (bf16[512,512]{1,0:T(8,128)(2,1)S(1)}, bf16[512,512]{1,0:T(8,128)(2,1)}) fusion(bf16[1024,1024]{1,0:T(8,128)(2,1)} %refs_0_, s32[]{:T(128)S(6)} %select_n.13), kind=kLoop, calls=%fused_computation.19 | loop fusion | bytes 2097156 | tf_op jit(solution)/shard_map/dynamic_slice | solution.py:396
  15.9 2.5 %collective-permute-done.1.refs_2_ = bf16[128,1024]{1,0:T(8,128)(2,1)} collective-permute-done((bf16[128,1024]{1,0:T(8,128)(2,1)}, bf16[128,1024]{1,0:T(8,128)(2,1)}, u32[]{:S(2)}, u32[]{:S(2)}) %collective-permute-start.1) | collective-permute-done | bytes 262176 | tf_op jit(solution)/shard_map/ppermute | solution.py:352
  21.3 9.0 %collective-permute-done.5.refs_2_ = bf16[512,512]{1,0:T(8,128)(2,1)S(1)} collective-permute-done((bf16[512,512]{1,0:T(8,128)(2,1)S(1)}, bf16[512,512]{1,0:T(8,128)(2,1)S(1)}, u32[]{:S(2)}, u32[]{:S(2)}) %collective-permute-start.5) | collective-permute-done | bytes 524320 | tf_op jit(solution)/shard_map/ppermute | solution.py:352
  30.8 3.4 %collective-permute-done.4.refs_1_ = bf16[128,1024]{1,0:T(8,128)(2,1)} collective-permute-done((bf16[128,1024]{1,0:T(8,128)(2,1)}, bf16[128,1024]{1,0:T(8,128)(2,1)}, u32[]{:S(2)}, u32[]{:S(2)}) %collective-permute-start.4) | collective-permute-done | bytes 262176 | tf_op jit(solution)/shard_map/ppermute | solution.py:352
  34.2 1.5 %collective-permute-start.12 = (bf16[128,1024]{1,0:T(8,128)(2,1)}, bf16[128,1024]{1,0:T(8,128)(2,1)}, u32[]{:S(2)}, u32[]{:S(2)}) collective-permute-start(bf16[128,1024]{1,0:T(8,128)(2,1)} %collective-permute-done.1.refs_2_), channel_id=1, source_target_pairs={{0,8},{4,12},{8,0},{12,4},{1,9},{5,13},{9,1},{13,5},{2,10},{6,14},... | collective-permute-start | bytes 786440 | tf_op jit(solution)/shard_map/ppermute | solution.py:352
  36.4 11.2 %near.1 = (f32[4,128,1024]{2,1,0:T(8,128)S(1)}, bf16[4,128,1024]{2,1,0:T(8,128)(2,1)S(1)}) custom-call(s32[3]{0:T(128)S(1)} %pad_add_fusion.place_ref, bf16[128,1152]{1,0:T(8,128)(2,1)} %pad_maximum_fusion.1.refs_0_.refs_12_, bf16[128,1024]{1,0:T(8,128)(2,1)} %collective-permute-done.refs_1_, bf16[128,1024]{1,0:T(8,128)(2,1)} %collective-permute-done.1.refs_2_, ...), custom_call_target="tpu_custom_call" | custom-call | flops 1 | bytes 1 | tf_op jit(solution)/shard_map/near/pallas_call | solution.py:179
  48.9 1.5 %collective-permute-start.16 = (bf16[512,512]{1,0:T(8,128)(2,1)S(1)}, bf16[512,512]{1,0:T(8,128)(2,1)S(1)}, u32[]{:S(2)}, u32[]{:S(2)}) collective-permute-start(bf16[512,512]{1,0:T(8,128)(2,1)S(1)} %copy-done.4), channel_id=1, source_target_pairs={{0,8},{4,12},{8,0},{12,4},{1,9},{5,13},{9,1},{13,5},{2,10},{6,14},... | collective-permute-start | bytes 1572872 | tf_op jit(solution)/shard_map/ppermute | solution.py:352
  52.5 11.1 %far.1 = (f32[4,128,1024]{2,1,0:T(8,128)S(1)}, bf16[4,128,1024]{2,1,0:T(8,128)(2,1)S(1)}) custom-call(s32[3]{0:T(128)S(1)} %pad_add_fusion.place_ref, bf16[128,1152]{1,0:T(8,128)(2,1)} %collective-permute-done.2.refs_0_.refs_12_, bf16[128,1024]{1,0:T(8,128)(2,1)} %collective-permute-done.4.refs_1_, bf16[128,1024]{1,0:T(8,128)(2,1)} %collective-permute-done.12.refs_2_, ...), custom_call_target="tpu_custom_call" | custom-call | flops 1 | bytes 1 | tf_op jit(solution)/shard_map/far/pallas_call | solution.py:179
  64.2 1.5 %collective-permute-start.20 = (bf16[512,512]{1,0:T(8,128)(2,1)S(1)}, bf16[512,512]{1,0:T(8,128)(2,1)S(1)}, u32[]{:S(2)}, u32[]{:S(2)}) collective-permute-start(bf16[512,512]{1,0:T(8,128)(2,1)S(1)} %collective-permute-done.5.refs_2_), channel_id=1, source_target_pairs={{0,16},{16,0},{1,17},{17,1},{2,18},{18,2},{3,19},{19,3},{4,20},{20... | collective-permute-start | bytes 1572872 | tf_op jit(solution)/shard_map/ppermute | solution.py:352
  67.2 11.0 %collective-permute-done.20.refs_3_ = bf16[512,512]{1,0:T(8,128)(2,1)S(1)} collective-permute-done((bf16[512,512]{1,0:T(8,128)(2,1)S(1)}, bf16[512,512]{1,0:T(8,128)(2,1)S(1)}, u32[]{:S(2)}, u32[]{:S(2)}) %collective-permute-start.20) | collective-permute-done | bytes 524320 | tf_op jit(solution)/shard_map/ppermute | solution.py:352
  78.2 2.4 %collective-permute-done.18.far_ref = bf16[2,128,1024]{2,1,0:T(8,128)(2,1)S(1)} collective-permute-done((bf16[2,128,1024]{2,1,0:T(8,128)(2,1)S(1)}, bf16[2,128,1024]{2,1,0:T(8,128)(2,1)S(1)}, u32[]{:S(2)}, u32[]{:S(2)}) %collective-permute-start.18) | collective-permute-done | bytes 524320 | tf_op jit(solution)/shard_map/ppermute | solution.py:352
  81.8 1.5 %collective-permute-start.23 = (bf16[512,512]{1,0:T(8,128)(2,1)S(1)}, bf16[512,512]{1,0:T(8,128)(2,1)S(1)}, u32[]{:S(2)}, u32[]{:S(2)}) collective-permute-start(bf16[512,512]{1,0:T(8,128)(2,1)S(1)} %collective-permute-done.16.refs_6_), channel_id=1, source_target_pairs={{0,16},{16,0},{1,17},{17,1},{2,18},{18,2},{3,19},{19,3},{4,20},{20... | collective-permute-start | bytes 1572872 | tf_op jit(solution)/shard_map/ppermute | solution.py:352
  83.8 10.1 %collective-permute-done.21.hid_ref = bf16[2,128,1024]{2,1,0:T(8,128)(2,1)S(1)} collective-permute-done((bf16[2,128,1024]{2,1,0:T(8,128)(2,1)S(1)}, bf16[2,128,1024]{2,1,0:T(8,128)(2,1)S(1)}, u32[]{:S(2)}, u32[]{:S(2)}) %collective-permute-start.21) | collective-permute-done | bytes 524320 | tf_op jit(solution)/shard_map/ppermute | solution.py:352
  95.7 1.5 %collective-permute-start.33 = (bf16[1024,512]{1,0:T(8,128)(2,1)S(1)}, bf16[1024,512]{1,0:T(8,128)(2,1)S(1)}, u32[]{:S(2)}, u32[]{:S(2)}) collective-permute-start(bf16[1024,512]{1,0:T(8,128)(2,1)S(1)} %pad_maximum_fusion.refs_10_), channel_id=1, source_target_pairs={{0,8},{4,12},{8,0},{12,4},{1,9},{5,13},{9,1},{13,5},{2,10},{6,14},... | collective-permute-start | bytes 3145736 | tf_op jit(solution)/shard_map/ppermute | solution.py:352
  97.2 13.3 %collective-permute-done.26.got_ref = bf16[128,1024]{1,0:T(8,128)(2,1)S(1)} collective-permute-done((bf16[128,1024]{1,0:T(8,128)(2,1)S(1)}, bf16[128,1024]{1,0:T(8,128)(2,1)S(1)}, u32[]{:S(2)}, u32[]{:S(2)}) %collective-permute-start.26) | collective-permute-done | bytes 262176 | tf_op jit(solution)/shard_map/ppermute | solution.py:352
  111.4 1.8 %collective-permute-start.31 = (bf16[128,1024]{1,0:T(8,128)(2,1)}, bf16[128,1024]{1,0:T(8,128)(2,1)S(1)}, u32[]{:S(2)}, u32[]{:S(2)}) collective-permute-start(bf16[128,1024]{1,0:T(8,128)(2,1)} %sum_hid.1.refs_0_), channel_id=1, source_target_pairs={{0,1},{1,0},{2,3},{3,2},{4,5},{5,4},{6,7},{7,6},{8,9},{9,8},{10,11... | collective-permute-start | bytes 786440 | tf_op jit(solution)/shard_map/ppermute | solution.py:352
  113.2 7.8 %collective-permute-done.33.refs_12_ = bf16[1024,512]{1,0:T(8,128)(2,1)S(1)} collective-permute-done((bf16[1024,512]{1,0:T(8,128)(2,1)S(1)}, bf16[1024,512]{1,0:T(8,128)(2,1)S(1)}, u32[]{:S(2)}, u32[]{:S(2)}) %collective-permute-start.33) | collective-permute-done | bytes 1048608 | tf_op jit(solution)/shard_map/ppermute | solution.py:352
  121.0 4.5 %collective-permute-done.30.refs_0_.refs_2_ = bf16[128,1024]{1,0:T(8,128)(2,1)S(1)} collective-permute-done((bf16[128,1024]{1,0:T(8,128)(2,1)}, bf16[128,1024]{1,0:T(8,128)(2,1)S(1)}, u32[]{:S(2)}, u32[]{:S(2)}) %collective-permute-start.30) | collective-permute-done | bytes 262176 | tf_op jit(solution)/shard_map/ppermute | solution.py:352
  128.9 5.8 %collective-permute-done.34.refs_0_.refs_3_ = bf16[128,1024]{1,0:T(8,128)(2,1)S(1)} collective-permute-done((bf16[128,1024]{1,0:T(8,128)(2,1)S(1)}, bf16[128,1024]{1,0:T(8,128)(2,1)S(1)}, u32[]{:S(2)}, u32[]{:S(2)}) %collective-permute-start.34) | collective-permute-done | bytes 262176 | tf_op jit(solution)/shard_map/ppermute | solution.py:352
  134.9 6.2 %attend.1 = bf16[128,1024]{1,0:T(8,128)(2,1)} custom-call(s32[3]{0:T(128)S(1)} %pad_add_fusion.place_ref, bf16[128,1024]{1,0:T(8,128)(2,1)S(1)} %copy-done.2, bf16[128,1024]{1,0:T(8,128)(2,1)S(1)} %collective-permute-done.31.refs_0_.refs_1_, bf16[128,1024]{1,0:T(8,128)(2,1)S(1)} %collective-permute-done.30.refs_0_.refs_2_, ...), custom_call_target="tpu_custom_call" | custom-call | flops 1 | bytes 1 | tf_op jit(solution)/shard_map/attend/pallas_call | solution.py:333
  (93 shorter events, 21.5 us)
Async XLA Ops:
  0.7 15.2 %collective-permute-start = (bf16[128,1024]{1,0:T(8,128)(2,1)}, bf16[128,1024]{1,0:T(8,128)(2,1)}, u32[]{:S(2)}, u32[]{:S(2)}) collective-permute-start(bf16[128,1024]{1,0:T(8,128)(2,1)} %resid_ref.1), channel_id=1, source_target_pairs={{0,1},{1,0},{2,3},{3,2},{4,5},{5,4},{6,7},{7,6},{8,9},{9,8},{10,11... | collective-permute-start | bytes 786440 | tf_op jit(solution)/shard_map/ppermute | solution.py:352
  3.7 14.7 %collective-permute-start.1 = (bf16[128,1024]{1,0:T(8,128)(2,1)}, bf16[128,1024]{1,0:T(8,128)(2,1)}, u32[]{:S(2)}, u32[]{:S(2)}) collective-permute-start(bf16[128,1024]{1,0:T(8,128)(2,1)} %resid_ref.1), channel_id=1, source_target_pairs={{0,2},{1,3},{2,0},{3,1},{4,6},{5,7},{6,4},{7,5},{8,10},{9,11},{10,... | collective-permute-start | bytes 786440 | tf_op jit(solution)/shard_map/ppermute | solution.py:352
  12.4 17.8 %collective-permute-start.5 = (bf16[512,512]{1,0:T(8,128)(2,1)S(1)}, bf16[512,512]{1,0:T(8,128)(2,1)S(1)}, u32[]{:S(2)}, u32[]{:S(2)}) collective-permute-start(bf16[512,512]{1,0:T(8,128)(2,1)S(1)} %get-tuple-element.166), channel_id=1, source_target_pairs={{0,8},{4,12},{8,0},{12,4},{1,9},{5,13},{9,1},{13,5},{2,10},{6,14},... | collective-permute-start | bytes 1572872 | tf_op jit(solution)/shard_map/ppermute | solution.py:352
  19.6 16.7 %collective-permute-start.6 = (bf16[128,1152]{1,0:T(8,128)(2,1)}, bf16[128,1152]{1,0:T(8,128)(2,1)S(1)}, u32[]{:S(2)}, u32[]{:S(2)}) collective-permute-start(bf16[128,1152]{1,0:T(8,128)(2,1)} %pad_maximum_fusion.1.refs_0_.refs_12_), channel_id=1, source_target_pairs={{0,4},{4,0},{8,12},{12,8},{1,5},{5,1},{9,13},{13,9},{2,6},{6,2},{1... | collective-permute-start | bytes 884744 | tf_op jit(solution)/shard_map/ppermute | solution.py:352
  19.6 14.6 %collective-permute-start.4 = (bf16[128,1024]{1,0:T(8,128)(2,1)}, bf16[128,1024]{1,0:T(8,128)(2,1)}, u32[]{:S(2)}, u32[]{:S(2)}) collective-permute-start(bf16[128,1024]{1,0:T(8,128)(2,1)} %collective-permute-done.refs_1_), channel_id=1, source_target_pairs={{0,8},{4,12},{8,0},{12,4},{1,9},{5,13},{9,1},{13,5},{2,10},{6,14},... | collective-permute-start | bytes 786440 | tf_op jit(solution)/shard_map/ppermute | solution.py:352
  21.1 13.2 %collective-permute-start.8 = (bf16[128,1024]{1,0:T(8,128)(2,1)}, bf16[128,1024]{1,0:T(8,128)(2,1)S(1)}, u32[]{:S(2)}, u32[]{:S(2)}) collective-permute-start(bf16[128,1024]{1,0:T(8,128)(2,1)} %collective-permute-done.1.refs_2_), channel_id=1, source_target_pairs={{0,4},{4,0},{8,12},{12,8},{1,5},{5,1},{9,13},{13,9},{2,6},{6,2},{1... | collective-permute-start | bytes 786440 | tf_op jit(solution)/shard_map/ppermute | solution.py:352
  30.3 17.3 %collective-permute-start.10 = (bf16[128,1152]{1,0:T(8,128)(2,1)}, bf16[128,1152]{1,0:T(8,128)(2,1)S(1)}, u32[]{:S(2)}, u32[]{:S(2)}) collective-permute-start(bf16[128,1152]{1,0:T(8,128)(2,1)} %collective-permute-done.2.refs_0_.refs_12_), channel_id=1, source_target_pairs={{0,4},{4,0},{8,12},{12,8},{1,5},{5,1},{9,13},{13,9},{2,6},{6,2},{1... | collective-permute-start | bytes 884744 | tf_op jit(solution)/shard_map/ppermute | solution.py:352
  34.2 13.3 %collective-permute-start.12 = (bf16[128,1024]{1,0:T(8,128)(2,1)}, bf16[128,1024]{1,0:T(8,128)(2,1)}, u32[]{:S(2)}, u32[]{:S(2)}) collective-permute-start(bf16[128,1024]{1,0:T(8,128)(2,1)} %collective-permute-done.1.refs_2_), channel_id=1, source_target_pairs={{0,8},{4,12},{8,0},{12,4},{1,9},{5,13},{9,1},{13,5},{2,10},{6,14},... | collective-permute-start | bytes 786440 | tf_op jit(solution)/shard_map/ppermute | solution.py:352
  35.7 13.2 %collective-permute-start.13 = (bf16[128,1024]{1,0:T(8,128)(2,1)}, bf16[128,1024]{1,0:T(8,128)(2,1)}, u32[]{:S(2)}, u32[]{:S(2)}) collective-permute-start(bf16[128,1024]{1,0:T(8,128)(2,1)} %collective-permute-done.3.refs_3_), channel_id=1, source_target_pairs={{0,8},{4,12},{8,0},{12,4},{1,9},{5,13},{9,1},{13,5},{2,10},{6,14},... | collective-permute-start | bytes 786440 | tf_op jit(solution)/shard_map/ppermute | solution.py:352
  36.3 12.6 %collective-permute-start.11 = (bf16[128,1024]{1,0:T(8,128)(2,1)}, bf16[128,1024]{1,0:T(8,128)(2,1)S(1)}, u32[]{:S(2)}, u32[]{:S(2)}) collective-permute-start(bf16[128,1024]{1,0:T(8,128)(2,1)} %collective-permute-done.4.refs_1_), channel_id=1, source_target_pairs={{0,4},{4,0},{8,12},{12,8},{1,5},{5,1},{9,13},{13,9},{2,6},{6,2},{1... | collective-permute-start | bytes 786440 | tf_op jit(solution)/shard_map/ppermute | solution.py:352
  48.9 14.8 %collective-permute-start.16 = (bf16[512,512]{1,0:T(8,128)(2,1)S(1)}, bf16[512,512]{1,0:T(8,128)(2,1)S(1)}, u32[]{:S(2)}, u32[]{:S(2)}) collective-permute-start(bf16[512,512]{1,0:T(8,128)(2,1)S(1)} %copy-done.4), channel_id=1, source_target_pairs={{0,8},{4,12},{8,0},{12,4},{1,9},{5,13},{9,1},{13,5},{2,10},{6,14},... | collective-permute-start | bytes 1572872 | tf_op jit(solution)/shard_map/ppermute | solution.py:352
  63.9 14.3 %collective-permute-start.19 = (bf16[4,128,1024]{2,1,0:T(8,128)(2,1)S(1)}, bf16[4,128,1024]{2,1,0:T(8,128)(2,1)S(1)}, u32[]{:S(2)}, u32[]{:S(2)}) collective-permute-start(bf16[4,128,1024]{2,1,0:T(8,128)(2,1)S(1)} %get-tuple-element.106), channel_id=1, source_target_pairs={{0,4},{4,0},{8,12},{12,8},{1,5},{5,1},{9,13},{13,9},{2,6},{6,2},{1... | collective-permute-start | bytes 3145736 | tf_op jit(solution)/shard_map/ppermute | solution.py:352
  64.2 14.0 %collective-permute-start.20 = (bf16[512,512]{1,0:T(8,128)(2,1)S(1)}, bf16[512,512]{1,0:T(8,128)(2,1)S(1)}, u32[]{:S(2)}, u32[]{:S(2)}) collective-permute-start(bf16[512,512]{1,0:T(8,128)(2,1)S(1)} %collective-permute-done.5.refs_2_), channel_id=1, source_target_pairs={{0,16},{16,0},{1,17},{17,1},{2,18},{18,2},{3,19},{19,3},{4,20},{20... | collective-permute-start | bytes 1572872 | tf_op jit(solution)/shard_map/ppermute | solution.py:352
  66.6 14.0 %collective-permute-start.18 = (bf16[2,128,1024]{2,1,0:T(8,128)(2,1)S(1)}, bf16[2,128,1024]{2,1,0:T(8,128)(2,1)S(1)}, u32[]{:S(2)}, u32[]{:S(2)}) collective-permute-start(bf16[2,128,1024]{2,1,0:T(8,128)(2,1)S(1)} %get-tuple-element.105), channel_id=1, source_target_pairs={{0,8},{4,12},{8,0},{12,4},{1,9},{5,13},{9,1},{13,5},{2,10},{6,14},... | collective-permute-start | bytes 1572872 | tf_op jit(solution)/shard_map/ppermute | solution.py:352
  80.8 13.2 %collective-permute-start.21 = (bf16[2,128,1024]{2,1,0:T(8,128)(2,1)S(1)}, bf16[2,128,1024]{2,1,0:T(8,128)(2,1)S(1)}, u32[]{:S(2)}, u32[]{:S(2)}) collective-permute-start(bf16[2,128,1024]{2,1,0:T(8,128)(2,1)S(1)} %sum_chip.1), channel_id=1, source_target_pairs={{0,1},{1,0},{2,3},{3,2},{4,5},{5,4},{6,7},{7,6},{8,9},{9,8},{10,11... | collective-permute-start | bytes 1572872 | tf_op jit(solution)/shard_map/ppermute | solution.py:352
  81.3 12.9 %collective-permute-start.22 = (bf16[2,128,1024]{2,1,0:T(8,128)(2,1)S(1)}, bf16[2,128,1024]{2,1,0:T(8,128)(2,1)S(1)}, u32[]{:S(2)}, u32[]{:S(2)}) collective-permute-start(bf16[2,128,1024]{2,1,0:T(8,128)(2,1)S(1)} %get-tuple-element.112), channel_id=1, source_target_pairs={{0,8},{4,12},{8,0},{12,4},{1,9},{5,13},{9,1},{13,5},{2,10},{6,14},... | collective-permute-start | bytes 1572872 | tf_op jit(solution)/shard_map/ppermute | solution.py:352
  94.4 16.2 %collective-permute-start.27 = (bf16[1024,1024]{1,0:T(8,128)(2,1)S(1)}, bf16[1024,1024]{1,0:T(8,128)(2,1)S(1)}, u32[]{:S(2)}, u32[]{:S(2)}) collective-permute-start(bf16[1024,1024]{1,0:T(8,128)(2,1)S(1)} %copy-done), channel_id=1, source_target_pairs={{0,4},{4,0},{8,12},{12,8},{1,5},{5,1},{9,13},{13,9},{2,6},{6,2},{1... | collective-permute-start | bytes 6291464 | tf_op jit(solution)/shard_map/ppermute | solution.py:352
  94.5 16.1 %collective-permute-start.28 = (bf16[512,512]{1,0:T(8,128)(2,1)S(1)}, bf16[512,512]{1,0:T(8,128)(2,1)S(1)}, u32[]{:S(2)}, u32[]{:S(2)}) collective-permute-start(bf16[512,512]{1,0:T(8,128)(2,1)S(1)} %collective-permute-done.16.refs_6_), channel_id=1, source_target_pairs={{0,4},{4,0},{8,12},{12,8},{1,5},{5,1},{9,13},{13,9},{2,6},{6,2},{1... | collective-permute-start | bytes 1572872 | tf_op jit(solution)/shard_map/ppermute | solution.py:352
  95.0 15.6 %collective-permute-start.29 = (bf16[512,512]{1,0:T(8,128)(2,1)S(1)}, bf16[512,512]{1,0:T(8,128)(2,1)S(1)}, u32[]{:S(2)}, u32[]{:S(2)}) collective-permute-start(bf16[512,512]{1,0:T(8,128)(2,1)S(1)} %collective-permute-done.23.refs_7_), channel_id=1, source_target_pairs={{0,4},{4,0},{8,12},{12,8},{1,5},{5,1},{9,13},{13,9},{2,6},{6,2},{1... | collective-permute-start | bytes 1572872 | tf_op jit(solution)/shard_map/ppermute | solution.py:352
  95.3 15.2 %collective-permute-start.26 = (bf16[128,1024]{1,0:T(8,128)(2,1)S(1)}, bf16[128,1024]{1,0:T(8,128)(2,1)S(1)}, u32[]{:S(2)}, u32[]{:S(2)}) collective-permute-start(bf16[128,1024]{1,0:T(8,128)(2,1)S(1)} %get-tuple-element.121), channel_id=1, source_target_pairs={{0,2},{1,3},{2,0},{3,1},{4,6},{5,7},{6,4},{7,5},{8,10},{9,11},{10,... | collective-permute-start | bytes 786440 | tf_op jit(solution)/shard_map/ppermute | solution.py:352
  95.7 25.3 %collective-permute-start.33 = (bf16[1024,512]{1,0:T(8,128)(2,1)S(1)}, bf16[1024,512]{1,0:T(8,128)(2,1)S(1)}, u32[]{:S(2)}, u32[]{:S(2)}) collective-permute-start(bf16[1024,512]{1,0:T(8,128)(2,1)S(1)} %pad_maximum_fusion.refs_10_), channel_id=1, source_target_pairs={{0,8},{4,12},{8,0},{12,4},{1,9},{5,13},{9,1},{13,5},{2,10},{6,14},... | collective-permute-start | bytes 3145736 | tf_op jit(solution)/shard_map/ppermute | solution.py:352
  110.6 15.4 %collective-permute-start.32 = (bf16[1024,512]{1,0:T(8,128)(2,1)S(1)}, bf16[1024,512]{1,0:T(8,128)(2,1)S(1)}, u32[]{:S(2)}, u32[]{:S(2)}) collective-permute-start(bf16[1024,512]{1,0:T(8,128)(2,1)S(1)} %pad_maximum_fusion.refs_10_), channel_id=1, source_target_pairs={{0,4},{4,0},{8,12},{12,8},{1,5},{5,1},{9,13},{13,9},{2,6},{6,2},{1... | collective-permute-start | bytes 3145736 | tf_op jit(solution)/shard_map/ppermute | solution.py:352
  111.4 14.1 %collective-permute-start.30 = (bf16[128,1024]{1,0:T(8,128)(2,1)}, bf16[128,1024]{1,0:T(8,128)(2,1)S(1)}, u32[]{:S(2)}, u32[]{:S(2)}) collective-permute-start(bf16[128,1024]{1,0:T(8,128)(2,1)} %sum_hid.1.refs_0_), channel_id=1, source_target_pairs={{0,2},{1,3},{2,0},{3,1},{4,6},{5,7},{6,4},{7,5},{8,10},{9,11},{10,... | collective-permute-start | bytes 786440 | tf_op jit(solution)/shard_map/ppermute | solution.py:352
  111.4 14.5 %collective-permute-start.31 = (bf16[128,1024]{1,0:T(8,128)(2,1)}, bf16[128,1024]{1,0:T(8,128)(2,1)S(1)}, u32[]{:S(2)}, u32[]{:S(2)}) collective-permute-start(bf16[128,1024]{1,0:T(8,128)(2,1)} %sum_hid.1.refs_0_), channel_id=1, source_target_pairs={{0,1},{1,0},{2,3},{3,2},{4,5},{5,4},{6,7},{7,6},{8,9},{9,8},{10,11... | collective-permute-start | bytes 786440 | tf_op jit(solution)/shard_map/ppermute | solution.py:352
  (21 other events, 233.9 us)
